TPU v7x, 512 devices: a whole 4x8x8 slice. The times are simulated.
512 devices in a mesh: blk: 16 (over x_hi, y), head: 32 (over z, x_lo, core).
Axes of the slice: x: 4 (x_hi: 2, x_lo: 2; x = x_hi * 2 + x_lo), y: 8, z: 8, core: 2. Of those that a mesh axis runs over, the one named last changes fastest.
Arguments:
- queries: bfloat16 [65536, 4096], P(('blk', 'head')), may hold values from -14 to 14
- keys: bfloat16 [65536, 4096], P(('blk', 'head')), may hold values from -14 to 14
- values: bfloat16 [65536, 4096], P(('blk', 'head')), may hold values from -15 to 15
- key_blocks: int32 [128, 6], replicated, may hold values from 0 to 127, as said below
- counts: int32 [128], replicated, may hold values from 3 to 6, as said below
Outputs:
- attended: bfloat16 [65536, 4096], P(('blk', 'head'))
Inputs may be any that keep to these rules, and one draw needn't show every extreme that they name: `key_blocks`: row b lists, in slots below counts[b], distinct key blocks that lie in the cycle shard of b (shard = block // 8) or in one of the two shards beside it on the closed cycle of 16 shards; slots 0, 1, 2 hold b, b - 1 and b + 1 modulo 128; unused slots repeat slot 0. `counts`: some row uses all 6 slots and some row uses 3.
All inputs are finite; a program needn't handle non-finite values.
Results may differ from a plain program's by a relative error of at most 0.0036.
Values may be sent and summed in bfloat16 or wider, within the bound.
No kernel may reach another device: no remote copies, remote signals or barrier semaphores. Data moves between devices by JAX's collectives and lax.ppermute only.
A program may use at most 64 MiB of HBM per device.

v0:
```python
import jax
import jax.numpy as jnp
from jax import lax
from jax.sharding import PartitionSpec as P

HD = 128
BLOCK = 512
MAXB = 6


def from_behind(value, axis, steps):
    count = lax.axis_size(axis)
    pairs = [(source, (source + steps) % count) for source in range(count)]
    return lax.ppermute(value, axis, pairs)


def attend_shard(query_rows, context, listed_rows, count_rows):
    scale = HD ** (-0.5)
    group_rows = query_rows.shape[0]
    heads_local = query_rows.shape[1] // HD
    blocks_here = group_rows // BLOCK
    q_blocks = query_rows.reshape(blocks_here, BLOCK, heads_local, HD)
    pair_blocks = context.reshape(2, 3 * blocks_here, BLOCK, heads_local, HD)
    slot_ids = jnp.arange(MAXB, dtype=jnp.int32)

    def attend_block(inputs):
        query_block, listed, amount = inputs
        chosen = pair_blocks[:, listed]
        usable = (slot_ids < amount)[None, None, :, None]
        scores = (
            jnp.einsum("qhd,jkhd->hqjk", query_block, chosen[0], preferred_element_type=jnp.float32)
            * scale
        )
        top = jnp.max(jnp.where(usable, scores, -jnp.inf), axis=(2, 3), keepdims=True)
        expo = jnp.where(usable, jnp.exp(scores - top), 0.0)
        total = jnp.sum(expo, axis=(2, 3))
        weights = expo.astype(jnp.bfloat16)
        mixed = jnp.einsum("hqjk,jkhd->qhd", weights, chosen[1], preferred_element_type=jnp.float32)
        mixed = mixed / jnp.transpose(total)[:, :, None]
        return mixed.astype(jnp.bfloat16).reshape(BLOCK, heads_local * HD)

    result = lax.map(attend_block, (q_blocks, listed_rows, count_rows))
    return result.reshape(group_rows, heads_local * HD)


def local(queries, keys, values, key_blocks, counts):
    cycle_size = lax.axis_size("blk")
    query_rows = lax.all_to_all(queries, "head", split_axis=1, concat_axis=0, tiled=True)
    head_pair = lax.all_to_all(
        jnp.stack([keys, values]), "head", split_axis=2, concat_axis=1, tiled=True
    )
    earlier = from_behind(head_pair, "blk", 1)
    later = from_behind(head_pair, "blk", -1)
    context = jnp.concatenate([earlier, head_pair, later], axis=1)
    blocks_here = query_rows.shape[0] // BLOCK
    total_blocks = blocks_here * cycle_size
    first_block = lax.axis_index("blk") * blocks_here
    listed_rows = lax.dynamic_slice_in_dim(key_blocks, first_block, blocks_here, 0)
    count_rows = lax.dynamic_slice_in_dim(counts, first_block, blocks_here, 0)
    local_index = jnp.mod(listed_rows - first_block + blocks_here, total_blocks)
    attended_rows = attend_shard(query_rows, context, local_index, count_rows)
    return lax.all_to_all(attended_rows, "head", split_axis=0, concat_axis=1, tiled=True)


def solution(mesh):
    placed = (
        P(("blk", "head"), None),
        P(("blk", "head"), None),
        P(("blk", "head"), None),
        P(),
        P(),
    )
    return jax.shard_map(
        local, mesh=mesh, in_specs=placed, out_specs=P(("blk", "head"), None), check_vma=False
    )
```

profile of v0, /device:TPU:1, one launch (start us, length us, event | category | flops | bytes accessed | tf_op | source)
XLA Modules:
  0.0 267.8 jit_solution(9537263089981001835)
XLA Ops:
  0.0 3.2 %pad_maximum_fusion.1 = bf16[2,128,4096]{2,1,0:T(8,128)(2,1)} fusion(bf16[1,128,4096]{2,1,0:T(8,128)(2,1)} %bitcast.90, bf16[1,128,4096]{2,1,0:T(8,128)(2,1)} %bitcast.91), kind=kLoop, calls=%fused_computation.29 | loop fusion | flops 1048576 | bytes 4194304 | tf_op jit(solution)/shard_map/stack | solution.py:50
  3.2 4.7 %copy.42 = bf16[2,128,4096]{1,0,2:T(2,128)(2,1)S(1)} copy(bf16[2,128,4096]{2,1,0:T(8,128)(2,1)} %pad_maximum_fusion.1) | data formatting | bytes 4194304 | tf_op jit(solution)/shard_map/stack | solution.py:50
  7.9 63.4 %all_to_all.53 = bf16[2,128,4096]{1,0,2:T(2,128)(2,1)} all-to-all(bf16[2,128,4096]{1,0,2:T(2,128)(2,1)S(1)} %copy.42), channel_id=1, replica_groups=mesh['blk'=16,'head'=32] {'head'}, dimensions={2} | all-to-all | bytes 4194304 | tf_op jit(solution)/shard_map/all_to_all | solution.py:49
  71.3 4.9 %copy.43 = bf16[2,128,32,128]{3,1,2,0:T(8,128)(2,1)S(1)} copy(bf16[2,128,32,128]{1,0,3,2:T(2,128)(2,1)} %bitcast.83) | data formatting | bytes 4194304 | tf_op jit(solution)/shard_map/all_to_all | solution.py:49
  76.2 3.2 %collective-permute-start = (bf16[2,4096,128]{2,1,0:T(8,128)(2,1)S(1)}, bf16[2,4096,128]{2,1,0:T(8,128)(2,1)}, u32[]{:S(2)}, u32[]{:S(2)}) collective-permute-start(bf16[2,4096,128]{2,1,0:T(8,128)(2,1)S(1)} %bitcast.84), channel_id=1, source_target_pairs={{0,32},{32,64},{64,96},{96,128},{128,160},{160,192},{192,224},{224... | collective-permute-start | bytes 6291464 | tf_op jit(solution)/shard_map/ppermute | solution.py:14
  79.4 6.0 %collective-permute-start.1 = (bf16[2,4096,128]{2,1,0:T(8,128)(2,1)S(1)}, bf16[2,4096,128]{2,1,0:T(8,128)(2,1)}, u32[]{:S(2)}, u32[]{:S(2)}) collective-permute-start(bf16[2,4096,128]{2,1,0:T(8,128)(2,1)S(1)} %bitcast.85), channel_id=1, source_target_pairs={{0,480},{32,0},{64,32},{96,64},{128,96},{160,128},{192,160},{224,1... | collective-permute-start | bytes 6291464 | tf_op jit(solution)/shard_map/ppermute | solution.py:14
  86.7 5.7 %all-to-all-start.1 = ((bf16[128,32,128]{2,0,1:T(8,128)(2,1)}), bf16[128,32,128]{2,0,1:T(8,128)(2,1)}, u32[]{:S(2)}, u32[]{:S(2)}) async-start(bf16[128,32,128]{2,0,1:T(8,128)(2,1)} %copy_bitcast_fusion.1), calls=%async_computation.1 | async-start | bytes 2097152 | tf_op jit(solution)/shard_map/all_to_all | solution.py:48
  92.7 45.5 %collective-permute-done = bf16[2,4096,128]{2,1,0:T(8,128)(2,1)} collective-permute-done((bf16[2,4096,128]{2,1,0:T(8,128)(2,1)S(1)}, bf16[2,4096,128]{2,1,0:T(8,128)(2,1)}, u32[]{:S(2)}, u32[]{:S(2)}) %collective-permute-start) | collective-permute-done | bytes 2097184 | tf_op jit(solution)/shard_map/ppermute | solution.py:14
  139.0 10.3 %pad_maximum_fusion = bf16[2,12288,128]{2,1,0:T(8,128)(2,1)} fusion(bf16[2,4096,128]{2,1,0:T(8,128)(2,1)} %collective-permute-done.1, bf16[2,4096,128]{2,1,0:T(8,128)(2,1)S(1)} %bitcast.86, bf16[2,4096,128]{2,1,0:T(8,128)(2,1)} %collective-permute-done), kind=kLoop, calls=%fused_computation.28 | loop fusion | flops 18874368 | bytes 12582912 | tf_op jit(solution)/shard_map/concatenate | solution.py:54
  149.3 82.7 %while.11 = (s32[]{:T(128)}, bf16[8,512,128]{2,1,0:T(8,128)(2,1)}, s32[8,6]{1,0:T(8,128)S(1)}, bf16[2,24,512,1,128]{4,2,1,0,3:T(8,128)(2,1)}, s32[8]{0:T(128)S(1)}, /*index=5*/bf16[8,512,1,128]{3,1,2,0:T(8,128)(2,1)}, s32[]{:T(128)}) while((s32[]{:T(128)}, bf16[8,512,128]{2,1,0:T(8,128)(2,1)}, s32[8,6]{1,0:T(8,128)S(1)}, ...), condition=%wide.region_3.4_spmd.clone, body=%wide.region_0.3_spmd.clone.sunk | while | flops 822738944 | bytes 27541708 | solution.py:42
  149.3 3.6 %gather_fusion = bf16[6,2,512,128]{3,2,1,0:T(8,128)(2,1)S(1)} fusion(bf16[2,24,512,128]{3,2,1,0:T(8,128)(2,1)} %bitcast.82, s32[1024]{0:T(1024)S(1)} %pad_clamp_fusion.2), kind=kCustom, calls=%fused_computation.clone.clone.1 | custom fusion | bytes 3145752 | tf_op jit(solution)/shard_map/while/body/eval_jaxpr/gather | solution.py:28
  159.6 3.6 %gather_fusion = bf16[6,2,512,128]{3,2,1,0:T(8,128)(2,1)S(1)} fusion(bf16[2,24,512,128]{3,2,1,0:T(8,128)(2,1)} %bitcast.82, s32[1024]{0:T(1024)S(1)} %pad_clamp_fusion.2), kind=kCustom, calls=%fused_computation.clone.clone.1 | custom fusion | bytes 3145752 | tf_op jit(solution)/shard_map/while/body/eval_jaxpr/gather | solution.py:28
  164.6 1.9 select_reduce_fusion.2
  170.0 3.6 %gather_fusion = bf16[6,2,512,128]{3,2,1,0:T(8,128)(2,1)S(1)} fusion(bf16[2,24,512,128]{3,2,1,0:T(8,128)(2,1)} %bitcast.82, s32[1024]{0:T(1024)S(1)} %pad_clamp_fusion.2), kind=kCustom, calls=%fused_computation.clone.clone.1 | custom fusion | bytes 3145752 | tf_op jit(solution)/shard_map/while/body/eval_jaxpr/gather | solution.py:28
  175.0 1.9 select_reduce_fusion.2
  180.3 3.6 %gather_fusion = bf16[6,2,512,128]{3,2,1,0:T(8,128)(2,1)S(1)} fusion(bf16[2,24,512,128]{3,2,1,0:T(8,128)(2,1)} %bitcast.82, s32[1024]{0:T(1024)S(1)} %pad_clamp_fusion.2), kind=kCustom, calls=%fused_computation.clone.clone.1 | custom fusion | bytes 3145752 | tf_op jit(solution)/shard_map/while/body/eval_jaxpr/gather | solution.py:28
  190.6 3.6 %gather_fusion = bf16[6,2,512,128]{3,2,1,0:T(8,128)(2,1)S(1)} fusion(bf16[2,24,512,128]{3,2,1,0:T(8,128)(2,1)} %bitcast.82, s32[1024]{0:T(1024)S(1)} %pad_clamp_fusion.2), kind=kCustom, calls=%fused_computation.clone.clone.1 | custom fusion | bytes 3145752 | tf_op jit(solution)/shard_map/while/body/eval_jaxpr/gather | solution.py:28
  195.6 1.9 select_reduce_fusion.2
  201.0 3.6 %gather_fusion = bf16[6,2,512,128]{3,2,1,0:T(8,128)(2,1)S(1)} fusion(bf16[2,24,512,128]{3,2,1,0:T(8,128)(2,1)} %bitcast.82, s32[1024]{0:T(1024)S(1)} %pad_clamp_fusion.2), kind=kCustom, calls=%fused_computation.clone.clone.1 | custom fusion | bytes 3145752 | tf_op jit(solution)/shard_map/while/body/eval_jaxpr/gather | solution.py:28
  211.3 3.6 %gather_fusion = bf16[6,2,512,128]{3,2,1,0:T(8,128)(2,1)S(1)} fusion(bf16[2,24,512,128]{3,2,1,0:T(8,128)(2,1)} %bitcast.82, s32[1024]{0:T(1024)S(1)} %pad_clamp_fusion.2), kind=kCustom, calls=%fused_computation.clone.clone.1 | custom fusion | bytes 3145752 | tf_op jit(solution)/shard_map/while/body/eval_jaxpr/gather | solution.py:28
  216.3 1.9 select_reduce_fusion.2
  221.6 3.6 %gather_fusion = bf16[6,2,512,128]{3,2,1,0:T(8,128)(2,1)S(1)} fusion(bf16[2,24,512,128]{3,2,1,0:T(8,128)(2,1)} %bitcast.82, s32[1024]{0:T(1024)S(1)} %pad_clamp_fusion.2), kind=kCustom, calls=%fused_computation.clone.clone.1 | custom fusion | bytes 3145752 | tf_op jit(solution)/shard_map/while/body/eval_jaxpr/gather | solution.py:28
  226.6 1.9 select_reduce_fusion.2
  232.0 33.9 %all_to_all.54 = bf16[32,128,128]{2,1,0:T(8,128)(2,1)S(1)} all-to-all(bf16[32,128,128]{2,1,0:T(8,128)(2,1)} %bitcast.89), channel_id=1, replica_groups=mesh['blk'=16,'head'=32] {'head'}, dimensions={0} | all-to-all | bytes 2097152 | tf_op jit(solution)/shard_map/all_to_all | solution.py:62
  (91 shorter events, 48.1 us)
Async XLA Ops:
  0.0 85.4 %copy-start = (bf16[128,4096]{1,0:T(8,128)(2,1)S(1)}, bf16[128,4096]{1,0:T(8,128)(2,1)}, u32[]{:S(2)}) copy-start(bf16[128,4096]{1,0:T(8,128)(2,1)} %param.7) | copy-start | bytes 3145732
  7.9 84.6 %copy-start.1 = (s32[128,6]{0,1:T(8,128)S(1)}, s32[128,6]{0,1:T(8,128)}, u32[]{:S(2)}) copy-start(s32[128,6]{0,1:T(8,128)} %param.10) | copy-start | bytes 9220
  7.9 84.7 %copy-start.2 = (s32[128]{0:T(128)S(1)}, s32[128]{0:T(128)}, u32[]{:S(2)}) copy-start(s32[128]{0:T(128)} %param.11) | copy-start | bytes 1540
  76.2 62.0 %collective-permute-start = (bf16[2,4096,128]{2,1,0:T(8,128)(2,1)S(1)}, bf16[2,4096,128]{2,1,0:T(8,128)(2,1)}, u32[]{:S(2)}, u32[]{:S(2)}) collective-permute-start(bf16[2,4096,128]{2,1,0:T(8,128)(2,1)S(1)} %bitcast.84), channel_id=1, source_target_pairs={{0,32},{32,64},{64,96},{96,128},{128,160},{160,192},{192,224},{224... | collective-permute-start | bytes 6291464 | tf_op jit(solution)/shard_map/ppermute | solution.py:14
  79.4 59.5 %collective-permute-start.1 = (bf16[2,4096,128]{2,1,0:T(8,128)(2,1)S(1)}, bf16[2,4096,128]{2,1,0:T(8,128)(2,1)}, u32[]{:S(2)}, u32[]{:S(2)}) collective-permute-start(bf16[2,4096,128]{2,1,0:T(8,128)(2,1)S(1)} %bitcast.85), channel_id=1, source_target_pairs={{0,480},{32,0},{64,32},{96,64},{128,96},{160,128},{192,160},{224,1... | collective-permute-start | bytes 6291464 | tf_op jit(solution)/shard_map/ppermute | solution.py:14
  86.7 62.6 %all-to-all-start.1 = ((bf16[128,32,128]{2,0,1:T(8,128)(2,1)}), bf16[128,32,128]{2,0,1:T(8,128)(2,1)}, u32[]{:S(2)}, u32[]{:S(2)}) async-start(bf16[128,32,128]{2,0,1:T(8,128)(2,1)} %copy_bitcast_fusion.1), calls=%async_computation.1 | async-start | bytes 2097152 | tf_op jit(solution)/shard_map/all_to_all | solution.py:48
where the time goes:
time: 271 us; the launch traced here: 268 us
  blocking collectives  97.3 us (36%)
  local copies, waits for them, and re-layouts  54.1 us (20%)
  waiting for transfers between devices  46.3 us (17%)
  other arithmetic  29.2 us (11%)
  matrix products  25.6 us (9%)
  starting transfers between devices  14.9 us (5%)
    all_to_all x1, blocking collectives, local(): lax.all_to_all(jnp.stack([keys, values]), 'head', split_axis=2, concat_ax...  63.4 us
    ppermute x2, waiting for transfers between devices, from_behind(): return lax.ppermute(value, axis, pairs)  46.3 us
    all_to_all x1, blocking collectives, local(): lax.all_to_all(attended_rows, 'head', split_axis=0, concat_axis=1, tiled=...  33.9 us
    gather x16, local copies, waits for them, and re-layouts, attend_block(): chosen = pair_blocks[:, listed]  29.9 us
    dot_general x8, matrix products, attend_block(): jnp.einsum('qhd,jkhd->hqjk', query_block, chosen[0], preferred_element_ty...  15.2 us
    reduce_sum x8, other arithmetic, attend_block(): total = jnp.sum(expo, axis=(2, 3))  10.6 us
    dot_general x8, matrix products, attend_block(): jnp.einsum('hqjk,jkhd->qhd', weights, chosen[1], preferred_element_type=j...  10.5 us
    concatenate x1, other arithmetic, local(): context = jnp.concatenate([earlier, head_pair, later], axis=1)  10.3 us
  transfers between devices with their start and end apart: 3, of which 2 were waited for; matrix products, arithmetic and copies ran while one was open for 4% of the time, Pallas kernels for 0%

commit v1 on v0

v1 whole, which is shorter than its diff:
```python
import functools

import jax
import jax.numpy as jnp
from jax import lax
from jax.experimental import pallas as pl
from jax.experimental.pallas import tpu as pltpu
from jax.sharding import PartitionSpec as P

HD = 128
BLOCK = 512
MAXB = 6


def from_behind(value, axis, steps):
    count = lax.axis_size(axis)
    pairs = [(source, (source + steps) % count) for source in range(count)]
    return lax.ppermute(value, axis, pairs)


def attention_kernel(idx_ref, cnt_ref, q_ref, kp, ko, kn, vp, vo, vn, o_ref,
                     k_scr, v_scr, s_scr, m_scr, l_scr, acc_scr, sem, *, shard_rows):
    b = pl.program_id(0)

    @pl.when(b == 0)
    def _load_context():
        copies = []
        for i, (src, dst, part) in enumerate(
            ((kp, k_scr, 0), (ko, k_scr, 1), (kn, k_scr, 2),
             (vp, v_scr, 0), (vo, v_scr, 1), (vn, v_scr, 2))
        ):
            copy = pltpu.make_async_copy(
                src, dst.at[pl.ds(part * shard_rows, shard_rows)], sem.at[i]
            )
            copy.start()
            copies.append(copy)
        for copy in copies:
            copy.wait()

    scale = HD ** (-0.5)
    amount = cnt_ref[b]
    m_scr[...] = jnp.full(m_scr.shape, -jnp.inf, jnp.float32)
    for j in range(MAXB):
        @pl.when(j < amount)
        def _scores():
            start = pl.multiple_of(idx_ref[b * MAXB + j] * BLOCK, BLOCK)
            key_block = k_scr[pl.ds(start, BLOCK), :]
            scores = lax.dot_general(
                q_ref[...], key_block, (((1,), (1,)), ((), ())),
                preferred_element_type=jnp.float32,
            ) * scale
            s_scr[j] = scores
            m_scr[...] = jnp.maximum(m_scr[...], jnp.max(scores, axis=1, keepdims=True))

    l_scr[...] = jnp.zeros(l_scr.shape, jnp.float32)
    acc_scr[...] = jnp.zeros(acc_scr.shape, jnp.float32)
    for j in range(MAXB):
        @pl.when(j < amount)
        def _mix():
            start = pl.multiple_of(idx_ref[b * MAXB + j] * BLOCK, BLOCK)
            value_block = v_scr[pl.ds(start, BLOCK), :]
            expo = jnp.exp(s_scr[j] - m_scr[...])
            l_scr[...] += jnp.sum(expo, axis=1, keepdims=True)
            acc_scr[...] += jnp.dot(
                expo.astype(jnp.bfloat16), value_block, preferred_element_type=jnp.float32
            )

    o_ref[...] = (acc_scr[...] / l_scr[...]).astype(o_ref.dtype)


def attend(query_rows, k_parts, v_parts, local_index, count_rows):
    rows, width = query_rows.shape
    blocks_here = rows // BLOCK
    shard_rows = k_parts[0].shape[0]
    flops = blocks_here * MAXB * BLOCK * BLOCK * width * 4
    cost = pl.CostEstimate(
        flops=flops,
        transcendentals=blocks_here * MAXB * BLOCK * BLOCK,
        bytes_accessed=(2 + 6) * rows * width * 2,
    )
    any_spec = pl.BlockSpec(memory_space=pl.ANY)
    grid_spec = pltpu.PrefetchScalarGridSpec(
        num_scalar_prefetch=2,
        grid=(blocks_here,),
        in_specs=[pl.BlockSpec((BLOCK, width), lambda b, idx, cnt: (b, 0))] + [any_spec] * 6,
        out_specs=pl.BlockSpec((BLOCK, width), lambda b, idx, cnt: (b, 0)),
        scratch_shapes=[
            pltpu.VMEM((3 * shard_rows, width), jnp.bfloat16),
            pltpu.VMEM((3 * shard_rows, width), jnp.bfloat16),
            pltpu.VMEM((MAXB, BLOCK, BLOCK), jnp.float32),
            pltpu.VMEM((BLOCK, 1), jnp.float32),
            pltpu.VMEM((BLOCK, 1), jnp.float32),
            pltpu.VMEM((BLOCK, width), jnp.float32),
            pltpu.SemaphoreType.DMA((6,)),
        ],
    )
    return pl.pallas_call(
        functools.partial(attention_kernel, shard_rows=shard_rows),
        out_shape=jax.ShapeDtypeStruct((rows, width), jnp.bfloat16),
        grid_spec=grid_spec,
        compiler_params=pltpu.CompilerParams(dimension_semantics=("arbitrary",)),
        cost_estimate=cost,
    )(local_index, count_rows, query_rows, *k_parts, *v_parts)


def local(queries, keys, values, key_blocks, counts):
    cycle_size = lax.axis_size("blk")

    def to_heads(x):
        return lax.all_to_all(x, "head", split_axis=1, concat_axis=0, tiled=True)

    key_rows = to_heads(keys)
    value_rows = to_heads(values)
    query_rows = to_heads(queries)
    k_parts = (from_behind(key_rows, "blk", 1), key_rows, from_behind(key_rows, "blk", -1))
    v_parts = (from_behind(value_rows, "blk", 1), value_rows, from_behind(value_rows, "blk", -1))
    blocks_here = query_rows.shape[0] // BLOCK
    total_blocks = blocks_here * cycle_size
    first_block = lax.axis_index("blk") * blocks_here
    listed_rows = lax.dynamic_slice_in_dim(key_blocks, first_block, blocks_here, 0)
    count_rows = lax.dynamic_slice_in_dim(counts, first_block, blocks_here, 0)
    local_index = jnp.mod(listed_rows - first_block + blocks_here, total_blocks)
    local_index = jnp.clip(local_index, 0, 3 * blocks_here - 1).reshape(-1)
    attended_rows = attend(query_rows, k_parts, v_parts, local_index, count_rows)
    return lax.all_to_all(attended_rows, "head", split_axis=0, concat_axis=1, tiled=True)


def solution(mesh):
    placed = (
        P(("blk", "head"), None),
        P(("blk", "head"), None),
        P(("blk", "head"), None),
        P(),
        P(),
    )
    return jax.shard_map(
        local, mesh=mesh, in_specs=placed, out_specs=P(("blk", "head"), None), check_vma=False
    )
```

time: 271 us -> 224 us (0.83)
  blocking collectives: 97.3 us -> 37.2 us
  waiting for transfers between devices: 46.3 us -> 98.1 us
  local copies, waits for them, and re-layouts: 54.1 us -> 8.15 us
  Pallas kernels: 0 us -> 38.4 us
  other arithmetic: 29.2 us -> 0.08 us
  starting transfers between devices: 14.9 us -> 41.5 us
  matrix products: 25.6 us -> 0 us
    all_to_all x1 -> x0, blocking collectives: 63.4 us -> none  [local(): lax.all_to_all(jnp.stack([keys, values]), 'head', split_axis=2, concat_ax...]
    all_to_all x1 -> x3, waiting for transfers between devices: 0.01 us -> 61.9 us  [to_heads(): return lax.all_to_all(x, 'head', split_axis=1, concat_axis=0, tiled=True)]
    pallas_call x0 -> x1, Pallas kernels: none -> 38.4 us  [attend(): pl.pallas_call(functools.partial(attention_kernel, shard_rows=shard_rows)...]
    gather x16 -> x0, local copies, waits for them, and re-layouts: 29.9 us -> none  [attend_block(): chosen = pair_blocks[:, listed]]
    dot_general x16 -> x0, matrix products: 25.6 us -> none  [the longest x8 15.2 us: attend_block(): jnp.einsum('qhd,jkhd->hqjk', query_block, chosen[0], preferred_element_ty...]
    all_to_all x1 -> x3, starting transfers between devices: 5.73 us -> 23.5 us  [to_heads(): return lax.all_to_all(x, 'head', split_axis=1, concat_axis=0, tiled=True)]
    reduce_sum x8 -> x0, other arithmetic: 10.6 us -> none  [attend_block(): total = jnp.sum(expo, axis=(2, 3))]
    concatenate x1 -> x0, other arithmetic: 10.3 us -> none  [local(): context = jnp.concatenate([earlier, head_pair, later], axis=1)]
  transfers between devices with their start and end apart: 3 -> 7, of which waited for: 2 -> 7; matrix products, arithmetic and copies ran while one was open for 4% -> 2% of each run, Pallas kernels for 0% -> 0%
where the time goes in v1:
time: 224 us
  waiting for transfers between devices  98.1 us (44%)
  starting transfers between devices  41.5 us (19%)
  Pallas kernels  38.4 us (17%)
  blocking collectives  37.2 us (17%)
  local copies, waits for them, and re-layouts  8.15 us (4%)
    all_to_all x3, waiting for transfers between devices, to_heads(): return lax.all_to_all(x, 'head', split_axis=1, concat_axis=0, tiled=True)  61.9 us
    pallas_call x1, Pallas kernels, attend(): pl.pallas_call(functools.partial(attention_kernel, shard_rows=shard_rows)...  38.4 us
    all_to_all x1, blocking collectives, local(): lax.all_to_all(attended_rows, 'head', split_axis=0, concat_axis=1, tiled=...  37.2 us
    ppermute x4, waiting for transfers between devices, from_behind(): return lax.ppermute(value, axis, pairs)  36.2 us
    all_to_all x3, starting transfers between devices, to_heads(): return lax.all_to_all(x, 'head', split_axis=1, concat_axis=0, tiled=True)  23.5 us
    ppermute x4, starting transfers between devices, from_behind(): return lax.ppermute(value, axis, pairs)  18.1 us
  transfers between devices with their start and end apart: 7, of which 7 were waited for; matrix products, arithmetic and copies ran while one was open for 2% of the time, Pallas kernels for 0%

profile of v1, /device:TPU:1, one launch (start us, length us, event | category | flops | bytes accessed | tf_op | source)
XLA Modules:
  0.0 223.5 jit_solution(17929702220834928951)
XLA Ops:
  0.0 1.2 copy-done
  1.2 1.3 copy_bitcast_fusion.2
  2.5 13.0 %all-to-all-start.1 = ((bf16[128,32,128]{2,0,1:T(8,128)(2,1)}), bf16[128,32,128]{2,0,1:T(8,128)(2,1)S(1)}, u32[]{:S(2)}, u32[]{:S(2)}) async-start(bf16[128,32,128]{2,0,1:T(8,128)(2,1)} %copy_bitcast_fusion.2), calls=%async_computation.1 | async-start | bytes 2097152 | tf_op jit(solution)/shard_map/all_to_all | solution.py:110
  15.5 1.3 copy_bitcast_fusion.1
  16.8 26.9 %all-to-all-done.1 = bf16[128,32,128]{2,0,1:T(8,128)(2,1)S(1)} async-done(((bf16[128,32,128]{2,0,1:T(8,128)(2,1)}), bf16[128,32,128]{2,0,1:T(8,128)(2,1)S(1)}, u32[]{:S(2)}, u32[]{:S(2)}) %all-to-all-start.1) | async-done | bytes 1048608 | tf_op jit(solution)/shard_map/all_to_all | solution.py:110
  43.7 5.4 %all-to-all-start.2 = ((bf16[128,32,128]{2,0,1:T(8,128)(2,1)}), bf16[128,32,128]{2,0,1:T(8,128)(2,1)}, u32[]{:S(2)}, u32[]{:S(2)}) async-start(bf16[128,32,128]{2,0,1:T(8,128)(2,1)} %copy_bitcast_fusion.1), calls=%async_computation.2 | async-start | bytes 2097152 | tf_op jit(solution)/shard_map/all_to_all | solution.py:110
  49.1 1.3 copy_bitcast_fusion.3
  50.4 26.9 %all-to-all-done.2 = bf16[128,32,128]{2,0,1:T(8,128)(2,1)} async-done(((bf16[128,32,128]{2,0,1:T(8,128)(2,1)}), bf16[128,32,128]{2,0,1:T(8,128)(2,1)}, u32[]{:S(2)}, u32[]{:S(2)}) %all-to-all-start.2) | async-done | bytes 1048608 | tf_op jit(solution)/shard_map/all_to_all | solution.py:110
  77.4 5.0 %all-to-all-start = ((bf16[128,32,128]{2,0,1:T(8,128)(2,1)}), bf16[128,32,128]{2,0,1:T(8,128)(2,1)S(1)}, u32[]{:S(2)}, u32[]{:S(2)}) async-start(bf16[128,32,128]{2,0,1:T(8,128)(2,1)} %copy_bitcast_fusion.3), calls=%async_computation | async-start | bytes 2097152 | tf_op jit(solution)/shard_map/all_to_all | solution.py:110
  82.3 7.3 %collective-permute-start.3 = (bf16[4096,128]{1,0:T(8,128)(2,1)}, bf16[4096,128]{1,0:T(8,128)(2,1)}, u32[]{:S(2)}, u32[]{:S(2)}) collective-permute-start(bf16[4096,128]{1,0:T(8,128)(2,1)} %bitcast.6.vo), channel_id=1, source_target_pairs={{0,480},{32,0},{64,32},{96,64},{128,96},{160,128},{192,160},{224,1... | collective-permute-start | bytes 3145736 | tf_op jit(solution)/shard_map/ppermute | solution.py:18
  89.6 1.9 collective-permute-start.2
  91.6 7.0 %collective-permute-start.1 = (bf16[4096,128]{1,0:T(8,128)(2,1)S(1)}, bf16[4096,128]{1,0:T(8,128)(2,1)}, u32[]{:S(2)}, u32[]{:S(2)}) collective-permute-start(bf16[4096,128]{1,0:T(8,128)(2,1)S(1)} %bitcast.31), channel_id=1, source_target_pairs={{0,480},{32,0},{64,32},{96,64},{128,96},{160,128},{192,160},{224,1... | collective-permute-start | bytes 3145736 | tf_op jit(solution)/shard_map/ppermute | solution.py:18
  98.5 1.9 collective-permute-start
  100.5 0.7 copy-done.6
  101.2 0.6 dynamic_slice.7.cnt_ref
  101.9 0.6 reshape.15.idx_ref
  102.6 8.1 %all-to-all-done = bf16[128,32,128]{2,0,1:T(8,128)(2,1)S(1)} async-done(((bf16[128,32,128]{2,0,1:T(8,128)(2,1)}), bf16[128,32,128]{2,0,1:T(8,128)(2,1)S(1)}, u32[]{:S(2)}, u32[]{:S(2)}) %all-to-all-start) | async-done | bytes 1048608 | tf_op jit(solution)/shard_map/all_to_all | solution.py:110
  110.7 8.9 %collective-permute-done.3.vn = bf16[4096,128]{1,0:T(8,128)(2,1)} collective-permute-done((bf16[4096,128]{1,0:T(8,128)(2,1)}, bf16[4096,128]{1,0:T(8,128)(2,1)}, u32[]{:S(2)}, u32[]{:S(2)}) %collective-permute-start.3) | collective-permute-done | bytes 1048608 | tf_op jit(solution)/shard_map/ppermute | solution.py:18
  119.5 4.9 %collective-permute-done.2.vp = bf16[4096,128]{1,0:T(8,128)(2,1)} collective-permute-done((bf16[4096,128]{1,0:T(8,128)(2,1)}, bf16[4096,128]{1,0:T(8,128)(2,1)}, u32[]{:S(2)}, u32[]{:S(2)}) %collective-permute-start.2) | collective-permute-done | bytes 1048608 | tf_op jit(solution)/shard_map/ppermute | solution.py:18
  124.4 17.5 %collective-permute-done.1.kn = bf16[4096,128]{1,0:T(8,128)(2,1)} collective-permute-done((bf16[4096,128]{1,0:T(8,128)(2,1)S(1)}, bf16[4096,128]{1,0:T(8,128)(2,1)}, u32[]{:S(2)}, u32[]{:S(2)}) %collective-permute-start.1) | collective-permute-done | bytes 1048608 | tf_op jit(solution)/shard_map/ppermute | solution.py:18
  141.9 5.0 %collective-permute-done.kp = bf16[4096,128]{1,0:T(8,128)(2,1)} collective-permute-done((bf16[4096,128]{1,0:T(8,128)(2,1)S(1)}, bf16[4096,128]{1,0:T(8,128)(2,1)}, u32[]{:S(2)}, u32[]{:S(2)}) %collective-permute-start) | collective-permute-done | bytes 1048608 | tf_op jit(solution)/shard_map/ppermute | solution.py:18
  146.8 38.4 %shard_map.55 = bf16[4096,128]{1,0:T(8,128)(2,1)} custom-call(s32[48]{0:T(128)} %reshape.15.idx_ref, s32[8]{0:T(128)} %dynamic_slice.7.cnt_ref, bf16[4096,128]{1,0:T(8,128)(2,1)} %bitcast.34, bf16[4096,128]{1,0:T(8,128)(2,1)} %collective-permute-done.kp, bf16[4096,128]{1,0:T(8,128)(2,1)} %bitcast.33, bf16[4096,128]{1,0:T(8,128)(2,1)} %collective-permute-done.1.kn, ...), custom_call_target="tpu_custom_call" | custom-call | flops 6442450944 | bytes 8388608 | tf_op jit(solution)/shard_map/pallas_call | solution.py:97
  185.2 37.2 %all_to_all.76 = bf16[32,128,128]{2,1,0:T(8,128)(2,1)S(1)} all-to-all(bf16[32,128,128]{2,1,0:T(8,128)(2,1)} %bitcast.35), channel_id=1, replica_groups=mesh['blk'=16,'head'=32] {'head'}, dimensions={0} | all-to-all | bytes 2097152 | tf_op jit(solution)/shard_map/all_to_all | solution.py:125
  222.4 1.1 copy_bitcast_fusion
  (14 shorter events, 0.2 us)
Async XLA Ops:
  0.0 1.2 copy-start
  2.5 13.0 %copy-start.1 = (bf16[128,4096]{1,0:T(8,128)(2,1)S(1)}, bf16[128,4096]{1,0:T(8,128)(2,1)}, u32[]{:S(2)}) copy-start(bf16[128,4096]{1,0:T(8,128)(2,1)} %param.7) | copy-start | bytes 3145732
  2.5 41.2 %all-to-all-start.1 = ((bf16[128,32,128]{2,0,1:T(8,128)(2,1)}), bf16[128,32,128]{2,0,1:T(8,128)(2,1)S(1)}, u32[]{:S(2)}, u32[]{:S(2)}) async-start(bf16[128,32,128]{2,0,1:T(8,128)(2,1)} %copy_bitcast_fusion.2), calls=%async_computation.1 | async-start | bytes 2097152 | tf_op jit(solution)/shard_map/all_to_all | solution.py:110
  16.8 32.3 %copy-start.2 = (bf16[128,4096]{1,0:T(8,128)(2,1)S(1)}, bf16[128,4096]{1,0:T(8,128)(2,1)}, u32[]{:S(2)}) copy-start(bf16[128,4096]{1,0:T(8,128)(2,1)} %param.5) | copy-start | bytes 3145732
  43.7 54.9 %copy-start.3 = (bf16[128,32,128]{2,0,1:T(8,128)(2,1)}, bf16[128,32,128]{2,0,1:T(8,128)(2,1)S(1)}, u32[]{:S(2)}) copy-start(bf16[128,32,128]{2,0,1:T(8,128)(2,1)S(1)} %all-to-all-done.1) | copy-start | bytes 3145732
  43.7 33.7 %all-to-all-start.2 = ((bf16[128,32,128]{2,0,1:T(8,128)(2,1)}), bf16[128,32,128]{2,0,1:T(8,128)(2,1)}, u32[]{:S(2)}, u32[]{:S(2)}) async-start(bf16[128,32,128]{2,0,1:T(8,128)(2,1)} %copy_bitcast_fusion.1), calls=%async_computation.2 | async-start | bytes 2097152 | tf_op jit(solution)/shard_map/all_to_all | solution.py:110
  77.4 33.3 %all-to-all-start = ((bf16[128,32,128]{2,0,1:T(8,128)(2,1)}), bf16[128,32,128]{2,0,1:T(8,128)(2,1)S(1)}, u32[]{:S(2)}, u32[]{:S(2)}) async-start(bf16[128,32,128]{2,0,1:T(8,128)(2,1)} %copy_bitcast_fusion.3), calls=%async_computation | async-start | bytes 2097152 | tf_op jit(solution)/shard_map/all_to_all | solution.py:110
  82.3 37.2 %collective-permute-start.3 = (bf16[4096,128]{1,0:T(8,128)(2,1)}, bf16[4096,128]{1,0:T(8,128)(2,1)}, u32[]{:S(2)}, u32[]{:S(2)}) collective-permute-start(bf16[4096,128]{1,0:T(8,128)(2,1)} %bitcast.6.vo), channel_id=1, source_target_pairs={{0,480},{32,0},{64,32},{96,64},{128,96},{160,128},{192,160},{224,1... | collective-permute-start | bytes 3145736 | tf_op jit(solution)/shard_map/ppermute | solution.py:18
  89.6 34.8 %collective-permute-start.2 = (bf16[4096,128]{1,0:T(8,128)(2,1)}, bf16[4096,128]{1,0:T(8,128)(2,1)}, u32[]{:S(2)}, u32[]{:S(2)}) collective-permute-start(bf16[4096,128]{1,0:T(8,128)(2,1)} %bitcast.6.vo), channel_id=1, source_target_pairs={{0,32},{32,64},{64,96},{96,128},{128,160},{160,192},{192,224},{224... | collective-permute-start | bytes 3145736 | tf_op jit(solution)/shard_map/ppermute | solution.py:18
  91.6 50.3 %collective-permute-start.1 = (bf16[4096,128]{1,0:T(8,128)(2,1)S(1)}, bf16[4096,128]{1,0:T(8,128)(2,1)}, u32[]{:S(2)}, u32[]{:S(2)}) collective-permute-start(bf16[4096,128]{1,0:T(8,128)(2,1)S(1)} %bitcast.31), channel_id=1, source_target_pairs={{0,480},{32,0},{64,32},{96,64},{128,96},{160,128},{192,160},{224,1... | collective-permute-start | bytes 3145736 | tf_op jit(solution)/shard_map/ppermute | solution.py:18
  98.5 48.3 %collective-permute-start = (bf16[4096,128]{1,0:T(8,128)(2,1)S(1)}, bf16[4096,128]{1,0:T(8,128)(2,1)}, u32[]{:S(2)}, u32[]{:S(2)}) collective-permute-start(bf16[4096,128]{1,0:T(8,128)(2,1)S(1)} %bitcast.32), channel_id=1, source_target_pairs={{0,32},{32,64},{64,96},{96,128},{128,160},{160,192},{192,224},{224... | collective-permute-start | bytes 3145736 | tf_op jit(solution)/shard_map/ppermute | solution.py:18
  100.5 1.3 copy-start.5
  100.5 0.7 copy-start.6
  110.6 36.2 %copy-start.4 = (bf16[128,32,128]{2,0,1:T(8,128)(2,1)}, bf16[128,32,128]{2,0,1:T(8,128)(2,1)S(1)}, u32[]{:S(2)}) copy-start(bf16[128,32,128]{2,0,1:T(8,128)(2,1)S(1)} %all-to-all-done) | copy-start | bytes 3145732

commit v2 on v1

--- a/solution.py
+++ b/solution.py
@@ -18,16 +18,21 @@
     return lax.ppermute(value, axis, pairs)
 
 
-def attention_kernel(idx_ref, cnt_ref, q_ref, kp, ko, kn, vp, vo, vn, o_ref,
+def attention_kernel(idx_ref, cnt_ref, q_ref, kv_prev, kv_own, kv_next, o_ref,
                      k_scr, v_scr, s_scr, m_scr, l_scr, acc_scr, sem, *, shard_rows):
     b = pl.program_id(0)
+    width = q_ref.shape[1]
 
     @pl.when(b == 0)
     def _load_context():
         copies = []
         for i, (src, dst, part) in enumerate(
-            ((kp, k_scr, 0), (ko, k_scr, 1), (kn, k_scr, 2),
-             (vp, v_scr, 0), (vo, v_scr, 1), (vn, v_scr, 2))
+            ((kv_own.at[:, pl.ds(0, width)], k_scr, 1),
+             (kv_own.at[:, pl.ds(width, width)], v_scr, 1),
+             (kv_prev.at[:, pl.ds(0, width)], k_scr, 0),
+             (kv_next.at[:, pl.ds(0, width)], k_scr, 2),
+             (kv_prev.at[:, pl.ds(width, width)], v_scr, 0),
+             (kv_next.at[:, pl.ds(width, width)], v_scr, 2))
         ):
             copy = pltpu.make_async_copy(
                 src, dst.at[pl.ds(part * shard_rows, shard_rows)], sem.at[i]
@@ -68,10 +73,10 @@
     o_ref[...] = (acc_scr[...] / l_scr[...]).astype(o_ref.dtype)
 
 
-def attend(query_rows, k_parts, v_parts, local_index, count_rows):
+def attend(query_rows, kv_parts, local_index, count_rows):
     rows, width = query_rows.shape
     blocks_here = rows // BLOCK
-    shard_rows = k_parts[0].shape[0]
+    shard_rows = kv_parts[0].shape[0]
     flops = blocks_here * MAXB * BLOCK * BLOCK * width * 4
     cost = pl.CostEstimate(
         flops=flops,
@@ -82,7 +87,7 @@
     grid_spec = pltpu.PrefetchScalarGridSpec(
         num_scalar_prefetch=2,
         grid=(blocks_here,),
-        in_specs=[pl.BlockSpec((BLOCK, width), lambda b, idx, cnt: (b, 0))] + [any_spec] * 6,
+        in_specs=[pl.BlockSpec((BLOCK, width), lambda b, idx, cnt: (b, 0))] + [any_spec] * 3,
         out_specs=pl.BlockSpec((BLOCK, width), lambda b, idx, cnt: (b, 0)),
         scratch_shapes=[
             pltpu.VMEM((3 * shard_rows, width), jnp.bfloat16),
@@ -100,7 +105,7 @@
         grid_spec=grid_spec,
         compiler_params=pltpu.CompilerParams(dimension_semantics=("arbitrary",)),
         cost_estimate=cost,
-    )(local_index, count_rows, query_rows, *k_parts, *v_parts)
+    )(local_index, count_rows, query_rows, *kv_parts)
 
 
 def local(queries, keys, values, key_blocks, counts):
@@ -109,11 +114,14 @@
     def to_heads(x):
         return lax.all_to_all(x, "head", split_axis=1, concat_axis=0, tiled=True)
 
-    key_rows = to_heads(keys)
-    value_rows = to_heads(values)
+    rows, model = keys.shape
+    heads = model // HD
+    paired = jnp.stack(
+        [keys.reshape(rows, heads, HD), values.reshape(rows, heads, HD)], axis=2
+    ).reshape(rows, 2 * model)
+    kv_rows = to_heads(paired)
     query_rows = to_heads(queries)
-    k_parts = (from_behind(key_rows, "blk", 1), key_rows, from_behind(key_rows, "blk", -1))
-    v_parts = (from_behind(value_rows, "blk", 1), value_rows, from_behind(value_rows, "blk", -1))
+    kv_parts = (from_behind(kv_rows, "blk", 1), kv_rows, from_behind(kv_rows, "blk", -1))
     blocks_here = query_rows.shape[0] // BLOCK
     total_blocks = blocks_here * cycle_size
     first_block = lax.axis_index("blk") * blocks_here
@@ -121,7 +129,7 @@
     count_rows = lax.dynamic_slice_in_dim(counts, first_block, blocks_here, 0)
     local_index = jnp.mod(listed_rows - first_block + blocks_here, total_blocks)
     local_index = jnp.clip(local_index, 0, 3 * blocks_here - 1).reshape(-1)
-    attended_rows = attend(query_rows, k_parts, v_parts, local_index, count_rows)
+    attended_rows = attend(query_rows, kv_parts, local_index, count_rows)
     return lax.all_to_all(attended_rows, "head", split_axis=0, concat_axis=1, tiled=True)
 
 

time: 224 us -> 212 us (0.946)
  blocking collectives: 37.2 us -> 95.6 us
  waiting for transfers between devices: 98.1 us -> 52.9 us
  starting transfers between devices: 41.5 us -> 15.1 us
  local copies, waits for them, and re-layouts: 8.15 us -> 10.4 us
    all_to_all x0 -> x1, blocking collectives: none -> 63.5 us  [to_heads(): return lax.all_to_all(x, 'head', split_axis=1, concat_axis=0, tiled=True)]
    ppermute x4 -> x2, waiting for transfers between devices: 36.2 us -> 0.01 us  [from_behind(): return lax.ppermute(value, axis, pairs)]
    all_to_all x3 -> x1, starting transfers between devices: 23.5 us -> 5.76 us  [to_heads(): return lax.all_to_all(x, 'head', split_axis=1, concat_axis=0, tiled=True)]
    all_to_all x3 -> x1, waiting for transfers between devices: 61.9 us -> 52.9 us  [to_heads(): return lax.all_to_all(x, 'head', split_axis=1, concat_axis=0, tiled=True)]
    ppermute x4 -> x2, starting transfers between devices: 18.1 us -> 9.31 us  [from_behind(): return lax.ppermute(value, axis, pairs)]
    all_to_all x1, blocking collectives: 37.2 us -> 32.1 us  [local(): lax.all_to_all(attended_rows, 'head', split_axis=0, concat_axis=1, tiled=...]
  transfers between devices with their start and end apart: 7 -> 3, of which waited for: 7 -> 1; matrix products, arithmetic and copies ran while one was open for 2% -> 1% of each run, Pallas kernels for 0% -> 0%
where the time goes in v2:
time: 212 us; the launch traced here: 211 us
  blocking collectives  95.6 us (45%)
  waiting for transfers between devices  52.9 us (25%)
  Pallas kernels  36.8 us (17%)
  starting transfers between devices  15.1 us (7%)
  local copies, waits for them, and re-layouts  10.4 us (5%)
    all_to_all x1, blocking collectives, to_heads(): return lax.all_to_all(x, 'head', split_axis=1, concat_axis=0, tiled=True)  63.5 us
    all_to_all x1, waiting for transfers between devices, to_heads(): return lax.all_to_all(x, 'head', split_axis=1, concat_axis=0, tiled=True)  52.9 us
    pallas_call x1, Pallas kernels, attend(): pl.pallas_call(functools.partial(attention_kernel, shard_rows=shard_rows)...  36.8 us
    all_to_all x1, blocking collectives, local(): lax.all_to_all(attended_rows, 'head', split_axis=0, concat_axis=1, tiled=...  32.1 us
    ppermute x2, starting transfers between devices, from_behind(): return lax.ppermute(value, axis, pairs)  9.31 us
    all_to_all x1, starting transfers between devices, to_heads(): return lax.all_to_all(x, 'head', split_axis=1, concat_axis=0, tiled=True)  5.76 us
  transfers between devices with their start and end apart: 3, of which 1 were waited for; matrix products, arithmetic and copies ran while one was open for 1% of the time, Pallas kernels for 0%

profile of v2, /device:TPU:1, one launch (start us, length us, event | category | flops | bytes accessed | tf_op | source)
XLA Modules:
  0.0 211.1 jit_solution(8896454045505669243)
XLA Ops:
  0.0 0.0 copy-start
  0.0 1.6 copy.12
  1.6 0.0 copy-done.2
  1.6 0.2 copy.13
  1.9 0.2 pad_maximum_fusion
  2.1 2.2 %copy.8 = bf16[128,32,2,128]{3,2,0,1:T(2,128)(2,1)S(1)} copy(bf16[128,32,2,128]{3,1,0,2:T(8,128)(2,1)S(1)} %pad_maximum_fusion) | data formatting | bytes 4194304 | tf_op jit(solution)/shard_map/stack | solution.py:119
  4.3 2.6 %all_to_all.46 = bf16[128,32,256]{2,0,1:T(8,128)(2,1)} reshape(bf16[128,32,2,128]{3,2,0,1:T(2,128)(2,1)S(1)} %copy.8) | data formatting | bytes 4194304 | tf_op jit(solution)/shard_map/all_to_all | solution.py:115
  6.9 63.5 %all_to_all.57 = bf16[128,32,256]{2,0,1:T(8,128)(2,1)S(1)} all-to-all(bf16[128,32,256]{2,0,1:T(8,128)(2,1)} %all_to_all.46), channel_id=1, replica_groups=mesh['blk'=16,'head'=32] {'head'}, dimensions={1} | all-to-all | bytes 4194304 | tf_op jit(solution)/shard_map/all_to_all | solution.py:115
  70.4 7.4 %collective-permute-start.1 = (bf16[4096,256]{1,0:T(8,128)(2,1)S(1)}, bf16[4096,256]{1,0:T(8,128)(2,1)}, u32[]{:S(2)}, u32[]{:S(2)}) collective-permute-start(bf16[4096,256]{1,0:T(8,128)(2,1)S(1)} %bitcast.30), channel_id=1, source_target_pairs={{0,480},{32,0},{64,32},{96,64},{128,96},{160,128},{192,160},{224,1... | collective-permute-start | bytes 6291464 | tf_op jit(solution)/shard_map/ppermute | solution.py:18
  77.8 1.9 collective-permute-start
  79.7 0.0 copy-done
  79.7 1.3 copy_bitcast_fusion.1
  81.0 0.0 copy-done.1
  81.0 5.8 %all-to-all-start = ((bf16[128,32,128]{2,0,1:T(8,128)(2,1)}), bf16[128,32,128]{2,0,1:T(8,128)(2,1)}, u32[]{:S(2)}, u32[]{:S(2)}) async-start(bf16[128,32,128]{2,0,1:T(8,128)(2,1)} %copy_bitcast_fusion.1), calls=%async_computation | async-start | bytes 2097152 | tf_op jit(solution)/shard_map/all_to_all | solution.py:115
  86.8 0.7 dynamic_slice.7.cnt_ref
  87.4 0.1 fusion.1
  87.5 0.1 copy.6
  87.6 0.6 reshape.14.idx_ref
  88.2 52.9 %all-to-all-done = bf16[128,32,128]{2,0,1:T(8,128)(2,1)} async-done(((bf16[128,32,128]{2,0,1:T(8,128)(2,1)}), bf16[128,32,128]{2,0,1:T(8,128)(2,1)}, u32[]{:S(2)}, u32[]{:S(2)}) %all-to-all-start) | async-done | bytes 1048608 | tf_op jit(solution)/shard_map/all_to_all | solution.py:115
  141.0 0.0 collective-permute-done.1.kv_next
  141.0 0.0 collective-permute-done.kv_prev
  141.0 36.8 %shard_map.55 = bf16[4096,128]{1,0:T(8,128)(2,1)} custom-call(s32[48]{0:T(128)} %reshape.14.idx_ref, s32[8]{0:T(128)} %dynamic_slice.7.cnt_ref, bf16[4096,128]{1,0:T(8,128)(2,1)} %bitcast.1.q_ref, bf16[4096,256]{1,0:T(8,128)(2,1)} %collective-permute-done.kv_prev, bf16[4096,256]{1,0:T(8,128)(2,1)} %bitcast.32, bf16[4096,256]{1,0:T(8,128)(2,1)} %collective-permute-done.1.kv_next), custom_call_target="tpu_custom_call" | custom-call | flops 6442450944 | bytes 8388608 | tf_op jit(solution)/shard_map/pallas_call | solution.py:102
  177.8 32.1 %all_to_all.58 = bf16[32,128,128]{2,1,0:T(8,128)(2,1)S(1)} all-to-all(bf16[32,128,128]{2,1,0:T(8,128)(2,1)} %bitcast.35), channel_id=1, replica_groups=mesh['blk'=16,'head'=32] {'head'}, dimensions={0} | all-to-all | bytes 2097152 | tf_op jit(solution)/shard_map/all_to_all | solution.py:133
  210.0 1.1 copy_bitcast_fusion
  (6 shorter events, 0.0 us)
Async XLA Ops:
  0.0 79.7 %copy-start = (bf16[128,4096]{1,0:T(8,128)(2,1)S(1)}, bf16[128,4096]{1,0:T(8,128)(2,1)}, u32[]{:S(2)}) copy-start(bf16[128,4096]{1,0:T(8,128)(2,1)} %param.5) | copy-start | bytes 3145732
  0.0 1.6 copy-start.2
  70.4 10.6 %copy-start.1 = (bf16[128,32,256]{2,0,1:T(8,128)(2,1)}, bf16[128,32,256]{2,0,1:T(8,128)(2,1)S(1)}, u32[]{:S(2)}) copy-start(bf16[128,32,256]{2,0,1:T(8,128)(2,1)S(1)} %all_to_all.57) | copy-start | bytes 6291460
  70.4 16.4 %copy-start.4 = (s32[128]{0:T(128)S(1)}, s32[128]{0:T(128)}, u32[]{:S(2)}) copy-start(s32[128]{0:T(128)} %param.9) | copy-start | bytes 1540
  70.4 17.0 %copy-start.3 = (s32[128,6]{0,1:T(8,128)S(1)}, s32[128,6]{0,1:T(8,128)}, u32[]{:S(2)}) copy-start(s32[128,6]{0,1:T(8,128)} %param.8) | copy-start | bytes 9220
  70.4 70.7 %collective-permute-start.1 = (bf16[4096,256]{1,0:T(8,128)(2,1)S(1)}, bf16[4096,256]{1,0:T(8,128)(2,1)}, u32[]{:S(2)}, u32[]{:S(2)}) collective-permute-start(bf16[4096,256]{1,0:T(8,128)(2,1)S(1)} %bitcast.30), channel_id=1, source_target_pairs={{0,480},{32,0},{64,32},{96,64},{128,96},{160,128},{192,160},{224,1... | collective-permute-start | bytes 6291464 | tf_op jit(solution)/shard_map/ppermute | solution.py:18
  77.8 63.3 %collective-permute-start = (bf16[4096,256]{1,0:T(8,128)(2,1)S(1)}, bf16[4096,256]{1,0:T(8,128)(2,1)}, u32[]{:S(2)}, u32[]{:S(2)}) collective-permute-start(bf16[4096,256]{1,0:T(8,128)(2,1)S(1)} %bitcast.31), channel_id=1, source_target_pairs={{0,32},{32,64},{64,96},{96,128},{128,160},{160,192},{192,224},{224... | collective-permute-start | bytes 6291464 | tf_op jit(solution)/shard_map/ppermute | solution.py:18
  81.0 60.1 %all-to-all-start = ((bf16[128,32,128]{2,0,1:T(8,128)(2,1)}), bf16[128,32,128]{2,0,1:T(8,128)(2,1)}, u32[]{:S(2)}, u32[]{:S(2)}) async-start(bf16[128,32,128]{2,0,1:T(8,128)(2,1)} %copy_bitcast_fusion.1), calls=%async_computation | async-start | bytes 2097152 | tf_op jit(solution)/shard_map/all_to_all | solution.py:115

commit v3 on v2

--- a/solution.py
+++ b/solution.py
@@ -75,27 +75,28 @@
 
 def attend(query_rows, kv_parts, local_index, count_rows):
     rows, width = query_rows.shape
-    blocks_here = rows // BLOCK
     shard_rows = kv_parts[0].shape[0]
-    flops = blocks_here * MAXB * BLOCK * BLOCK * width * 4
+    blocks_here = shard_rows // BLOCK
+    q_block = rows // blocks_here
+    flops = blocks_here * MAXB * q_block * BLOCK * width * 4
     cost = pl.CostEstimate(
         flops=flops,
-        transcendentals=blocks_here * MAXB * BLOCK * BLOCK,
-        bytes_accessed=(2 + 6) * rows * width * 2,
+        transcendentals=blocks_here * MAXB * q_block * BLOCK,
+        bytes_accessed=(2 * rows + 6 * shard_rows) * width * 2,
     )
     any_spec = pl.BlockSpec(memory_space=pl.ANY)
     grid_spec = pltpu.PrefetchScalarGridSpec(
         num_scalar_prefetch=2,
         grid=(blocks_here,),
-        in_specs=[pl.BlockSpec((BLOCK, width), lambda b, idx, cnt: (b, 0))] + [any_spec] * 3,
-        out_specs=pl.BlockSpec((BLOCK, width), lambda b, idx, cnt: (b, 0)),
+        in_specs=[pl.BlockSpec((q_block, width), lambda b, idx, cnt: (b, 0))] + [any_spec] * 3,
+        out_specs=pl.BlockSpec((q_block, width), lambda b, idx, cnt: (b, 0)),
         scratch_shapes=[
             pltpu.VMEM((3 * shard_rows, width), jnp.bfloat16),
             pltpu.VMEM((3 * shard_rows, width), jnp.bfloat16),
-            pltpu.VMEM((MAXB, BLOCK, BLOCK), jnp.float32),
-            pltpu.VMEM((BLOCK, 1), jnp.float32),
-            pltpu.VMEM((BLOCK, 1), jnp.float32),
-            pltpu.VMEM((BLOCK, width), jnp.float32),
+            pltpu.VMEM((MAXB, q_block, BLOCK), jnp.float32),
+            pltpu.VMEM((q_block, 1), jnp.float32),
+            pltpu.VMEM((q_block, 1), jnp.float32),
+            pltpu.VMEM((q_block, width), jnp.float32),
             pltpu.SemaphoreType.DMA((6,)),
         ],
     )
@@ -120,17 +121,21 @@
         [keys.reshape(rows, heads, HD), values.reshape(rows, heads, HD)], axis=2
     ).reshape(rows, 2 * model)
     kv_rows = to_heads(paired)
-    query_rows = to_heads(queries)
+    half = rows // 2
+    query_halves = [to_heads(queries[:half]), to_heads(queries[half:])]
     kv_parts = (from_behind(kv_rows, "blk", 1), kv_rows, from_behind(kv_rows, "blk", -1))
-    blocks_here = query_rows.shape[0] // BLOCK
+    blocks_here = kv_rows.shape[0] // BLOCK
     total_blocks = blocks_here * cycle_size
     first_block = lax.axis_index("blk") * blocks_here
     listed_rows = lax.dynamic_slice_in_dim(key_blocks, first_block, blocks_here, 0)
     count_rows = lax.dynamic_slice_in_dim(counts, first_block, blocks_here, 0)
     local_index = jnp.mod(listed_rows - first_block + blocks_here, total_blocks)
     local_index = jnp.clip(local_index, 0, 3 * blocks_here - 1).reshape(-1)
-    attended_rows = attend(query_rows, kv_parts, local_index, count_rows)
-    return lax.all_to_all(attended_rows, "head", split_axis=0, concat_axis=1, tiled=True)
+    outs = []
+    for query_rows in query_halves:
+        attended_rows = attend(query_rows, kv_parts, local_index, count_rows)
+        outs.append(lax.all_to_all(attended_rows, "head", split_axis=0, concat_axis=1, tiled=True))
+    return jnp.concatenate(outs, axis=0)
 
 
 def solution(mesh):

time: 212 us -> 237 us (1.12)
  blocking collectives: 95.6 us -> 63.6 us
  Pallas kernels: 36.8 us -> 60.8 us
  starting transfers between devices: 15.1 us -> 34.4 us
  waiting for transfers between devices: 52.9 us -> 65.6 us
    all_to_all x1 -> x0, blocking collectives: 32.1 us -> none  [local(): lax.all_to_all(attended_rows, 'head', split_axis=0, concat_axis=1, tiled=...]
    pallas_call x1 -> x2, Pallas kernels: 36.8 us -> 60.8 us  [attend(): pl.pallas_call(functools.partial(attention_kernel, shard_rows=shard_rows)...]
    all_to_all x0 -> x2, waiting for transfers between devices: none -> 16.6 us  [local(): lax.all_to_all(attended_rows, 'head', split_axis=0, concat_axis=1, tiled=...]
    all_to_all x0 -> x2, starting transfers between devices: none -> 16.5 us  [local(): lax.all_to_all(attended_rows, 'head', split_axis=0, concat_axis=1, tiled=...]
    all_to_all x1 -> x2, waiting for transfers between devices: 52.9 us -> 49 us  [to_heads(): return lax.all_to_all(x, 'head', split_axis=1, concat_axis=0, tiled=True)]
    all_to_all x1 -> x2, starting transfers between devices: 5.76 us -> 8.71 us  [to_heads(): return lax.all_to_all(x, 'head', split_axis=1, concat_axis=0, tiled=True)]
  transfers between devices with their start and end apart: 3 -> 6, of which waited for: 1 -> 2; matrix products, arithmetic and copies ran while one was open for 1% -> 1% of each run, Pallas kernels for 0% -> 26%
where the time goes in v3:
time: 237 us; the launch traced here: 236 us
  waiting for transfers between devices  65.6 us (28%)
  blocking collectives  63.6 us (27%)
  Pallas kernels  60.8 us (26%)
  starting transfers between devices  34.4 us (15%)
  local copies, waits for them, and re-layouts  10 us (4%)
    all_to_all x1, blocking collectives, to_heads(): return lax.all_to_all(x, 'head', split_axis=1, concat_axis=0, tiled=True)  63.6 us
    pallas_call x2, Pallas kernels, attend(): pl.pallas_call(functools.partial(attention_kernel, shard_rows=shard_rows)...  60.8 us
    all_to_all x2, waiting for transfers between devices, to_heads(): return lax.all_to_all(x, 'head', split_axis=1, concat_axis=0, tiled=True)  49 us
    all_to_all x2, waiting for transfers between devices, local(): lax.all_to_all(attended_rows, 'head', split_axis=0, concat_axis=1, tiled=...  16.6 us
    all_to_all x2, starting transfers between devices, local(): lax.all_to_all(attended_rows, 'head', split_axis=0, concat_axis=1, tiled=...  16.5 us
    ppermute x2, starting transfers between devices, from_behind(): return lax.ppermute(value, axis, pairs)  9.17 us
    all_to_all x2, starting transfers between devices, to_heads(): return lax.all_to_all(x, 'head', split_axis=1, concat_axis=0, tiled=True)  8.71 us
  transfers between devices with their start and end apart: 6, of which 2 were waited for; matrix products, arithmetic and copies ran while one was open for 1% of the time, Pallas kernels for 26%

profile of v3, /device:TPU:1, one launch (start us, length us, event | category | flops | bytes accessed | tf_op | source)
XLA Modules:
  0.0 236.0 jit_solution(10344494834936631277)
XLA Ops:
  0.0 1.5 copy.16
  1.6 0.2 copy.17
  1.8 0.2 pad_maximum_fusion
  2.0 2.2 copy.8
  4.2 2.7 %all_to_all.74 = bf16[128,32,256]{2,0,1:T(8,128)(2,1)} reshape(bf16[128,32,2,128]{3,2,0,1:T(2,128)(2,1)S(1)} %copy.8) | data formatting | bytes 4194304 | tf_op jit(solution)/shard_map/all_to_all | solution.py:116
  6.8 63.6 %all_to_all.95 = bf16[128,32,256]{2,0,1:T(8,128)(2,1)S(1)} all-to-all(bf16[128,32,256]{2,0,1:T(8,128)(2,1)} %all_to_all.74), channel_id=1, replica_groups=mesh['blk'=16,'head'=32] {'head'}, dimensions={1} | all-to-all | bytes 4194304 | tf_op jit(solution)/shard_map/all_to_all | solution.py:116
  70.5 7.3 %collective-permute-start.1 = (bf16[4096,256]{1,0:T(8,128)(2,1)S(1)}, bf16[4096,256]{1,0:T(8,128)(2,1)}, u32[]{:S(2)}, u32[]{:S(2)}) collective-permute-start(bf16[4096,256]{1,0:T(8,128)(2,1)S(1)} %bitcast.45), channel_id=1, source_target_pairs={{0,480},{32,0},{64,32},{96,64},{128,96},{160,128},{192,160},{224,1... | collective-permute-start | bytes 6291464 | tf_op jit(solution)/shard_map/ppermute | solution.py:18
  77.7 1.9 collective-permute-start
  79.7 0.1 slice_bitcast_fusion.1
  79.8 0.9 copy.22
  80.7 5.0 %all-to-all-start.3 = ((bf16[64,32,128]{2,0,1:T(8,128)(2,1)}), bf16[64,32,128]{2,0,1:T(8,128)(2,1)S(1)}, u32[]{:S(2)}, u32[]{:S(2)}) async-start(bf16[64,32,128]{2,0,1:T(8,128)(2,1)} %bitcast.41), calls=%async_computation.3 | async-start | bytes 1048576 | tf_op jit(solution)/shard_map/all_to_all | solution.py:116
  85.8 0.9 copy.23
  86.7 49.0 %all-to-all-done.3 = bf16[64,32,128]{2,0,1:T(8,128)(2,1)S(1)} async-done(((bf16[64,32,128]{2,0,1:T(8,128)(2,1)}), bf16[64,32,128]{2,0,1:T(8,128)(2,1)S(1)}, u32[]{:S(2)}, u32[]{:S(2)}) %all-to-all-start.3) | async-done | bytes 524320 | tf_op jit(solution)/shard_map/all_to_all | solution.py:116
  135.7 3.7 %all-to-all-start = ((bf16[64,32,128]{2,0,1:T(8,128)(2,1)}), bf16[64,32,128]{2,0,1:T(8,128)(2,1)S(1)}, u32[]{:S(2)}, u32[]{:S(2)}) async-start(bf16[64,32,128]{2,0,1:T(8,128)(2,1)} %bitcast.42), calls=%async_computation | async-start | bytes 1048576 | tf_op jit(solution)/shard_map/all_to_all | solution.py:116
  139.4 0.6 dynamic_slice.7.cnt_ref
  140.0 0.1 fusion.1
  140.1 0.1 copy.6
  140.1 0.6 reshape.20.idx_ref
  140.8 30.4 %shard_map.56 = bf16[2048,128]{1,0:T(8,128)(2,1)} custom-call(s32[48]{0:T(128)} %reshape.20.idx_ref, s32[8]{0:T(128)} %dynamic_slice.7.cnt_ref, bf16[2048,128]{1,0:T(8,128)(2,1)} %bitcast.52, bf16[4096,256]{1,0:T(8,128)(2,1)} %collective-permute-done.kv_prev, bf16[4096,256]{1,0:T(8,128)(2,1)} %bitcast.47, bf16[4096,256]{1,0:T(8,128)(2,1)} %collective-permute-done.1.kv_next), custom_call_target="tpu_custom_call" | custom-call | flops 3221225472 | bytes 7340032 | tf_op jit(solution)/shard_map/pallas_call | solution.py:103
  171.2 8.2 %all-to-all-start.4 = ((bf16[32,64,128]{2,1,0:T(8,128)(2,1)}), bf16[32,64,128]{2,1,0:T(8,128)(2,1)S(1)}, u32[]{:S(2)}, u32[]{:S(2)}) async-start(bf16[32,64,128]{2,1,0:T(8,128)(2,1)} %bitcast.53), calls=%async_computation.4 | async-start | bytes 1048576 | tf_op jit(solution)/shard_map/all_to_all | solution.py:137
  179.5 30.4 %shard_map.55 = bf16[2048,128]{1,0:T(8,128)(2,1)} custom-call(s32[48]{0:T(128)} %reshape.20.idx_ref, s32[8]{0:T(128)} %dynamic_slice.7.cnt_ref, bf16[2048,128]{1,0:T(8,128)(2,1)} %bitcast.51, bf16[4096,256]{1,0:T(8,128)(2,1)} %collective-permute-done.kv_prev, bf16[4096,256]{1,0:T(8,128)(2,1)} %bitcast.48, bf16[4096,256]{1,0:T(8,128)(2,1)} %collective-permute-done.1.kv_next), custom_call_target="tpu_custom_call" | custom-call | flops 3221225472 | bytes 7340032 | tf_op jit(solution)/shard_map/pallas_call | solution.py:103
  209.9 8.3 %all-to-all-start.2 = ((bf16[32,64,128]{2,1,0:T(8,128)(2,1)}), bf16[32,64,128]{2,1,0:T(8,128)(2,1)S(1)}, u32[]{:S(2)}, u32[]{:S(2)}) async-start(bf16[32,64,128]{2,1,0:T(8,128)(2,1)} %bitcast.54), calls=%async_computation.2 | async-start | bytes 1048576 | tf_op jit(solution)/shard_map/all_to_all | solution.py:137
  218.2 16.6 %all-to-all-done.2 = bf16[32,64,128]{2,1,0:T(8,128)(2,1)S(1)} async-done(((bf16[32,64,128]{2,1,0:T(8,128)(2,1)}), bf16[32,64,128]{2,1,0:T(8,128)(2,1)S(1)}, u32[]{:S(2)}, u32[]{:S(2)}) %all-to-all-start.2) | async-done | bytes 524320 | tf_op jit(solution)/shard_map/all_to_all | solution.py:137
  235.0 1.1 pad_maximum_fusion.1
  (20 shorter events, 0.2 us)
Async XLA Ops:
  0.0 1.6 copy-start.1
  6.8 72.8 %copy-start.2 = (bf16[128,4096]{1,0:T(8,128)(2,1)S(1)}, bf16[128,4096]{1,0:T(8,128)(2,1)}, u32[]{:S(2)}) copy-start(bf16[128,4096]{1,0:T(8,128)(2,1)} %param.5) | copy-start | bytes 3145732
  70.5 10.3 %copy-start = (bf16[128,32,256]{2,0,1:T(8,128)(2,1)}, bf16[128,32,256]{2,0,1:T(8,128)(2,1)S(1)}, u32[]{:S(2)}) copy-start(bf16[128,32,256]{2,0,1:T(8,128)(2,1)S(1)} %all_to_all.95) | copy-start | bytes 6291460
  70.5 70.3 %collective-permute-start.1 = (bf16[4096,256]{1,0:T(8,128)(2,1)S(1)}, bf16[4096,256]{1,0:T(8,128)(2,1)}, u32[]{:S(2)}, u32[]{:S(2)}) collective-permute-start(bf16[4096,256]{1,0:T(8,128)(2,1)S(1)} %bitcast.45), channel_id=1, source_target_pairs={{0,480},{32,0},{64,32},{96,64},{128,96},{160,128},{192,160},{224,1... | collective-permute-start | bytes 6291464 | tf_op jit(solution)/shard_map/ppermute | solution.py:18
  77.7 63.0 %collective-permute-start = (bf16[4096,256]{1,0:T(8,128)(2,1)S(1)}, bf16[4096,256]{1,0:T(8,128)(2,1)}, u32[]{:S(2)}, u32[]{:S(2)}) collective-permute-start(bf16[4096,256]{1,0:T(8,128)(2,1)S(1)} %bitcast.46), channel_id=1, source_target_pairs={{0,32},{32,64},{64,96},{96,128},{128,160},{160,192},{192,224},{224... | collective-permute-start | bytes 6291464 | tf_op jit(solution)/shard_map/ppermute | solution.py:18
  79.8 59.6 %copy-start.6 = (s32[128]{0:T(128)S(1)}, s32[128]{0:T(128)}, u32[]{:S(2)}) copy-start(s32[128]{0:T(128)} %param.9) | copy-start | bytes 1540
  79.8 60.2 %copy-start.5 = (s32[128,6]{0,1:T(8,128)S(1)}, s32[128,6]{0,1:T(8,128)}, u32[]{:S(2)}) copy-start(s32[128,6]{0,1:T(8,128)} %param.8) | copy-start | bytes 9220
  80.7 54.9 %all-to-all-start.3 = ((bf16[64,32,128]{2,0,1:T(8,128)(2,1)}), bf16[64,32,128]{2,0,1:T(8,128)(2,1)S(1)}, u32[]{:S(2)}, u32[]{:S(2)}) async-start(bf16[64,32,128]{2,0,1:T(8,128)(2,1)} %bitcast.41), calls=%async_computation.3 | async-start | bytes 1048576 | tf_op jit(solution)/shard_map/all_to_all | solution.py:116
  135.7 5.1 %copy-start.4 = (bf16[64,32,128]{2,0,1:T(8,128)(2,1)}, bf16[64,32,128]{2,0,1:T(8,128)(2,1)S(1)}, u32[]{:S(2)}) copy-start(bf16[64,32,128]{2,0,1:T(8,128)(2,1)S(1)} %all-to-all-done.3) | copy-start | bytes 1572868
  135.7 35.5 %all-to-all-start = ((bf16[64,32,128]{2,0,1:T(8,128)(2,1)}), bf16[64,32,128]{2,0,1:T(8,128)(2,1)S(1)}, u32[]{:S(2)}, u32[]{:S(2)}) async-start(bf16[64,32,128]{2,0,1:T(8,128)(2,1)} %bitcast.42), calls=%async_computation | async-start | bytes 1048576 | tf_op jit(solution)/shard_map/all_to_all | solution.py:116
  171.2 8.3 %copy-start.3 = (bf16[64,32,128]{2,0,1:T(8,128)(2,1)}, bf16[64,32,128]{2,0,1:T(8,128)(2,1)S(1)}, u32[]{:S(2)}) copy-start(bf16[64,32,128]{2,0,1:T(8,128)(2,1)S(1)} %all-to-all-done) | copy-start | bytes 1572868
  171.2 38.7 %all-to-all-start.4 = ((bf16[32,64,128]{2,1,0:T(8,128)(2,1)}), bf16[32,64,128]{2,1,0:T(8,128)(2,1)S(1)}, u32[]{:S(2)}, u32[]{:S(2)}) async-start(bf16[32,64,128]{2,1,0:T(8,128)(2,1)} %bitcast.53), calls=%async_computation.4 | async-start | bytes 1048576 | tf_op jit(solution)/shard_map/all_to_all | solution.py:137
  209.9 25.0 %all-to-all-start.2 = ((bf16[32,64,128]{2,1,0:T(8,128)(2,1)}), bf16[32,64,128]{2,1,0:T(8,128)(2,1)S(1)}, u32[]{:S(2)}, u32[]{:S(2)}) async-start(bf16[32,64,128]{2,1,0:T(8,128)(2,1)} %bitcast.54), calls=%async_computation.2 | async-start | bytes 1048576 | tf_op jit(solution)/shard_map/all_to_all | solution.py:137

commit v4 on v2

--- a/solution.py
+++ b/solution.py
@@ -51,11 +51,11 @@
             start = pl.multiple_of(idx_ref[b * MAXB + j] * BLOCK, BLOCK)
             key_block = k_scr[pl.ds(start, BLOCK), :]
             scores = lax.dot_general(
-                q_ref[...], key_block, (((1,), (1,)), ((), ())),
+                key_block, q_ref[...], (((1,), (1,)), ((), ())),
                 preferred_element_type=jnp.float32,
             ) * scale
             s_scr[j] = scores
-            m_scr[...] = jnp.maximum(m_scr[...], jnp.max(scores, axis=1, keepdims=True))
+            m_scr[...] = jnp.maximum(m_scr[...], jnp.max(scores, axis=0, keepdims=True))
 
     l_scr[...] = jnp.zeros(l_scr.shape, jnp.float32)
     acc_scr[...] = jnp.zeros(acc_scr.shape, jnp.float32)
@@ -65,12 +65,13 @@
             start = pl.multiple_of(idx_ref[b * MAXB + j] * BLOCK, BLOCK)
             value_block = v_scr[pl.ds(start, BLOCK), :]
             expo = jnp.exp(s_scr[j] - m_scr[...])
-            l_scr[...] += jnp.sum(expo, axis=1, keepdims=True)
-            acc_scr[...] += jnp.dot(
-                expo.astype(jnp.bfloat16), value_block, preferred_element_type=jnp.float32
+            l_scr[...] += jnp.sum(expo, axis=0, keepdims=True)
+            acc_scr[...] += lax.dot_general(
+                value_block, expo.astype(jnp.bfloat16), (((0,), (0,)), ((), ())),
+                preferred_element_type=jnp.float32,
             )
 
-    o_ref[...] = (acc_scr[...] / l_scr[...]).astype(o_ref.dtype)
+    o_ref[...] = jnp.transpose(acc_scr[...] / l_scr[...]).astype(o_ref.dtype)
 
 
 def attend(query_rows, kv_parts, local_index, count_rows):
@@ -93,9 +94,9 @@
             pltpu.VMEM((3 * shard_rows, width), jnp.bfloat16),
             pltpu.VMEM((3 * shard_rows, width), jnp.bfloat16),
             pltpu.VMEM((MAXB, BLOCK, BLOCK), jnp.float32),
-            pltpu.VMEM((BLOCK, 1), jnp.float32),
-            pltpu.VMEM((BLOCK, 1), jnp.float32),
-            pltpu.VMEM((BLOCK, width), jnp.float32),
+            pltpu.VMEM((1, BLOCK), jnp.float32),
+            pltpu.VMEM((1, BLOCK), jnp.float32),
+            pltpu.VMEM((width, BLOCK), jnp.float32),
             pltpu.SemaphoreType.DMA((6,)),
         ],
     )

time: 212 us -> 207 us (0.976)
  Pallas kernels: 36.8 us -> 32.2 us
    pallas_call x1, Pallas kernels: 36.8 us -> 32.2 us  [attend(): pl.pallas_call(functools.partial(attention_kernel, shard_rows=shard_rows)...]
where the time goes in v4:
time: 207 us
  blocking collectives  95.6 us (46%)
  waiting for transfers between devices  52.9 us (26%)
  Pallas kernels  32.2 us (16%)
  starting transfers between devices  15.1 us (7%)
  local copies, waits for them, and re-layouts  10.4 us (5%)
    all_to_all x1, blocking collectives, to_heads(): return lax.all_to_all(x, 'head', split_axis=1, concat_axis=0, tiled=True)  63.5 us
    all_to_all x1, waiting for transfers between devices, to_heads(): return lax.all_to_all(x, 'head', split_axis=1, concat_axis=0, tiled=True)  52.9 us
    pallas_call x1, Pallas kernels, attend(): pl.pallas_call(functools.partial(attention_kernel, shard_rows=shard_rows)...  32.2 us
    all_to_all x1, blocking collectives, local(): lax.all_to_all(attended_rows, 'head', split_axis=0, concat_axis=1, tiled=...  32.1 us
    ppermute x2, starting transfers between devices, from_behind(): return lax.ppermute(value, axis, pairs)  9.31 us
    all_to_all x1, starting transfers between devices, to_heads(): return lax.all_to_all(x, 'head', split_axis=1, concat_axis=0, tiled=True)  5.76 us
  transfers between devices with their start and end apart: 3, of which 1 were waited for; matrix products, arithmetic and copies ran while one was open for 1% of the time, Pallas kernels for 0%

profile of v4, /device:TPU:1, one launch (start us, length us, event | category | flops | bytes accessed | tf_op | source)
XLA Modules:
  0.0 206.5 jit_solution(13088294224449334176)
XLA Ops:
  0.0 0.0 copy-start
  0.0 1.6 copy.12
  1.6 0.0 copy-done.2
  1.6 0.2 copy.13
  1.9 0.2 pad_maximum_fusion
  2.1 2.2 %copy.8 = bf16[128,32,2,128]{3,2,0,1:T(2,128)(2,1)S(1)} copy(bf16[128,32,2,128]{3,1,0,2:T(8,128)(2,1)S(1)} %pad_maximum_fusion) | data formatting | bytes 4194304 | tf_op jit(solution)/shard_map/stack | solution.py:120
  4.3 2.6 %all_to_all.46 = bf16[128,32,256]{2,0,1:T(8,128)(2,1)} reshape(bf16[128,32,2,128]{3,2,0,1:T(2,128)(2,1)S(1)} %copy.8) | data formatting | bytes 4194304 | tf_op jit(solution)/shard_map/all_to_all | solution.py:116
  6.9 63.5 %all_to_all.57 = bf16[128,32,256]{2,0,1:T(8,128)(2,1)S(1)} all-to-all(bf16[128,32,256]{2,0,1:T(8,128)(2,1)} %all_to_all.46), channel_id=1, replica_groups=mesh['blk'=16,'head'=32] {'head'}, dimensions={1} | all-to-all | bytes 4194304 | tf_op jit(solution)/shard_map/all_to_all | solution.py:116
  70.4 7.4 %collective-permute-start.1 = (bf16[4096,256]{1,0:T(8,128)(2,1)S(1)}, bf16[4096,256]{1,0:T(8,128)(2,1)}, u32[]{:S(2)}, u32[]{:S(2)}) collective-permute-start(bf16[4096,256]{1,0:T(8,128)(2,1)S(1)} %bitcast.30), channel_id=1, source_target_pairs={{0,480},{32,0},{64,32},{96,64},{128,96},{160,128},{192,160},{224,1... | collective-permute-start | bytes 6291464 | tf_op jit(solution)/shard_map/ppermute | solution.py:18
  77.8 1.9 collective-permute-start
  79.7 0.0 copy-done
  79.7 1.3 copy_bitcast_fusion.1
  81.0 0.0 copy-done.1
  81.0 5.8 %all-to-all-start = ((bf16[128,32,128]{2,0,1:T(8,128)(2,1)}), bf16[128,32,128]{2,0,1:T(8,128)(2,1)}, u32[]{:S(2)}, u32[]{:S(2)}) async-start(bf16[128,32,128]{2,0,1:T(8,128)(2,1)} %copy_bitcast_fusion.1), calls=%async_computation | async-start | bytes 2097152 | tf_op jit(solution)/shard_map/all_to_all | solution.py:116
  86.8 0.7 dynamic_slice.7.cnt_ref
  87.4 0.1 fusion.1
  87.5 0.1 copy.6
  87.6 0.6 reshape.14.idx_ref
  88.2 52.9 %all-to-all-done = bf16[128,32,128]{2,0,1:T(8,128)(2,1)} async-done(((bf16[128,32,128]{2,0,1:T(8,128)(2,1)}), bf16[128,32,128]{2,0,1:T(8,128)(2,1)}, u32[]{:S(2)}, u32[]{:S(2)}) %all-to-all-start) | async-done | bytes 1048608 | tf_op jit(solution)/shard_map/all_to_all | solution.py:116
  141.0 0.0 collective-permute-done.1.kv_next
  141.0 0.0 collective-permute-done.kv_prev
  141.0 32.2 %shard_map.55 = bf16[4096,128]{1,0:T(8,128)(2,1)} custom-call(s32[48]{0:T(128)} %reshape.14.idx_ref, s32[8]{0:T(128)} %dynamic_slice.7.cnt_ref, bf16[4096,128]{1,0:T(8,128)(2,1)} %bitcast.1.q_ref, bf16[4096,256]{1,0:T(8,128)(2,1)} %collective-permute-done.kv_prev, bf16[4096,256]{1,0:T(8,128)(2,1)} %bitcast.32, bf16[4096,256]{1,0:T(8,128)(2,1)} %collective-permute-done.1.kv_next), custom_call_target="tpu_custom_call" | custom-call | flops 6442450944 | bytes 8388608 | tf_op jit(solution)/shard_map/pallas_call | solution.py:103
  173.3 32.1 %all_to_all.58 = bf16[32,128,128]{2,1,0:T(8,128)(2,1)S(1)} all-to-all(bf16[32,128,128]{2,1,0:T(8,128)(2,1)} %bitcast.35), channel_id=1, replica_groups=mesh['blk'=16,'head'=32] {'head'}, dimensions={0} | all-to-all | bytes 2097152 | tf_op jit(solution)/shard_map/all_to_all | solution.py:134
  205.4 1.1 copy_bitcast_fusion
  (6 shorter events, 0.0 us)
Async XLA Ops:
  0.0 79.7 %copy-start = (bf16[128,4096]{1,0:T(8,128)(2,1)S(1)}, bf16[128,4096]{1,0:T(8,128)(2,1)}, u32[]{:S(2)}) copy-start(bf16[128,4096]{1,0:T(8,128)(2,1)} %param.5) | copy-start | bytes 3145732
  0.0 1.6 copy-start.2
  70.4 10.6 %copy-start.1 = (bf16[128,32,256]{2,0,1:T(8,128)(2,1)}, bf16[128,32,256]{2,0,1:T(8,128)(2,1)S(1)}, u32[]{:S(2)}) copy-start(bf16[128,32,256]{2,0,1:T(8,128)(2,1)S(1)} %all_to_all.57) | copy-start | bytes 6291460
  70.4 16.4 %copy-start.4 = (s32[128]{0:T(128)S(1)}, s32[128]{0:T(128)}, u32[]{:S(2)}) copy-start(s32[128]{0:T(128)} %param.9) | copy-start | bytes 1540
  70.4 17.0 %copy-start.3 = (s32[128,6]{0,1:T(8,128)S(1)}, s32[128,6]{0,1:T(8,128)}, u32[]{:S(2)}) copy-start(s32[128,6]{0,1:T(8,128)} %param.8) | copy-start | bytes 9220
  70.4 70.7 %collective-permute-start.1 = (bf16[4096,256]{1,0:T(8,128)(2,1)S(1)}, bf16[4096,256]{1,0:T(8,128)(2,1)}, u32[]{:S(2)}, u32[]{:S(2)}) collective-permute-start(bf16[4096,256]{1,0:T(8,128)(2,1)S(1)} %bitcast.30), channel_id=1, source_target_pairs={{0,480},{32,0},{64,32},{96,64},{128,96},{160,128},{192,160},{224,1... | collective-permute-start | bytes 6291464 | tf_op jit(solution)/shard_map/ppermute | solution.py:18
  77.8 63.3 %collective-permute-start = (bf16[4096,256]{1,0:T(8,128)(2,1)S(1)}, bf16[4096,256]{1,0:T(8,128)(2,1)}, u32[]{:S(2)}, u32[]{:S(2)}) collective-permute-start(bf16[4096,256]{1,0:T(8,128)(2,1)S(1)} %bitcast.31), channel_id=1, source_target_pairs={{0,32},{32,64},{64,96},{96,128},{128,160},{160,192},{192,224},{224... | collective-permute-start | bytes 6291464 | tf_op jit(solution)/shard_map/ppermute | solution.py:18
  81.0 60.1 %all-to-all-start = ((bf16[128,32,128]{2,0,1:T(8,128)(2,1)}), bf16[128,32,128]{2,0,1:T(8,128)(2,1)}, u32[]{:S(2)}, u32[]{:S(2)}) async-start(bf16[128,32,128]{2,0,1:T(8,128)(2,1)} %copy_bitcast_fusion.1), calls=%async_computation | async-start | bytes 2097152 | tf_op jit(solution)/shard_map/all_to_all | solution.py:116

commit v5 on v4

v5 whole, which is shorter than its diff:
```python
import functools

import jax
import jax.numpy as jnp
from jax import lax
from jax.experimental import pallas as pl
from jax.experimental.pallas import tpu as pltpu
from jax.sharding import PartitionSpec as P

HD = 128
BLOCK = 512
MAXB = 6


def from_behind(value, axis, steps):
    count = lax.axis_size(axis)
    pairs = [(source, (source + steps) % count) for source in range(count)]
    return lax.ppermute(value, axis, pairs)


def own_kernel(idx_ref, cnt_ref, q_ref, kv_own, m_ref, l_ref, acc_ref,
               k_scr, v_scr, s_scr, sem, *, blocks):
    b = pl.program_id(0)
    width = q_ref.shape[1]
    shard_rows = blocks * BLOCK

    @pl.when(b == 0)
    def _load_context():
        copies = [
            pltpu.make_async_copy(kv_own.at[:, pl.ds(0, width)], k_scr, sem.at[0]),
            pltpu.make_async_copy(kv_own.at[:, pl.ds(width, width)], v_scr, sem.at[1]),
        ]
        for copy in copies:
            copy.start()
        for copy in copies:
            copy.wait()

    scale = HD ** (-0.5)
    amount = cnt_ref[b]

    def usable(j):
        g = idx_ref[b * MAXB + j]
        return (j < amount) & (g >= blocks) & (g < 2 * blocks)

    def row(j):
        return pl.multiple_of((idx_ref[b * MAXB + j] - blocks) * BLOCK, BLOCK)

    m_ref[...] = jnp.full(m_ref.shape, -jnp.inf, jnp.float32)
    for j in range(MAXB):
        @pl.when(usable(j))
        def _scores():
            scores = lax.dot_general(
                k_scr[pl.ds(row(j), BLOCK), :], q_ref[...], (((1,), (1,)), ((), ())),
                preferred_element_type=jnp.float32,
            ) * scale
            s_scr[j] = scores
            m_ref[...] = jnp.maximum(m_ref[...], jnp.max(scores, axis=0, keepdims=True))

    l_ref[...] = jnp.zeros(l_ref.shape, jnp.float32)
    acc_ref[...] = jnp.zeros(acc_ref.shape, jnp.float32)
    for j in range(MAXB):
        @pl.when(usable(j))
        def _mix():
            expo = jnp.exp(s_scr[j] - m_ref[...])
            l_ref[...] += jnp.sum(expo, axis=0, keepdims=True)
            acc_ref[...] += lax.dot_general(
                v_scr[pl.ds(row(j), BLOCK), :], expo.astype(jnp.bfloat16),
                (((0,), (0,)), ((), ())), preferred_element_type=jnp.float32,
            )


def rest_kernel(idx_ref, cnt_ref, q_ref, m_in, l_in, acc_in, kv_prev, kv_next, o_ref,
                k_scr, v_scr, s_scr, m_scr, l_scr, acc_scr, sem, *, blocks):
    b = pl.program_id(0)
    width = q_ref.shape[1]
    shard_rows = blocks * BLOCK

    @pl.when(b == 0)
    def _load_context():
        copies = []
        for i, (src, dst, part) in enumerate(
            ((kv_prev.at[:, pl.ds(0, width)], k_scr, 0),
             (kv_next.at[:, pl.ds(0, width)], k_scr, 1),
             (kv_prev.at[:, pl.ds(width, width)], v_scr, 0),
             (kv_next.at[:, pl.ds(width, width)], v_scr, 1))
        ):
            copy = pltpu.make_async_copy(
                src, dst.at[pl.ds(part * shard_rows, shard_rows)], sem.at[i]
            )
            copy.start()
            copies.append(copy)
        for copy in copies:
            copy.wait()

    scale = HD ** (-0.5)
    amount = cnt_ref[b]

    def usable(j):
        g = idx_ref[b * MAXB + j]
        return (j < amount) & ((g < blocks) | (g >= 2 * blocks))

    def row(j):
        g = idx_ref[b * MAXB + j]
        return pl.multiple_of(jnp.where(g < blocks, g, g - blocks) * BLOCK, BLOCK)

    m_scr[...] = m_in[...]
    for j in range(MAXB):
        @pl.when(usable(j))
        def _scores():
            scores = lax.dot_general(
                k_scr[pl.ds(row(j), BLOCK), :], q_ref[...], (((1,), (1,)), ((), ())),
                preferred_element_type=jnp.float32,
            ) * scale
            s_scr[j] = scores
            m_scr[...] = jnp.maximum(m_scr[...], jnp.max(scores, axis=0, keepdims=True))

    alpha = jnp.exp(m_in[...] - m_scr[...])
    l_scr[...] = alpha * l_in[...]
    acc_scr[...] = alpha * acc_in[...]
    for j in range(MAXB):
        @pl.when(usable(j))
        def _mix():
            expo = jnp.exp(s_scr[j] - m_scr[...])
            l_scr[...] += jnp.sum(expo, axis=0, keepdims=True)
            acc_scr[...] += lax.dot_general(
                v_scr[pl.ds(row(j), BLOCK), :], expo.astype(jnp.bfloat16),
                (((0,), (0,)), ((), ())), preferred_element_type=jnp.float32,
            )

    o_ref[...] = jnp.transpose(acc_scr[...] / l_scr[...]).astype(o_ref.dtype)


def attend_own(query_rows, kv_own, local_index, count_rows):
    rows, width = query_rows.shape
    blocks = rows // BLOCK
    cost = pl.CostEstimate(
        flops=blocks * 4 * BLOCK * BLOCK * width * 4,
        transcendentals=blocks * 4 * BLOCK * BLOCK,
        bytes_accessed=rows * width * 2 * 3 + blocks * (width + 2) * BLOCK * 4,
    )
    q_spec = pl.BlockSpec((BLOCK, width), lambda b, idx, cnt: (b, 0))
    row_spec = pl.BlockSpec((None, 1, BLOCK), lambda b, idx, cnt: (b, 0, 0))
    acc_spec = pl.BlockSpec((None, width, BLOCK), lambda b, idx, cnt: (b, 0, 0))
    grid_spec = pltpu.PrefetchScalarGridSpec(
        num_scalar_prefetch=2,
        grid=(blocks,),
        in_specs=[q_spec, pl.BlockSpec(memory_space=pl.ANY)],
        out_specs=[row_spec, row_spec, acc_spec],
        scratch_shapes=[
            pltpu.VMEM((rows, width), jnp.bfloat16),
            pltpu.VMEM((rows, width), jnp.bfloat16),
            pltpu.VMEM((MAXB, BLOCK, BLOCK), jnp.float32),
            pltpu.SemaphoreType.DMA((2,)),
        ],
    )
    return pl.pallas_call(
        functools.partial(own_kernel, blocks=blocks),
        out_shape=[
            jax.ShapeDtypeStruct((blocks, 1, BLOCK), jnp.float32),
            jax.ShapeDtypeStruct((blocks, 1, BLOCK), jnp.float32),
            jax.ShapeDtypeStruct((blocks, width, BLOCK), jnp.float32),
        ],
        grid_spec=grid_spec,
        compiler_params=pltpu.CompilerParams(dimension_semantics=("arbitrary",)),
        cost_estimate=cost,
    )(local_index, count_rows, query_rows, kv_own)


def attend_rest(query_rows, partial, kv_prev, kv_next, local_index, count_rows):
    rows, width = query_rows.shape
    blocks = rows // BLOCK
    cost = pl.CostEstimate(
        flops=blocks * 2 * BLOCK * BLOCK * width * 4,
        transcendentals=blocks * 2 * BLOCK * BLOCK,
        bytes_accessed=rows * width * 2 * 6 + blocks * (width + 2) * BLOCK * 4,
    )
    q_spec = pl.BlockSpec((BLOCK, width), lambda b, idx, cnt: (b, 0))
    row_spec = pl.BlockSpec((None, 1, BLOCK), lambda b, idx, cnt: (b, 0, 0))
    acc_spec = pl.BlockSpec((None, width, BLOCK), lambda b, idx, cnt: (b, 0, 0))
    any_spec = pl.BlockSpec(memory_space=pl.ANY)
    grid_spec = pltpu.PrefetchScalarGridSpec(
        num_scalar_prefetch=2,
        grid=(blocks,),
        in_specs=[q_spec, row_spec, row_spec, acc_spec, any_spec, any_spec],
        out_specs=q_spec,
        scratch_shapes=[
            pltpu.VMEM((2 * rows, width), jnp.bfloat16),
            pltpu.VMEM((2 * rows, width), jnp.bfloat16),
            pltpu.VMEM((MAXB, BLOCK, BLOCK), jnp.float32),
            pltpu.VMEM((1, BLOCK), jnp.float32),
            pltpu.VMEM((1, BLOCK), jnp.float32),
            pltpu.VMEM((width, BLOCK), jnp.float32),
            pltpu.SemaphoreType.DMA((4,)),
        ],
    )
    return pl.pallas_call(
        functools.partial(rest_kernel, blocks=blocks),
        out_shape=jax.ShapeDtypeStruct((rows, width), jnp.bfloat16),
        grid_spec=grid_spec,
        compiler_params=pltpu.CompilerParams(dimension_semantics=("arbitrary",)),
        cost_estimate=cost,
    )(local_index, count_rows, query_rows, *partial, kv_prev, kv_next)


def local(queries, keys, values, key_blocks, counts):
    cycle_size = lax.axis_size("blk")

    def to_heads(x):
        return lax.all_to_all(x, "head", split_axis=1, concat_axis=0, tiled=True)

    rows, model = keys.shape
    heads = model // HD
    query_rows = to_heads(queries)
    after_queries = (query_rows[0, 0] * 0).astype(keys.dtype)
    paired = jnp.stack(
        [keys.reshape(rows, heads, HD), values.reshape(rows, heads, HD) + after_queries], axis=2
    ).reshape(rows, 2 * model)
    kv_rows = to_heads(paired)
    blocks_here = query_rows.shape[0] // BLOCK
    total_blocks = blocks_here * cycle_size
    first_block = lax.axis_index("blk") * blocks_here
    listed_rows = lax.dynamic_slice_in_dim(key_blocks, first_block, blocks_here, 0)
    count_rows = lax.dynamic_slice_in_dim(counts, first_block, blocks_here, 0)
    local_index = jnp.mod(listed_rows - first_block + blocks_here, total_blocks)
    local_index = jnp.clip(local_index, 0, 3 * blocks_here - 1).reshape(-1)
    partial = attend_own(query_rows, kv_rows, local_index, count_rows)
    kv_prev = from_behind(kv_rows, "blk", 1)
    kv_next = from_behind(kv_rows, "blk", -1)
    attended_rows = attend_rest(query_rows, partial, kv_prev, kv_next, local_index, count_rows)
    return lax.all_to_all(attended_rows, "head", split_axis=0, concat_axis=1, tiled=True)


def solution(mesh):
    placed = (
        P(("blk", "head"), None),
        P(("blk", "head"), None),
        P(("blk", "head"), None),
        P(),
        P(),
    )
    return jax.shard_map(
        local, mesh=mesh, in_specs=placed, out_specs=P(("blk", "head"), None), check_vma=False
    )
```

time: 207 us -> 218 us (1.053)
  starting transfers between devices: 15.1 us -> 22.1 us
  blocking collectives: 95.6 us -> 90.8 us
  Pallas kernels: 32.2 us -> 34.8 us
    ppermute x2, waiting for transfers between devices: 0.01 us -> 27.7 us  [from_behind(): return lax.ppermute(value, axis, pairs)]
    all_to_all x1, waiting for transfers between devices: 52.9 us -> 26.7 us  [to_heads(): return lax.all_to_all(x, 'head', split_axis=1, concat_axis=0, tiled=True)]
    all_to_all x1, starting transfers between devices: 5.76 us -> 12.9 us  [to_heads(): return lax.all_to_all(x, 'head', split_axis=1, concat_axis=0, tiled=True)]
    all_to_all x1, blocking collectives: 63.5 us -> 56.4 us  [to_heads(): return lax.all_to_all(x, 'head', split_axis=1, concat_axis=0, tiled=True)]
    pallas_call x1 -> x2, Pallas kernels: 32.2 us -> 34.8 us  [the longest x1 20.2 us: attend_own(): pl.pallas_call(functools.partial(own_kernel, blocks=blocks), out_shape=[j...]
    all_to_all x1, blocking collectives: 32.1 us -> 34.4 us  [local(): lax.all_to_all(attended_rows, 'head', split_axis=0, concat_axis=1, tiled=...]
  transfers between devices with their start and end apart: 3 -> 3, of which waited for: 1 -> 3; matrix products, arithmetic and copies ran while one was open for 1% -> 1% of each run, Pallas kernels for 0% -> 9%
where the time goes in v5:
time: 218 us; the launch traced here: 216 us
  blocking collectives  90.8 us (42%)
  waiting for transfers between devices  54.4 us (25%)
  Pallas kernels  34.8 us (16%)
  starting transfers between devices  22.1 us (10%)
  local copies, waits for them, and re-layouts  12 us (6%)
    all_to_all x1, blocking collectives, to_heads(): return lax.all_to_all(x, 'head', split_axis=1, concat_axis=0, tiled=True)  56.4 us
    all_to_all x1, blocking collectives, local(): lax.all_to_all(attended_rows, 'head', split_axis=0, concat_axis=1, tiled=...  34.4 us
    ppermute x2, waiting for transfers between devices, from_behind(): return lax.ppermute(value, axis, pairs)  27.7 us
    all_to_all x1, waiting for transfers between devices, to_heads(): return lax.all_to_all(x, 'head', split_axis=1, concat_axis=0, tiled=True)  26.7 us
    pallas_call x1, Pallas kernels, attend_own(): pl.pallas_call(functools.partial(own_kernel, blocks=blocks), out_shape=[j...  20.2 us
    pallas_call x1, Pallas kernels, attend_rest(): pl.pallas_call(functools.partial(rest_kernel, blocks=blocks), out_shape=j...  14.6 us
    all_to_all x1, starting transfers between devices, to_heads(): return lax.all_to_all(x, 'head', split_axis=1, concat_axis=0, tiled=True)  12.9 us
    ppermute x2, starting transfers between devices, from_behind(): return lax.ppermute(value, axis, pairs)  9.17 us
  transfers between devices with their start and end apart: 3, of which 3 were waited for; matrix products, arithmetic and copies ran while one was open for 1% of the time, Pallas kernels for 9%

profile of v5, /device:TPU:1, one launch (start us, length us, event | category | flops | bytes accessed | tf_op | source)
XLA Modules:
  0.0 216.3 jit_solution(16263914174003161906)
XLA Ops:
  0.0 1.2 copy-done
  1.2 1.3 copy_bitcast_fusion.1
  2.5 12.9 %all-to-all-start = ((bf16[128,32,128]{2,0,1:T(8,128)(2,1)}), bf16[128,32,128]{2,0,1:T(8,128)(2,1)S(1)}, u32[]{:S(2)}, u32[]{:S(2)}) async-start(bf16[128,32,128]{2,0,1:T(8,128)(2,1)} %copy_bitcast_fusion.1), calls=%async_computation | async-start | bytes 2097152 | tf_op jit(solution)/shard_map/all_to_all | solution.py:209
  15.4 1.4 copy.12
  16.9 26.7 %all-to-all-done = bf16[128,32,128]{2,0,1:T(8,128)(2,1)S(1)} async-done(((bf16[128,32,128]{2,0,1:T(8,128)(2,1)}), bf16[128,32,128]{2,0,1:T(8,128)(2,1)S(1)}, u32[]{:S(2)}, u32[]{:S(2)}) %all-to-all-start) | async-done | bytes 1048608 | tf_op jit(solution)/shard_map/all_to_all | solution.py:209
  43.5 0.6 slice.4
  44.8 1.3 add_bitcast_fusion
  46.1 0.2 copy.13
  46.3 0.2 pad_maximum_fusion
  46.5 2.2 copy.8
  48.7 2.6 %all_to_all.46 = bf16[128,32,256]{2,0,1:T(8,128)(2,1)} reshape(bf16[128,32,2,128]{3,2,0,1:T(2,128)(2,1)S(1)} %copy.8) | data formatting | bytes 4194304 | tf_op jit(solution)/shard_map/all_to_all | solution.py:209
  51.3 56.4 %all_to_all.57 = bf16[128,32,256]{2,0,1:T(8,128)(2,1)} all-to-all(bf16[128,32,256]{2,0,1:T(8,128)(2,1)} %all_to_all.46), channel_id=1, replica_groups=mesh['blk'=16,'head'=32] {'head'}, dimensions={1} | all-to-all | bytes 4194304 | tf_op jit(solution)/shard_map/all_to_all | solution.py:209
  107.7 7.3 %collective-permute-start.1 = (bf16[4096,256]{1,0:T(8,128)(2,1)}, bf16[4096,256]{1,0:T(8,128)(2,1)S(1)}, u32[]{:S(2)}, u32[]{:S(2)}) collective-permute-start(bf16[4096,256]{1,0:T(8,128)(2,1)} %bitcast.5.kv_own), channel_id=1, source_target_pairs={{0,480},{32,0},{64,32},{96,64},{128,96},{160,128},{192,160},{224,1... | collective-permute-start | bytes 6291464 | tf_op jit(solution)/shard_map/ppermute | solution.py:18
  114.9 1.9 collective-permute-start
  116.9 0.7 dynamic_slice.7.cnt_ref
  117.5 0.1 fusion.1
  117.6 0.1 copy.6
  117.7 0.6 reshape.29.idx_ref
  118.3 20.2 %shard_map.55 = (f32[8,1,512]{2,1,0:T(1,128)}, f32[8,1,512]{2,1,0:T(1,128)}, f32[8,128,512]{2,1,0:T(8,128)}) custom-call(s32[48]{0:T(128)} %reshape.29.idx_ref, s32[8]{0:T(128)} %dynamic_slice.7.cnt_ref, bf16[4096,128]{1,0:T(8,128)(2,1)} %bitcast.31, bf16[4096,256]{1,0:T(8,128)(2,1)} %bitcast.5.kv_own), custom_call_target="tpu_custom_call" | custom-call | flops 4294967296 | bytes 5275648 | tf_op jit(solution)/shard_map/pallas_call | solution.py:156
  138.5 20.2 %collective-permute-done.1.kv_next = bf16[4096,256]{1,0:T(8,128)(2,1)S(1)} collective-permute-done((bf16[4096,256]{1,0:T(8,128)(2,1)}, bf16[4096,256]{1,0:T(8,128)(2,1)S(1)}, u32[]{:S(2)}, u32[]{:S(2)}) %collective-permute-start.1) | collective-permute-done | bytes 2097184 | tf_op jit(solution)/shard_map/ppermute | solution.py:18
  158.8 7.4 %collective-permute-done.kv_prev = bf16[4096,256]{1,0:T(8,128)(2,1)} collective-permute-done((bf16[4096,256]{1,0:T(8,128)(2,1)}, bf16[4096,256]{1,0:T(8,128)(2,1)}, u32[]{:S(2)}, u32[]{:S(2)}) %collective-permute-start) | collective-permute-done | bytes 2097184 | tf_op jit(solution)/shard_map/ppermute | solution.py:18
  166.2 14.6 %shard_map.56 = bf16[4096,128]{1,0:T(8,128)(2,1)} custom-call(s32[48]{0:T(128)} %reshape.29.idx_ref, s32[8]{0:T(128)} %dynamic_slice.7.cnt_ref, bf16[4096,128]{1,0:T(8,128)(2,1)} %bitcast.32, f32[8,1,512]{2,1,0:T(1,128)} %get-tuple-element.8.m_in, f32[8,1,512]{2,1,0:T(1,128)} %get-tuple-element.9.l_in, f32[8,128,512]{2,1,0:T(8,128)} %get-tuple-element.10.acc_in, ...), custom_call_target="tpu_custom_call" | custom-call | flops 2147483648 | bytes 8421376 | tf_op jit(solution)/shard_map/pallas_call | solution.py:196
  180.8 34.4 %all_to_all.58 = bf16[32,128,128]{2,1,0:T(8,128)(2,1)S(1)} all-to-all(bf16[32,128,128]{2,1,0:T(8,128)(2,1)} %bitcast.33), channel_id=1, replica_groups=mesh['blk'=16,'head'=32] {'head'}, dimensions={0} | all-to-all | bytes 2097152 | tf_op jit(solution)/shard_map/all_to_all | solution.py:230
  215.2 1.1 copy_bitcast_fusion
  (9 shorter events, 0.0 us)
Async XLA Ops:
  0.0 1.2 copy-start
  2.5 41.1 %all-to-all-start = ((bf16[128,32,128]{2,0,1:T(8,128)(2,1)}), bf16[128,32,128]{2,0,1:T(8,128)(2,1)S(1)}, u32[]{:S(2)}, u32[]{:S(2)}) async-start(bf16[128,32,128]{2,0,1:T(8,128)(2,1)} %copy_bitcast_fusion.1), calls=%async_computation | async-start | bytes 2097152 | tf_op jit(solution)/shard_map/all_to_all | solution.py:209
  43.5 2.8 %copy-start.1 = (bf16[128,32,128]{2,0,1:T(8,128)(2,1)}, bf16[128,32,128]{2,0,1:T(8,128)(2,1)S(1)}, u32[]{:S(2)}) copy-start(bf16[128,32,128]{2,0,1:T(8,128)(2,1)S(1)} %all-to-all-done) | copy-start | bytes 3145732
  51.3 65.6 %copy-start.4 = (s32[128]{0:T(128)S(1)}, s32[128]{0:T(128)}, u32[]{:S(2)}) copy-start(s32[128]{0:T(128)} %param.9) | copy-start | bytes 1540
  51.3 66.2 %copy-start.3 = (s32[128,6]{0,1:T(8,128)S(1)}, s32[128,6]{0,1:T(8,128)}, u32[]{:S(2)}) copy-start(s32[128,6]{0,1:T(8,128)} %param.8) | copy-start | bytes 9220
  107.7 51.1 %collective-permute-start.1 = (bf16[4096,256]{1,0:T(8,128)(2,1)}, bf16[4096,256]{1,0:T(8,128)(2,1)S(1)}, u32[]{:S(2)}, u32[]{:S(2)}) collective-permute-start(bf16[4096,256]{1,0:T(8,128)(2,1)} %bitcast.5.kv_own), channel_id=1, source_target_pairs={{0,480},{32,0},{64,32},{96,64},{128,96},{160,128},{192,160},{224,1... | collective-permute-start | bytes 6291464 | tf_op jit(solution)/shard_map/ppermute | solution.py:18
  114.9 51.3 %collective-permute-start = (bf16[4096,256]{1,0:T(8,128)(2,1)}, bf16[4096,256]{1,0:T(8,128)(2,1)}, u32[]{:S(2)}, u32[]{:S(2)}) collective-permute-start(bf16[4096,256]{1,0:T(8,128)(2,1)} %bitcast.5.kv_own), channel_id=1, source_target_pairs={{0,32},{32,64},{64,96},{96,128},{128,160},{160,192},{192,224},{224... | collective-permute-start | bytes 6291464 | tf_op jit(solution)/shard_map/ppermute | solution.py:18
  158.7 7.5 %copy-start.2 = (bf16[4096,256]{1,0:T(8,128)(2,1)}, bf16[4096,256]{1,0:T(8,128)(2,1)S(1)}, u32[]{:S(2)}) copy-start(bf16[4096,256]{1,0:T(8,128)(2,1)S(1)} %collective-permute-done.1.kv_next) | copy-start | bytes 6291460

commit v6 on v4

--- a/solution.py
+++ b/solution.py
@@ -10,6 +10,7 @@
 HD = 128
 BLOCK = 512
 MAXB = 6
+TILES = 4
 
 
 def from_behind(value, axis, steps):
@@ -19,23 +20,23 @@
 
 
 def attention_kernel(idx_ref, cnt_ref, q_ref, kv_prev, kv_own, kv_next, o_ref,
-                     k_scr, v_scr, s_scr, m_scr, l_scr, acc_scr, sem, *, shard_rows):
+                     k_scr, v_scr, s_scr, m_scr, l_scr, acc_scr, sem):
     b = pl.program_id(0)
-    width = q_ref.shape[1]
+    sources = kv_own.shape[0]
 
     @pl.when(b == 0)
     def _load_context():
         copies = []
         for i, (src, dst, part) in enumerate(
-            ((kv_own.at[:, pl.ds(0, width)], k_scr, 1),
-             (kv_own.at[:, pl.ds(width, width)], v_scr, 1),
-             (kv_prev.at[:, pl.ds(0, width)], k_scr, 0),
-             (kv_next.at[:, pl.ds(0, width)], k_scr, 2),
-             (kv_prev.at[:, pl.ds(width, width)], v_scr, 0),
-             (kv_next.at[:, pl.ds(width, width)], v_scr, 2))
+            ((kv_own.at[:, 0], k_scr, 1),
+             (kv_own.at[:, 1], v_scr, 1),
+             (kv_prev.at[:, 0], k_scr, 0),
+             (kv_next.at[:, 0], k_scr, 2),
+             (kv_prev.at[:, 1], v_scr, 0),
+             (kv_next.at[:, 1], v_scr, 2))
         ):
             copy = pltpu.make_async_copy(
-                src, dst.at[pl.ds(part * shard_rows, shard_rows)], sem.at[i]
+                src, dst.at[pl.ds(part * sources, sources)], sem.at[i]
             )
             copy.start()
             copies.append(copy)
@@ -48,8 +49,8 @@
     for j in range(MAXB):
         @pl.when(j < amount)
         def _scores():
-            start = pl.multiple_of(idx_ref[b * MAXB + j] * BLOCK, BLOCK)
-            key_block = k_scr[pl.ds(start, BLOCK), :]
+            start = pl.multiple_of(idx_ref[b * MAXB + j] * TILES, TILES)
+            key_block = k_scr[pl.ds(start, TILES)].reshape(BLOCK, HD)
             scores = lax.dot_general(
                 key_block, q_ref[...], (((1,), (1,)), ((), ())),
                 preferred_element_type=jnp.float32,
@@ -62,8 +63,8 @@
     for j in range(MAXB):
         @pl.when(j < amount)
         def _mix():
-            start = pl.multiple_of(idx_ref[b * MAXB + j] * BLOCK, BLOCK)
-            value_block = v_scr[pl.ds(start, BLOCK), :]
+            start = pl.multiple_of(idx_ref[b * MAXB + j] * TILES, TILES)
+            value_block = v_scr[pl.ds(start, TILES)].reshape(BLOCK, HD)
             expo = jnp.exp(s_scr[j] - m_scr[...])
             l_scr[...] += jnp.sum(expo, axis=0, keepdims=True)
             acc_scr[...] += lax.dot_general(
@@ -77,7 +78,7 @@
 def attend(query_rows, kv_parts, local_index, count_rows):
     rows, width = query_rows.shape
     blocks_here = rows // BLOCK
-    shard_rows = kv_parts[0].shape[0]
+    sources, _, tile, _ = kv_parts[0].shape
     flops = blocks_here * MAXB * BLOCK * BLOCK * width * 4
     cost = pl.CostEstimate(
         flops=flops,
@@ -91,8 +92,8 @@
         in_specs=[pl.BlockSpec((BLOCK, width), lambda b, idx, cnt: (b, 0))] + [any_spec] * 3,
         out_specs=pl.BlockSpec((BLOCK, width), lambda b, idx, cnt: (b, 0)),
         scratch_shapes=[
-            pltpu.VMEM((3 * shard_rows, width), jnp.bfloat16),
-            pltpu.VMEM((3 * shard_rows, width), jnp.bfloat16),
+            pltpu.VMEM((3 * sources, tile, width), jnp.bfloat16),
+            pltpu.VMEM((3 * sources, tile, width), jnp.bfloat16),
             pltpu.VMEM((MAXB, BLOCK, BLOCK), jnp.float32),
             pltpu.VMEM((1, BLOCK), jnp.float32),
             pltpu.VMEM((1, BLOCK), jnp.float32),
@@ -101,7 +102,7 @@
         ],
     )
     return pl.pallas_call(
-        functools.partial(attention_kernel, shard_rows=shard_rows),
+        attention_kernel,
         out_shape=jax.ShapeDtypeStruct((rows, width), jnp.bfloat16),
         grid_spec=grid_spec,
         compiler_params=pltpu.CompilerParams(dimension_semantics=("arbitrary",)),
@@ -115,12 +116,9 @@
     def to_heads(x):
         return lax.all_to_all(x, "head", split_axis=1, concat_axis=0, tiled=True)
 
-    rows, model = keys.shape
-    heads = model // HD
-    paired = jnp.stack(
-        [keys.reshape(rows, heads, HD), values.reshape(rows, heads, HD)], axis=2
-    ).reshape(rows, 2 * model)
-    kv_rows = to_heads(paired)
+    rows = keys.shape[0]
+    kv_rows = to_heads(jnp.concatenate([keys, values], axis=0))
+    kv_rows = kv_rows.reshape(lax.axis_size("head"), 2, rows, HD)
     query_rows = to_heads(queries)
     kv_parts = (from_behind(kv_rows, "blk", 1), kv_rows, from_behind(kv_rows, "blk", -1))
     blocks_here = query_rows.shape[0] // BLOCK

time: 207 us -> 202 us (0.976)
  local copies, waits for them, and re-layouts: 10.4 us -> 3.73 us
    all_to_all x2 -> x1, local copies, waits for them, and re-layouts: 3.88 us -> 1.26 us  [to_heads(): return lax.all_to_all(x, 'head', split_axis=1, concat_axis=0, tiled=True)]
    all_to_all x0 -> x1, other arithmetic: none -> 2.2 us  [to_heads(): return lax.all_to_all(x, 'head', split_axis=1, concat_axis=0, tiled=True)]
    another operation x1 -> x0, local copies, waits for them, and re-layouts: 2.16 us -> none  [local(): jnp.stack([keys.reshape(rows, heads, HD), values.reshape(rows, heads, HD)...]
where the time goes in v6:
time: 202 us; the launch traced here: 200 us
  blocking collectives  95.4 us (47%)
  waiting for transfers between devices  52.9 us (26%)
  Pallas kernels  31 us (15%)
  starting transfers between devices  15 us (7%)
  local copies, waits for them, and re-layouts  3.73 us (2%)
  other arithmetic  2.28 us (1%)
    all_to_all x1, blocking collectives, to_heads(): return lax.all_to_all(x, 'head', split_axis=1, concat_axis=0, tiled=True)  63.3 us
    all_to_all x1, waiting for transfers between devices, to_heads(): return lax.all_to_all(x, 'head', split_axis=1, concat_axis=0, tiled=True)  52.9 us
    all_to_all x1, blocking collectives, local(): lax.all_to_all(attended_rows, 'head', split_axis=0, concat_axis=1, tiled=...  32.1 us
    pallas_call x1, Pallas kernels, attend(): pl.pallas_call(attention_kernel, out_shape=jax.ShapeDtypeStruct((rows, wi...  31 us
    ppermute x2, starting transfers between devices, from_behind(): return lax.ppermute(value, axis, pairs)  9.31 us
    all_to_all x1, starting transfers between devices, to_heads(): return lax.all_to_all(x, 'head', split_axis=1, concat_axis=0, tiled=True)  5.74 us
  transfers between devices with their start and end apart: 3, of which 1 were waited for; matrix products, arithmetic and copies ran while one was open for 1% of the time, Pallas kernels for 0%

profile of v6, /device:TPU:1, one launch (start us, length us, event | category | flops | bytes accessed | tf_op | source)
XLA Modules:
  0.0 200.4 jit_solution(15875584499262031576)
XLA Ops:
  0.0 0.0 copy-start
  0.0 2.2 %copy_bitcast_fusion = bf16[256,32,128]{2,0,1:T(8,128)(2,1)S(1)} fusion(bf16[128,4096]{1,0:T(8,128)(2,1)} %param.7, bf16[128,4096]{1,0:T(8,128)(2,1)} %param.6), kind=kLoop, calls=%fused_computation | loop fusion | flops 4194304 | bytes 4194304 | tf_op jit(solution)/shard_map/all_to_all | solution.py:117
  2.2 63.3 %all_to_all.54 = bf16[256,32,128]{2,0,1:T(8,128)(2,1)S(1)} all-to-all(bf16[256,32,128]{2,0,1:T(8,128)(2,1)S(1)} %copy_bitcast_fusion), channel_id=1, replica_groups=mesh['blk'=16,'head'=32] {'head'}, dimensions={1} | all-to-all | bytes 4194304 | tf_op jit(solution)/shard_map/all_to_all | solution.py:117
  65.5 0.0 copy-start.1
  65.5 0.0 copy-start.3
  65.5 0.0 copy-start.2
  65.5 7.4 %collective-permute-start.1 = (bf16[32,2,128,128]{3,2,1,0:T(8,128)(2,1)S(1)}, bf16[32,2,128,128]{3,2,1,0:T(8,128)(2,1)}, u32[]{:S(2)}, u32[]{:S(2)}) collective-permute-start(bf16[32,2,128,128]{3,2,1,0:T(8,128)(2,1)S(1)} %bitcast.23), channel_id=1, source_target_pairs={{0,480},{32,0},{64,32},{96,64},{128,96},{160,128},{192,160},{224,1... | collective-permute-start | bytes 6291464 | tf_op jit(solution)/shard_map/ppermute | solution.py:19
  72.9 1.9 collective-permute-start
  74.8 0.0 copy-done
  74.9 1.3 copy_bitcast_fusion.2
  76.1 0.0 copy-done.1
  76.1 5.7 %all-to-all-start = ((bf16[128,32,128]{2,0,1:T(8,128)(2,1)}), bf16[128,32,128]{2,0,1:T(8,128)(2,1)}, u32[]{:S(2)}, u32[]{:S(2)}) async-start(bf16[128,32,128]{2,0,1:T(8,128)(2,1)} %copy_bitcast_fusion.2), calls=%async_computation | async-start | bytes 2097152 | tf_op jit(solution)/shard_map/all_to_all | solution.py:117
  81.9 0.0 copy-done.3
  81.9 0.6 dynamic_slice.7.cnt_ref
  82.5 0.0 copy-done.2
  82.5 0.1 fusion.1
  82.5 0.1 copy.6
  82.6 0.7 reshape.16.idx_ref
  83.3 52.9 %all-to-all-done = bf16[128,32,128]{2,0,1:T(8,128)(2,1)} async-done(((bf16[128,32,128]{2,0,1:T(8,128)(2,1)}), bf16[128,32,128]{2,0,1:T(8,128)(2,1)}, u32[]{:S(2)}, u32[]{:S(2)}) %all-to-all-start) | async-done | bytes 1048608 | tf_op jit(solution)/shard_map/all_to_all | solution.py:117
  136.2 0.0 collective-permute-done.1.kv_next
  136.2 0.0 collective-permute-done.kv_prev
  136.2 31.0 %shard_map.55 = bf16[4096,128]{1,0:T(8,128)(2,1)} custom-call(s32[48]{0:T(128)} %reshape.16.idx_ref, s32[8]{0:T(128)} %dynamic_slice.7.cnt_ref, bf16[4096,128]{1,0:T(8,128)(2,1)} %bitcast.1.q_ref, bf16[32,2,128,128]{3,2,1,0:T(8,128)(2,1)} %collective-permute-done.kv_prev, bf16[32,2,128,128]{3,2,1,0:T(8,128)(2,1)} %bitcast.25, ...), custom_call_target="tpu_custom_call" | custom-call | flops 6442450944 | bytes 8388608 | tf_op jit(solution)/shard_map/pallas_call | solution.py:104
  167.2 32.1 %all_to_all.55 = bf16[32,128,128]{2,1,0:T(8,128)(2,1)S(1)} all-to-all(bf16[32,128,128]{2,1,0:T(8,128)(2,1)} %bitcast.26), channel_id=1, replica_groups=mesh['blk'=16,'head'=32] {'head'}, dimensions={0} | all-to-all | bytes 2097152 | tf_op jit(solution)/shard_map/all_to_all | solution.py:132
  199.3 1.1 copy_bitcast_fusion.1
Async XLA Ops:
  0.0 74.8 %copy-start = (bf16[128,4096]{1,0:T(8,128)(2,1)S(1)}, bf16[128,4096]{1,0:T(8,128)(2,1)}, u32[]{:S(2)}) copy-start(bf16[128,4096]{1,0:T(8,128)(2,1)} %param.5) | copy-start | bytes 3145732
  65.5 10.6 %copy-start.1 = (bf16[256,32,128]{2,0,1:T(8,128)(2,1)}, bf16[256,32,128]{2,0,1:T(8,128)(2,1)S(1)}, u32[]{:S(2)}) copy-start(bf16[256,32,128]{2,0,1:T(8,128)(2,1)S(1)} %all_to_all.54) | copy-start | bytes 6291460
  65.5 16.4 %copy-start.3 = (s32[128]{0:T(128)S(1)}, s32[128]{0:T(128)}, u32[]{:S(2)}) copy-start(s32[128]{0:T(128)} %param.9) | copy-start | bytes 1540
  65.5 16.9 %copy-start.2 = (s32[128,6]{0,1:T(8,128)S(1)}, s32[128,6]{0,1:T(8,128)}, u32[]{:S(2)}) copy-start(s32[128,6]{0,1:T(8,128)} %param.8) | copy-start | bytes 9220
  65.5 70.7 %collective-permute-start.1 = (bf16[32,2,128,128]{3,2,1,0:T(8,128)(2,1)S(1)}, bf16[32,2,128,128]{3,2,1,0:T(8,128)(2,1)}, u32[]{:S(2)}, u32[]{:S(2)}) collective-permute-start(bf16[32,2,128,128]{3,2,1,0:T(8,128)(2,1)S(1)} %bitcast.23), channel_id=1, source_target_pairs={{0,480},{32,0},{64,32},{96,64},{128,96},{160,128},{192,160},{224,1... | collective-permute-start | bytes 6291464 | tf_op jit(solution)/shard_map/ppermute | solution.py:19
  72.9 63.3 %collective-permute-start = (bf16[32,2,128,128]{3,2,1,0:T(8,128)(2,1)S(1)}, bf16[32,2,128,128]{3,2,1,0:T(8,128)(2,1)}, u32[]{:S(2)}, u32[]{:S(2)}) collective-permute-start(bf16[32,2,128,128]{3,2,1,0:T(8,128)(2,1)S(1)} %bitcast.24), channel_id=1, source_target_pairs={{0,32},{32,64},{64,96},{96,128},{128,160},{160,192},{192,224},{224... | collective-permute-start | bytes 6291464 | tf_op jit(solution)/shard_map/ppermute | solution.py:19
  76.1 60.1 %all-to-all-start = ((bf16[128,32,128]{2,0,1:T(8,128)(2,1)}), bf16[128,32,128]{2,0,1:T(8,128)(2,1)}, u32[]{:S(2)}, u32[]{:S(2)}) async-start(bf16[128,32,128]{2,0,1:T(8,128)(2,1)} %copy_bitcast_fusion.2), calls=%async_computation | async-start | bytes 2097152 | tf_op jit(solution)/shard_map/all_to_all | solution.py:117

commit v7 on v4

--- a/solution.py
+++ b/solution.py
@@ -18,27 +18,25 @@
     return lax.ppermute(value, axis, pairs)
 
 
-def attention_kernel(idx_ref, cnt_ref, q_ref, kv_prev, kv_own, kv_next, o_ref,
-                     k_scr, v_scr, s_scr, m_scr, l_scr, acc_scr, sem, *, shard_rows):
+def attention_kernel(idx_ref, cnt_ref, q_ref, *refs):
+    slabs, (o_ref, k_scr, v_scr, s_scr, m_scr, l_scr, acc_scr, sem) = refs[:6], refs[6:]
     b = pl.program_id(0)
     width = q_ref.shape[1]
+    blocks = k_scr.shape[0] // 3
 
     @pl.when(b == 0)
     def _load_context():
         copies = []
-        for i, (src, dst, part) in enumerate(
-            ((kv_own.at[:, pl.ds(0, width)], k_scr, 1),
-             (kv_own.at[:, pl.ds(width, width)], v_scr, 1),
-             (kv_prev.at[:, pl.ds(0, width)], k_scr, 0),
-             (kv_next.at[:, pl.ds(0, width)], k_scr, 2),
-             (kv_prev.at[:, pl.ds(width, width)], v_scr, 0),
-             (kv_next.at[:, pl.ds(width, width)], v_scr, 2))
-        ):
-            copy = pltpu.make_async_copy(
-                src, dst.at[pl.ds(part * shard_rows, shard_rows)], sem.at[i]
-            )
-            copy.start()
-            copies.append(copy)
+        for i, slab in enumerate(slabs):
+            part, half = (1, 0, 2)[i // 2], i % 2
+            for column, dst in ((0, k_scr), (width, v_scr)):
+                copy = pltpu.make_async_copy(
+                    slab.at[:, :, pl.ds(column, width)],
+                    dst.at[pl.ds(part * blocks, blocks), half],
+                    sem.at[2 * i + column // width],
+                )
+                copy.start()
+                copies.append(copy)
         for copy in copies:
             copy.wait()
 
@@ -48,8 +46,7 @@
     for j in range(MAXB):
         @pl.when(j < amount)
         def _scores():
-            start = pl.multiple_of(idx_ref[b * MAXB + j] * BLOCK, BLOCK)
-            key_block = k_scr[pl.ds(start, BLOCK), :]
+            key_block = k_scr[idx_ref[b * MAXB + j]].reshape(BLOCK, HD)
             scores = lax.dot_general(
                 key_block, q_ref[...], (((1,), (1,)), ((), ())),
                 preferred_element_type=jnp.float32,
@@ -62,8 +59,7 @@
     for j in range(MAXB):
         @pl.when(j < amount)
         def _mix():
-            start = pl.multiple_of(idx_ref[b * MAXB + j] * BLOCK, BLOCK)
-            value_block = v_scr[pl.ds(start, BLOCK), :]
+            value_block = v_scr[idx_ref[b * MAXB + j]].reshape(BLOCK, HD)
             expo = jnp.exp(s_scr[j] - m_scr[...])
             l_scr[...] += jnp.sum(expo, axis=0, keepdims=True)
             acc_scr[...] += lax.dot_general(
@@ -77,7 +73,7 @@
 def attend(query_rows, kv_parts, local_index, count_rows):
     rows, width = query_rows.shape
     blocks_here = rows // BLOCK
-    shard_rows = kv_parts[0].shape[0]
+    shard_rows = rows
     flops = blocks_here * MAXB * BLOCK * BLOCK * width * 4
     cost = pl.CostEstimate(
         flops=flops,
@@ -88,20 +84,20 @@
     grid_spec = pltpu.PrefetchScalarGridSpec(
         num_scalar_prefetch=2,
         grid=(blocks_here,),
-        in_specs=[pl.BlockSpec((BLOCK, width), lambda b, idx, cnt: (b, 0))] + [any_spec] * 3,
+        in_specs=[pl.BlockSpec((BLOCK, width), lambda b, idx, cnt: (b, 0))] + [any_spec] * 6,
         out_specs=pl.BlockSpec((BLOCK, width), lambda b, idx, cnt: (b, 0)),
         scratch_shapes=[
-            pltpu.VMEM((3 * shard_rows, width), jnp.bfloat16),
-            pltpu.VMEM((3 * shard_rows, width), jnp.bfloat16),
+            pltpu.VMEM((3 * blocks_here, 2, BLOCK // 2, width), jnp.bfloat16),
+            pltpu.VMEM((3 * blocks_here, 2, BLOCK // 2, width), jnp.bfloat16),
             pltpu.VMEM((MAXB, BLOCK, BLOCK), jnp.float32),
             pltpu.VMEM((1, BLOCK), jnp.float32),
             pltpu.VMEM((1, BLOCK), jnp.float32),
             pltpu.VMEM((width, BLOCK), jnp.float32),
-            pltpu.SemaphoreType.DMA((6,)),
+            pltpu.SemaphoreType.DMA((12,)),
         ],
     )
     return pl.pallas_call(
-        functools.partial(attention_kernel, shard_rows=shard_rows),
+        attention_kernel,
         out_shape=jax.ShapeDtypeStruct((rows, width), jnp.bfloat16),
         grid_spec=grid_spec,
         compiler_params=pltpu.CompilerParams(dimension_semantics=("arbitrary",)),
@@ -120,9 +116,19 @@
     paired = jnp.stack(
         [keys.reshape(rows, heads, HD), values.reshape(rows, heads, HD)], axis=2
     ).reshape(rows, 2 * model)
-    kv_rows = to_heads(paired)
+    half = rows // 2
+    kv_parts = []
+    tie = None
+    for piece in (paired[:half], paired[half:]):
+        kv_rows = to_heads(piece)
+        if tie is not None:
+            kv_rows = kv_rows + tie
+        earlier, later = from_behind(kv_rows, "blk", 1), from_behind(kv_rows, "blk", -1)
+        tie = ((earlier[0, 0] + later[0, 0]) * 0).astype(kv_rows.dtype)
+        kv_parts.append((kv_rows, earlier, later))
     query_rows = to_heads(queries)
-    kv_parts = (from_behind(kv_rows, "blk", 1), kv_rows, from_behind(kv_rows, "blk", -1))
+    slab_shape = (lax.axis_size("head") * half // (BLOCK // 2), BLOCK // 2, 2 * HD)
+    kv_parts = [kv_parts[h][p].reshape(slab_shape) for p in range(3) for h in range(2)]
     blocks_here = query_rows.shape[0] // BLOCK
     total_blocks = blocks_here * cycle_size
     first_block = lax.axis_index("blk") * blocks_here

time: 207 us -> 200 us (0.966)
  blocking collectives: 95.6 us -> 37.8 us
  waiting for transfers between devices: 52.9 us -> 78 us
  starting transfers between devices: 15.1 us -> 38.2 us
  Pallas kernels: 32.2 us -> 29.1 us
  local copies, waits for them, and re-layouts: 10.4 us -> 13.2 us
    all_to_all x1 -> x0, blocking collectives: 63.5 us -> none  [to_heads(): return lax.all_to_all(x, 'head', split_axis=1, concat_axis=0, tiled=True)]
    ppermute x2 -> x4, waiting for transfers between devices: 0.01 us -> 24.4 us  [from_behind(): return lax.ppermute(value, axis, pairs)]
    all_to_all x1 -> x3, starting transfers between devices: 5.76 us -> 23.7 us  [to_heads(): return lax.all_to_all(x, 'head', split_axis=1, concat_axis=0, tiled=True)]
    all_to_all x1, blocking collectives: 32.1 us -> 37.8 us  [local(): lax.all_to_all(attended_rows, 'head', split_axis=0, concat_axis=1, tiled=...]
    ppermute x2 -> x4, starting transfers between devices: 9.31 us -> 14.5 us  [from_behind(): return lax.ppermute(value, axis, pairs)]
    slice x0 -> x5, local copies, waits for them, and re-layouts: none -> 4.41 us  [the longest x2 1.85 us: local(): tie = ((earlier[0, 0] + later[0, 0]) * 0).astype(kv_rows.dtype)]
    pallas_call x1, Pallas kernels: 32.2 us -> 29.1 us  [attend(): pl.pallas_call(attention_kernel, out_shape=jax.ShapeDtypeStruct((rows, wi...]
    all_to_all x1 -> x3, waiting for transfers between devices: 52.9 us -> 53.6 us  [to_heads(): return lax.all_to_all(x, 'head', split_axis=1, concat_axis=0, tiled=True)]
  transfers between devices with their start and end apart: 3 -> 7, of which waited for: 1 -> 7; matrix products, arithmetic and copies ran while one was open for 1% -> 3% of each run, Pallas kernels for 0% -> 0%
where the time goes in v7:
time: 200 us; the launch traced here: 198 us
  waiting for transfers between devices  78 us (39%)
  starting transfers between devices  38.2 us (19%)
  blocking collectives  37.8 us (19%)
  Pallas kernels  29.1 us (15%)
  local copies, waits for them, and re-layouts  13.2 us (7%)
    all_to_all x3, waiting for transfers between devices, to_heads(): return lax.all_to_all(x, 'head', split_axis=1, concat_axis=0, tiled=True)  53.6 us
    all_to_all x1, blocking collectives, local(): lax.all_to_all(attended_rows, 'head', split_axis=0, concat_axis=1, tiled=...  37.8 us
    pallas_call x1, Pallas kernels, attend(): pl.pallas_call(attention_kernel, out_shape=jax.ShapeDtypeStruct((rows, wi...  29.1 us
    ppermute x4, waiting for transfers between devices, from_behind(): return lax.ppermute(value, axis, pairs)  24.4 us
    all_to_all x3, starting transfers between devices, to_heads(): return lax.all_to_all(x, 'head', split_axis=1, concat_axis=0, tiled=True)  23.7 us
    ppermute x4, starting transfers between devices, from_behind(): return lax.ppermute(value, axis, pairs)  14.5 us
    all_to_all x3, local copies, waits for them, and re-layouts, to_heads(): return lax.all_to_all(x, 'head', split_axis=1, concat_axis=0, tiled=True)  4.26 us
  transfers between devices with their start and end apart: 7, of which 7 were waited for; matrix products, arithmetic and copies ran while one was open for 3% of the time, Pallas kernels for 0%

profile of v7, /device:TPU:1, one launch (start us, length us, event | category | flops | bytes accessed | tf_op | source)
XLA Modules:
  0.0 197.9 jit_solution(1363278832907124131)
XLA Ops:
  0.0 1.6 copy.13
  2.5 1.1 copy.8
  3.6 1.5 all_to_all.56
  5.1 13.0 %all-to-all-start.1 = ((bf16[64,32,256]{2,0,1:T(8,128)(2,1)}), bf16[64,32,256]{2,0,1:T(8,128)(2,1)}, u32[]{:S(2)}, u32[]{:S(2)}) async-start(bf16[64,32,256]{2,0,1:T(8,128)(2,1)} %all_to_all.56), calls=%async_computation.1 | async-start | bytes 2097152 | tf_op jit(solution)/shard_map/all_to_all | solution.py:112
  18.0 1.1 copy.9
  19.1 1.5 all_to_all.59
  20.6 25.6 %all-to-all-done.1 = bf16[64,32,256]{2,0,1:T(8,128)(2,1)} async-done(((bf16[64,32,256]{2,0,1:T(8,128)(2,1)}), bf16[64,32,256]{2,0,1:T(8,128)(2,1)}, u32[]{:S(2)}, u32[]{:S(2)}) %all-to-all-start.1) | async-done | bytes 1048608 | tf_op jit(solution)/shard_map/all_to_all | solution.py:112
  46.2 4.8 %all-to-all-start.2 = ((bf16[64,32,256]{2,0,1:T(8,128)(2,1)}), bf16[64,32,256]{2,0,1:T(8,128)(2,1)S(1)}, u32[]{:S(2)}, u32[]{:S(2)}) async-start(bf16[64,32,256]{2,0,1:T(8,128)(2,1)} %all_to_all.59), calls=%async_computation.2 | async-start | bytes 2097152 | tf_op jit(solution)/shard_map/all_to_all | solution.py:112
  51.0 7.3 %collective-permute-start.1 = (bf16[2048,256]{1,0:T(8,128)(2,1)}, bf16[2048,256]{1,0:T(8,128)(2,1)S(1)}, u32[]{:S(2)}, u32[]{:S(2)}) collective-permute-start(bf16[2048,256]{1,0:T(8,128)(2,1)} %bitcast.4), channel_id=1, source_target_pairs={{0,480},{32,0},{64,32},{96,64},{128,96},{160,128},{192,160},{224,1... | collective-permute-start | bytes 3145736 | tf_op jit(solution)/shard_map/ppermute | solution.py:18
  58.3 1.9 collective-permute-start
  60.2 1.3 copy_bitcast_fusion.1
  61.5 17.8 %all-to-all-done.2 = bf16[64,32,256]{2,0,1:T(8,128)(2,1)S(1)} async-done(((bf16[64,32,256]{2,0,1:T(8,128)(2,1)}), bf16[64,32,256]{2,0,1:T(8,128)(2,1)S(1)}, u32[]{:S(2)}, u32[]{:S(2)}) %all-to-all-start.2) | async-done | bytes 1048608 | tf_op jit(solution)/shard_map/all_to_all | solution.py:112
  79.3 6.0 %all-to-all-start = ((bf16[128,32,128]{2,0,1:T(8,128)(2,1)}), bf16[128,32,128]{2,0,1:T(8,128)(2,1)}, u32[]{:S(2)}, u32[]{:S(2)}) async-start(bf16[128,32,128]{2,0,1:T(8,128)(2,1)} %copy_bitcast_fusion.1), calls=%async_computation | async-start | bytes 2097152 | tf_op jit(solution)/shard_map/all_to_all | solution.py:112
  85.3 2.9 %collective-permute-done.1 = bf16[2048,256]{1,0:T(8,128)(2,1)S(1)} collective-permute-done((bf16[2048,256]{1,0:T(8,128)(2,1)}, bf16[2048,256]{1,0:T(8,128)(2,1)S(1)}, u32[]{:S(2)}, u32[]{:S(2)}) %collective-permute-start.1) | collective-permute-done | bytes 1048608 | tf_op jit(solution)/shard_map/ppermute | solution.py:18
  88.8 5.1 %collective-permute-done = bf16[2048,256]{1,0:T(8,128)(2,1)} collective-permute-done((bf16[2048,256]{1,0:T(8,128)(2,1)}, bf16[2048,256]{1,0:T(8,128)(2,1)}, u32[]{:S(2)}, u32[]{:S(2)}) %collective-permute-start) | collective-permute-done | bytes 1048608 | tf_op jit(solution)/shard_map/ppermute | solution.py:18
  93.9 1.3 slice.20
  96.6 2.6 %collective-permute-start.3 = (bf16[2048,256]{1,0:T(8,128)(2,1)S(1)}, bf16[2048,256]{1,0:T(8,128)(2,1)}, u32[]{:S(2)}, u32[]{:S(2)}) collective-permute-start(bf16[2048,256]{1,0:T(8,128)(2,1)S(1)} %bitcast.44), channel_id=1, source_target_pairs={{0,480},{32,0},{64,32},{96,64},{128,96},{160,128},{192,160},{224,1... | collective-permute-start | bytes 3145736 | tf_op jit(solution)/shard_map/ppermute | solution.py:18
  99.2 2.7 %collective-permute-start.2 = (bf16[2048,256]{1,0:T(8,128)(2,1)S(1)}, bf16[2048,256]{1,0:T(8,128)(2,1)}, u32[]{:S(2)}, u32[]{:S(2)}) collective-permute-start(bf16[2048,256]{1,0:T(8,128)(2,1)S(1)} %bitcast.45), channel_id=1, source_target_pairs={{0,32},{32,64},{64,96},{96,128},{128,160},{160,192},{192,224},{224... | collective-permute-start | bytes 3145736 | tf_op jit(solution)/shard_map/ppermute | solution.py:18
  103.3 10.2 %all-to-all-done = bf16[128,32,128]{2,0,1:T(8,128)(2,1)} async-done(((bf16[128,32,128]{2,0,1:T(8,128)(2,1)}), bf16[128,32,128]{2,0,1:T(8,128)(2,1)}, u32[]{:S(2)}, u32[]{:S(2)}) %all-to-all-start) | async-done | bytes 1048608 | tf_op jit(solution)/shard_map/all_to_all | solution.py:112
  113.5 11.0 %collective-permute-done.3 = bf16[2048,256]{1,0:T(8,128)(2,1)} collective-permute-done((bf16[2048,256]{1,0:T(8,128)(2,1)S(1)}, bf16[2048,256]{1,0:T(8,128)(2,1)}, u32[]{:S(2)}, u32[]{:S(2)}) %collective-permute-start.3) | collective-permute-done | bytes 1048608 | tf_op jit(solution)/shard_map/ppermute | solution.py:18
  124.5 5.4 %collective-permute-done.2 = bf16[2048,256]{1,0:T(8,128)(2,1)} collective-permute-done((bf16[2048,256]{1,0:T(8,128)(2,1)S(1)}, bf16[2048,256]{1,0:T(8,128)(2,1)}, u32[]{:S(2)}, u32[]{:S(2)}) %collective-permute-start.2) | collective-permute-done | bytes 1048608 | tf_op jit(solution)/shard_map/ppermute | solution.py:18
  129.9 29.1 %shard_map.55 = bf16[4096,128]{1,0:T(8,128)(2,1)} custom-call(s32[48]{0:T(128)} %reshape.45.idx_ref, s32[8]{0:T(128)} %dynamic_slice.7.cnt_ref, bf16[4096,128]{1,0:T(8,128)(2,1)} %bitcast.1.q_ref, bf16[8,256,256]{2,1,0:T(8,128)(2,1)} %bitcast.3.refs_0_, bf16[8,256,256]{2,1,0:T(8,128)(2,1)} %bitcast.46, bf16[8,256,256]{2,1,0:T(8,128)(2,1)} %bitcast.9.refs_2_, ...), custom_call_target="tpu_custom_call" | custom-call | flops 6442450944 | bytes 8388608 | tf_op jit(solution)/shard_map/pallas_call | solution.py:99
  159.0 37.8 %all_to_all.70 = bf16[32,128,128]{2,1,0:T(8,128)(2,1)S(1)} all-to-all(bf16[32,128,128]{2,1,0:T(8,128)(2,1)} %bitcast.49), channel_id=1, replica_groups=mesh['blk'=16,'head'=32] {'head'}, dimensions={0} | all-to-all | bytes 2097152 | tf_op jit(solution)/shard_map/all_to_all | solution.py:140
  196.8 1.1 copy_bitcast_fusion
  (22 shorter events, 3.0 us)
Async XLA Ops:
  0.0 60.2 %copy-start = (bf16[128,4096]{1,0:T(8,128)(2,1)S(1)}, bf16[128,4096]{1,0:T(8,128)(2,1)}, u32[]{:S(2)}) copy-start(bf16[128,4096]{1,0:T(8,128)(2,1)} %param.5) | copy-start | bytes 3145732
  0.0 1.7 copy-start.2
  5.1 41.1 %all-to-all-start.1 = ((bf16[64,32,256]{2,0,1:T(8,128)(2,1)}), bf16[64,32,256]{2,0,1:T(8,128)(2,1)}, u32[]{:S(2)}, u32[]{:S(2)}) async-start(bf16[64,32,256]{2,0,1:T(8,128)(2,1)} %all_to_all.56), calls=%async_computation.1 | async-start | bytes 2097152 | tf_op jit(solution)/shard_map/all_to_all | solution.py:112
  46.2 33.1 %all-to-all-start.2 = ((bf16[64,32,256]{2,0,1:T(8,128)(2,1)}), bf16[64,32,256]{2,0,1:T(8,128)(2,1)S(1)}, u32[]{:S(2)}, u32[]{:S(2)}) async-start(bf16[64,32,256]{2,0,1:T(8,128)(2,1)} %all_to_all.59), calls=%async_computation.2 | async-start | bytes 2097152 | tf_op jit(solution)/shard_map/all_to_all | solution.py:112
  51.0 37.2 %collective-permute-start.1 = (bf16[2048,256]{1,0:T(8,128)(2,1)}, bf16[2048,256]{1,0:T(8,128)(2,1)S(1)}, u32[]{:S(2)}, u32[]{:S(2)}) collective-permute-start(bf16[2048,256]{1,0:T(8,128)(2,1)} %bitcast.4), channel_id=1, source_target_pairs={{0,480},{32,0},{64,32},{96,64},{128,96},{160,128},{192,160},{224,1... | collective-permute-start | bytes 3145736 | tf_op jit(solution)/shard_map/ppermute | solution.py:18
  58.3 35.6 %collective-permute-start = (bf16[2048,256]{1,0:T(8,128)(2,1)}, bf16[2048,256]{1,0:T(8,128)(2,1)}, u32[]{:S(2)}, u32[]{:S(2)}) collective-permute-start(bf16[2048,256]{1,0:T(8,128)(2,1)} %bitcast.4), channel_id=1, source_target_pairs={{0,32},{32,64},{64,96},{96,128},{128,160},{160,192},{192,224},{224... | collective-permute-start | bytes 3145736 | tf_op jit(solution)/shard_map/ppermute | solution.py:18
  61.5 40.4 %copy-start.5 = (s32[128]{0:T(128)S(1)}, s32[128]{0:T(128)}, u32[]{:S(2)}) copy-start(s32[128]{0:T(128)} %param.9) | copy-start | bytes 1540
  61.5 41.0 %copy-start.3 = (s32[128,6]{0,1:T(8,128)S(1)}, s32[128,6]{0,1:T(8,128)}, u32[]{:S(2)}) copy-start(s32[128,6]{0,1:T(8,128)} %param.8) | copy-start | bytes 9220
  79.3 34.2 %all-to-all-start = ((bf16[128,32,128]{2,0,1:T(8,128)(2,1)}), bf16[128,32,128]{2,0,1:T(8,128)(2,1)}, u32[]{:S(2)}, u32[]{:S(2)}) async-start(bf16[128,32,128]{2,0,1:T(8,128)(2,1)} %copy_bitcast_fusion.1), calls=%async_computation | async-start | bytes 2097152 | tf_op jit(solution)/shard_map/all_to_all | solution.py:112
  88.2 8.3 %copy-start.4 = (bf16[2048,256]{1,0:T(8,128)(2,1)}, bf16[2048,256]{1,0:T(8,128)(2,1)S(1)}, u32[]{:S(2)}) copy-start(bf16[2048,256]{1,0:T(8,128)(2,1)S(1)} %collective-permute-done.1) | copy-start | bytes 3145732
  96.6 33.3 %copy-start.1 = (bf16[64,32,256]{2,0,1:T(8,128)(2,1)}, bf16[64,32,256]{2,0,1:T(8,128)(2,1)S(1)}, u32[]{:S(2)}) copy-start(bf16[64,32,256]{2,0,1:T(8,128)(2,1)S(1)} %broadcast_add_fusion) | copy-start | bytes 3145732
  96.6 27.9 %collective-permute-start.3 = (bf16[2048,256]{1,0:T(8,128)(2,1)S(1)}, bf16[2048,256]{1,0:T(8,128)(2,1)}, u32[]{:S(2)}, u32[]{:S(2)}) collective-permute-start(bf16[2048,256]{1,0:T(8,128)(2,1)S(1)} %bitcast.44), channel_id=1, source_target_pairs={{0,480},{32,0},{64,32},{96,64},{128,96},{160,128},{192,160},{224,1... | collective-permute-start | bytes 3145736 | tf_op jit(solution)/shard_map/ppermute | solution.py:18
  99.2 30.7 %collective-permute-start.2 = (bf16[2048,256]{1,0:T(8,128)(2,1)S(1)}, bf16[2048,256]{1,0:T(8,128)(2,1)}, u32[]{:S(2)}, u32[]{:S(2)}) collective-permute-start(bf16[2048,256]{1,0:T(8,128)(2,1)S(1)} %bitcast.45), channel_id=1, source_target_pairs={{0,32},{32,64},{64,96},{96,128},{128,160},{160,192},{192,224},{224... | collective-permute-start | bytes 3145736 | tf_op jit(solution)/shard_map/ppermute | solution.py:18

commit v8 on v5

v8 whole, which is shorter than its diff:
```python
import functools

import jax
import jax.numpy as jnp
from jax import lax
from jax.experimental import pallas as pl
from jax.experimental.pallas import tpu as pltpu
from jax.sharding import PartitionSpec as P

HD = 128
BLOCK = 512
MAXB = 6


def from_behind(value, axis, steps):
    count = lax.axis_size(axis)
    pairs = [(source, (source + steps) % count) for source in range(count)]
    return lax.ppermute(value, axis, pairs)


def load_slabs(slabs, k_scr, v_scr, sem, width, blocks):
    copies = []
    for i, slab in enumerate(slabs):
        part, half = i // 2, i % 2
        for column, dst in ((0, k_scr), (width, v_scr)):
            copy = pltpu.make_async_copy(
                slab.at[:, :, pl.ds(column, width)],
                dst.at[pl.ds(part * blocks, blocks), half],
                sem.at[2 * i + column // width],
            )
            copy.start()
            copies.append(copy)
    for copy in copies:
        copy.wait()


def own_kernel(idx_ref, cnt_ref, q_ref, own0, own1, m_ref, l_ref, acc_ref,
               k_scr, v_scr, s_scr, sem, *, blocks):
    b = pl.program_id(0)
    width = q_ref.shape[1]

    @pl.when(b == 0)
    def _load_context():
        load_slabs((own0, own1), k_scr, v_scr, sem, width, blocks)

    scale = HD ** (-0.5)
    amount = cnt_ref[b]

    def usable(j):
        g = idx_ref[b * MAXB + j]
        return (j < amount) & (g >= blocks) & (g < 2 * blocks)

    def row(j):
        return idx_ref[b * MAXB + j] - blocks

    m_ref[...] = jnp.full(m_ref.shape, -jnp.inf, jnp.float32)
    for j in range(MAXB):
        @pl.when(usable(j))
        def _scores():
            scores = lax.dot_general(
                k_scr[row(j)].reshape(BLOCK, HD), q_ref[...], (((1,), (1,)), ((), ())),
                preferred_element_type=jnp.float32,
            ) * scale
            s_scr[j] = scores
            m_ref[...] = jnp.maximum(m_ref[...], jnp.max(scores, axis=0, keepdims=True))

    l_ref[...] = jnp.zeros(l_ref.shape, jnp.float32)
    acc_ref[...] = jnp.zeros(acc_ref.shape, jnp.float32)
    for j in range(MAXB):
        @pl.when(usable(j))
        def _mix():
            expo = jnp.exp(s_scr[j] - m_ref[...])
            l_ref[...] += jnp.sum(expo, axis=0, keepdims=True)
            acc_ref[...] += lax.dot_general(
                v_scr[row(j)].reshape(BLOCK, HD), expo.astype(jnp.bfloat16),
                (((0,), (0,)), ((), ())), preferred_element_type=jnp.float32,
            )


def rest_kernel(idx_ref, cnt_ref, q_ref, m_in, l_in, acc_in, prev0, prev1, next0, next1,
                o_ref, k_scr, v_scr, s_scr, m_scr, l_scr, acc_scr, sem, *, blocks):
    b = pl.program_id(0)
    width = q_ref.shape[1]

    @pl.when(b == 0)
    def _load_context():
        load_slabs((prev0, prev1, next0, next1), k_scr, v_scr, sem, width, blocks)

    scale = HD ** (-0.5)
    amount = cnt_ref[b]

    def usable(j):
        g = idx_ref[b * MAXB + j]
        return (j < amount) & ((g < blocks) | (g >= 2 * blocks))

    def row(j):
        g = idx_ref[b * MAXB + j]
        return jnp.where(g < blocks, g, g - blocks)

    m_scr[...] = m_in[...]
    for j in range(MAXB):
        @pl.when(usable(j))
        def _scores():
            scores = lax.dot_general(
                k_scr[row(j)].reshape(BLOCK, HD), q_ref[...], (((1,), (1,)), ((), ())),
                preferred_element_type=jnp.float32,
            ) * scale
            s_scr[j] = scores
            m_scr[...] = jnp.maximum(m_scr[...], jnp.max(scores, axis=0, keepdims=True))

    alpha = jnp.exp(m_in[...] - m_scr[...])
    l_scr[...] = alpha * l_in[...]
    acc_scr[...] = alpha * acc_in[...]
    for j in range(MAXB):
        @pl.when(usable(j))
        def _mix():
            expo = jnp.exp(s_scr[j] - m_scr[...])
            l_scr[...] += jnp.sum(expo, axis=0, keepdims=True)
            acc_scr[...] += lax.dot_general(
                v_scr[row(j)].reshape(BLOCK, HD), expo.astype(jnp.bfloat16),
                (((0,), (0,)), ((), ())), preferred_element_type=jnp.float32,
            )

    o_ref[...] = jnp.transpose(acc_scr[...] / l_scr[...]).astype(o_ref.dtype)


def attend_own(query_rows, own_slabs, local_index, count_rows):
    rows, width = query_rows.shape
    blocks = rows // BLOCK
    cost = pl.CostEstimate(
        flops=blocks * 4 * BLOCK * BLOCK * width * 4,
        transcendentals=blocks * 4 * BLOCK * BLOCK,
        bytes_accessed=rows * width * 2 * 3 + blocks * (width + 2) * BLOCK * 4,
    )
    q_spec = pl.BlockSpec((BLOCK, width), lambda b, idx, cnt: (b, 0))
    row_spec = pl.BlockSpec((None, 1, BLOCK), lambda b, idx, cnt: (b, 0, 0))
    acc_spec = pl.BlockSpec((None, width, BLOCK), lambda b, idx, cnt: (b, 0, 0))
    grid_spec = pltpu.PrefetchScalarGridSpec(
        num_scalar_prefetch=2,
        grid=(blocks,),
        in_specs=[q_spec] + [pl.BlockSpec(memory_space=pl.ANY)] * 2,
        out_specs=[row_spec, row_spec, acc_spec],
        scratch_shapes=[
            pltpu.VMEM((blocks, 2, BLOCK // 2, width), jnp.bfloat16),
            pltpu.VMEM((blocks, 2, BLOCK // 2, width), jnp.bfloat16),
            pltpu.VMEM((MAXB, BLOCK, BLOCK), jnp.float32),
            pltpu.SemaphoreType.DMA((4,)),
        ],
    )
    return pl.pallas_call(
        functools.partial(own_kernel, blocks=blocks),
        out_shape=[
            jax.ShapeDtypeStruct((blocks, 1, BLOCK), jnp.float32),
            jax.ShapeDtypeStruct((blocks, 1, BLOCK), jnp.float32),
            jax.ShapeDtypeStruct((blocks, width, BLOCK), jnp.float32),
        ],
        grid_spec=grid_spec,
        compiler_params=pltpu.CompilerParams(dimension_semantics=("arbitrary",)),
        cost_estimate=cost,
    )(local_index, count_rows, query_rows, *own_slabs)


def attend_rest(query_rows, partial, side_slabs, local_index, count_rows):
    rows, width = query_rows.shape
    blocks = rows // BLOCK
    cost = pl.CostEstimate(
        flops=blocks * 2 * BLOCK * BLOCK * width * 4,
        transcendentals=blocks * 2 * BLOCK * BLOCK,
        bytes_accessed=rows * width * 2 * 6 + blocks * (width + 2) * BLOCK * 4,
    )
    q_spec = pl.BlockSpec((BLOCK, width), lambda b, idx, cnt: (b, 0))
    row_spec = pl.BlockSpec((None, 1, BLOCK), lambda b, idx, cnt: (b, 0, 0))
    acc_spec = pl.BlockSpec((None, width, BLOCK), lambda b, idx, cnt: (b, 0, 0))
    any_spec = pl.BlockSpec(memory_space=pl.ANY)
    grid_spec = pltpu.PrefetchScalarGridSpec(
        num_scalar_prefetch=2,
        grid=(blocks,),
        in_specs=[q_spec, row_spec, row_spec, acc_spec] + [any_spec] * 4,
        out_specs=q_spec,
        scratch_shapes=[
            pltpu.VMEM((2 * blocks, 2, BLOCK // 2, width), jnp.bfloat16),
            pltpu.VMEM((2 * blocks, 2, BLOCK // 2, width), jnp.bfloat16),
            pltpu.VMEM((MAXB, BLOCK, BLOCK), jnp.float32),
            pltpu.VMEM((1, BLOCK), jnp.float32),
            pltpu.VMEM((1, BLOCK), jnp.float32),
            pltpu.VMEM((width, BLOCK), jnp.float32),
            pltpu.SemaphoreType.DMA((8,)),
        ],
    )
    return pl.pallas_call(
        functools.partial(rest_kernel, blocks=blocks),
        out_shape=jax.ShapeDtypeStruct((rows, width), jnp.bfloat16),
        grid_spec=grid_spec,
        compiler_params=pltpu.CompilerParams(dimension_semantics=("arbitrary",)),
        cost_estimate=cost,
    )(local_index, count_rows, query_rows, *partial, *side_slabs)


def local(queries, keys, values, key_blocks, counts):
    cycle_size = lax.axis_size("blk")

    def to_heads(x):
        return lax.all_to_all(x, "head", split_axis=1, concat_axis=0, tiled=True)

    rows, model = keys.shape
    heads = model // HD
    paired = jnp.stack(
        [keys.reshape(rows, heads, HD), values.reshape(rows, heads, HD)], axis=2
    ).reshape(rows, 2 * model)
    half = rows // 2
    kv_parts = []
    tie = None
    for piece in (paired[:half], paired[half:]):
        kv_rows = to_heads(piece)
        if tie is not None:
            kv_rows = kv_rows + tie
        earlier, later = from_behind(kv_rows, "blk", 1), from_behind(kv_rows, "blk", -1)
        tie = ((earlier[0, 0] + later[0, 0]) * 0).astype(kv_rows.dtype)
        kv_parts.append((kv_rows, earlier, later))
    query_rows = to_heads(queries)
    slab_shape = (lax.axis_size("head") * half // (BLOCK // 2), BLOCK // 2, 2 * HD)
    kv_parts = [kv_parts[h][p].reshape(slab_shape) for p in range(3) for h in range(2)]
    own_slabs, side_slabs = kv_parts[:2], kv_parts[2:]
    blocks_here = query_rows.shape[0] // BLOCK
    total_blocks = blocks_here * cycle_size
    first_block = lax.axis_index("blk") * blocks_here
    listed_rows = lax.dynamic_slice_in_dim(key_blocks, first_block, blocks_here, 0)
    count_rows = lax.dynamic_slice_in_dim(counts, first_block, blocks_here, 0)
    local_index = jnp.mod(listed_rows - first_block + blocks_here, total_blocks)
    local_index = jnp.clip(local_index, 0, 3 * blocks_here - 1).reshape(-1)
    partial = attend_own(query_rows, own_slabs, local_index, count_rows)
    attended_rows = attend_rest(query_rows, partial, side_slabs, local_index, count_rows)
    return lax.all_to_all(attended_rows, "head", split_axis=0, concat_axis=1, tiled=True)


def solution(mesh):
    placed = (
        P(("blk", "head"), None),
        P(("blk", "head"), None),
        P(("blk", "head"), None),
        P(),
        P(),
    )
    return jax.shard_map(
        local, mesh=mesh, in_specs=placed, out_specs=P(("blk", "head"), None), check_vma=False
    )
```

time: 218 us -> 216 us (level)
  blocking collectives: 90.8 us -> 35.9 us
  waiting for transfers between devices: 54.4 us -> 82.7 us
  starting transfers between devices: 22.1 us -> 40.8 us
  local copies, waits for them, and re-layouts: 12 us -> 16.3 us
    all_to_all x1 -> x0, blocking collectives: 56.4 us -> none  [to_heads(): return lax.all_to_all(x, 'head', split_axis=1, concat_axis=0, tiled=True)]
    all_to_all x1 -> x3, waiting for transfers between devices: 26.7 us -> 52.5 us  [to_heads(): return lax.all_to_all(x, 'head', split_axis=1, concat_axis=0, tiled=True)]
    all_to_all x1 -> x3, starting transfers between devices: 12.9 us -> 22.7 us  [to_heads(): return lax.all_to_all(x, 'head', split_axis=1, concat_axis=0, tiled=True)]
    ppermute x2 -> x4, starting transfers between devices: 9.17 us -> 18.1 us  [from_behind(): return lax.ppermute(value, axis, pairs)]
    slice x1 -> x5, local copies, waits for them, and re-layouts: 0.59 us -> 3.66 us  [the longest x2 1.48 us: local(): paired[half:]]
    unnamed x12 -> x19, local copies, waits for them, and re-layouts: 2.93 us -> 5.81 us
    ppermute x2 -> x4, waiting for transfers between devices: 27.7 us -> 30.2 us  [from_behind(): return lax.ppermute(value, axis, pairs)]
  transfers between devices with their start and end apart: 3 -> 7, of which waited for: 3 -> 3; matrix products, arithmetic and copies ran while one was open for 1% -> 3% of each run, Pallas kernels for 9% -> 10%
where the time goes in v8:
time: 216 us; the launch traced here: 215 us
  waiting for transfers between devices  82.7 us (38%)
  starting transfers between devices  40.8 us (19%)
  Pallas kernels  36.6 us (17%)
  blocking collectives  35.9 us (17%)
  local copies, waits for them, and re-layouts  16.3 us (8%)
    all_to_all x3, waiting for transfers between devices, to_heads(): return lax.all_to_all(x, 'head', split_axis=1, concat_axis=0, tiled=True)  52.5 us
    all_to_all x1, blocking collectives, local(): lax.all_to_all(attended_rows, 'head', split_axis=0, concat_axis=1, tiled=...  35.9 us
    ppermute x4, waiting for transfers between devices, from_behind(): return lax.ppermute(value, axis, pairs)  30.2 us
    all_to_all x3, starting transfers between devices, to_heads(): return lax.all_to_all(x, 'head', split_axis=1, concat_axis=0, tiled=True)  22.7 us
    pallas_call x1, Pallas kernels, attend_own(): pl.pallas_call(functools.partial(own_kernel, blocks=blocks), out_shape=[j...  22.2 us
    ppermute x4, starting transfers between devices, from_behind(): return lax.ppermute(value, axis, pairs)  18.1 us
    pallas_call x1, Pallas kernels, attend_rest(): pl.pallas_call(functools.partial(rest_kernel, blocks=blocks), out_shape=j...  14.3 us
    unnamed x19, local copies, waits for them, and re-layouts  5.81 us
  transfers between devices with their start and end apart: 7, of which 3 were waited for; matrix products, arithmetic and copies ran while one was open for 3% of the time, Pallas kernels for 10%

profile of v8, /device:TPU:1, one launch (start us, length us, event | category | flops | bytes accessed | tf_op | source)
XLA Modules:
  0.0 214.9 jit_solution(14605033772512432542)
XLA Ops:
  0.0 1.6 copy.13
  2.5 1.1 copy.8
  3.6 1.5 all_to_all.56
  5.1 13.0 %all-to-all-start.1 = ((bf16[64,32,256]{2,0,1:T(8,128)(2,1)}), bf16[64,32,256]{2,0,1:T(8,128)(2,1)}, u32[]{:S(2)}, u32[]{:S(2)}) async-start(bf16[64,32,256]{2,0,1:T(8,128)(2,1)} %all_to_all.56), calls=%async_computation.1 | async-start | bytes 2097152 | tf_op jit(solution)/shard_map/all_to_all | solution.py:203
  18.0 1.1 copy.9
  19.1 1.5 all_to_all.59
  20.6 25.6 %all-to-all-done.1 = bf16[64,32,256]{2,0,1:T(8,128)(2,1)} async-done(((bf16[64,32,256]{2,0,1:T(8,128)(2,1)}), bf16[64,32,256]{2,0,1:T(8,128)(2,1)}, u32[]{:S(2)}, u32[]{:S(2)}) %all-to-all-start.1) | async-done | bytes 1048608 | tf_op jit(solution)/shard_map/all_to_all | solution.py:203
  46.2 4.8 %all-to-all-start.2 = ((bf16[64,32,256]{2,0,1:T(8,128)(2,1)}), bf16[64,32,256]{2,0,1:T(8,128)(2,1)S(1)}, u32[]{:S(2)}, u32[]{:S(2)}) async-start(bf16[64,32,256]{2,0,1:T(8,128)(2,1)} %all_to_all.59), calls=%async_computation.2 | async-start | bytes 2097152 | tf_op jit(solution)/shard_map/all_to_all | solution.py:203
  51.0 1.3 copy_bitcast_fusion.1
  52.3 26.9 %all-to-all-done.2 = bf16[64,32,256]{2,0,1:T(8,128)(2,1)S(1)} async-done(((bf16[64,32,256]{2,0,1:T(8,128)(2,1)}), bf16[64,32,256]{2,0,1:T(8,128)(2,1)S(1)}, u32[]{:S(2)}, u32[]{:S(2)}) %all-to-all-start.2) | async-done | bytes 1048608 | tf_op jit(solution)/shard_map/all_to_all | solution.py:203
  79.2 5.0 %all-to-all-start = ((bf16[128,32,128]{2,0,1:T(8,128)(2,1)}), bf16[128,32,128]{2,0,1:T(8,128)(2,1)S(1)}, u32[]{:S(2)}, u32[]{:S(2)}) async-start(bf16[128,32,128]{2,0,1:T(8,128)(2,1)} %copy_bitcast_fusion.1), calls=%async_computation | async-start | bytes 2097152 | tf_op jit(solution)/shard_map/all_to_all | solution.py:203
  84.2 3.2 %collective-permute-start = (bf16[2048,256]{1,0:T(8,128)(2,1)}, bf16[2048,256]{1,0:T(8,128)(2,1)S(1)}, u32[]{:S(2)}, u32[]{:S(2)}) collective-permute-start(bf16[2048,256]{1,0:T(8,128)(2,1)} %bitcast.5), channel_id=1, source_target_pairs={{0,32},{32,64},{64,96},{96,128},{128,160},{160,192},{192,224},{224... | collective-permute-start | bytes 3145736 | tf_op jit(solution)/shard_map/ppermute | solution.py:18
  87.4 6.0 %collective-permute-start.1 = (bf16[2048,256]{1,0:T(8,128)(2,1)}, bf16[2048,256]{1,0:T(8,128)(2,1)S(1)}, u32[]{:S(2)}, u32[]{:S(2)}) collective-permute-start(bf16[2048,256]{1,0:T(8,128)(2,1)} %bitcast.5), channel_id=1, source_target_pairs={{0,480},{32,0},{64,32},{96,64},{128,96},{160,128},{192,160},{224,1... | collective-permute-start | bytes 3145736 | tf_op jit(solution)/shard_map/ppermute | solution.py:18
  93.4 30.2 %collective-permute-done = bf16[2048,256]{1,0:T(8,128)(2,1)S(1)} collective-permute-done((bf16[2048,256]{1,0:T(8,128)(2,1)}, bf16[2048,256]{1,0:T(8,128)(2,1)S(1)}, u32[]{:S(2)}, u32[]{:S(2)}) %collective-permute-start) | collective-permute-done | bytes 1048608 | tf_op jit(solution)/shard_map/ppermute | solution.py:18
  125.2 1.0 copy-done.3
  127.9 1.1 broadcast_add_fusion
  129.0 1.9 collective-permute-start.2
  130.9 7.0 %collective-permute-start.3 = (bf16[2048,256]{1,0:T(8,128)(2,1)}, bf16[2048,256]{1,0:T(8,128)(2,1)}, u32[]{:S(2)}, u32[]{:S(2)}) collective-permute-start(bf16[2048,256]{1,0:T(8,128)(2,1)} %bitcast.11), channel_id=1, source_target_pairs={{0,480},{32,0},{64,32},{96,64},{128,96},{160,128},{192,160},{224,1... | collective-permute-start | bytes 3145736 | tf_op jit(solution)/shard_map/ppermute | solution.py:18
  139.3 1.0 copy-done.1
  140.3 22.2 %shard_map.55 = (f32[8,1,512]{2,1,0:T(1,128)}, f32[8,1,512]{2,1,0:T(1,128)}, f32[8,128,512]{2,1,0:T(8,128)}) custom-call(s32[48]{0:T(128)} %reshape.45.idx_ref, s32[8]{0:T(128)} %dynamic_slice.7.cnt_ref, bf16[4096,128]{1,0:T(8,128)(2,1)} %bitcast.42, bf16[8,256,256]{2,1,0:T(8,128)(2,1)} %bitcast.4.own0, bf16[8,256,256]{2,1,0:T(8,128)(2,1)} %bitcast.9.own1), custom_call_target="tpu_custom_call" | custom-call | flops 4294967296 | bytes 5275648 | tf_op jit(solution)/shard_map/pallas_call | solution.py:150
  162.5 1.0 copy-done.4
  163.5 14.3 %shard_map.56 = bf16[4096,128]{1,0:T(8,128)(2,1)} custom-call(s32[48]{0:T(128)} %reshape.45.idx_ref, s32[8]{0:T(128)} %dynamic_slice.7.cnt_ref, bf16[4096,128]{1,0:T(8,128)(2,1)} %bitcast.43, f32[8,1,512]{2,1,0:T(1,128)} %get-tuple-element.8.m_in, f32[8,1,512]{2,1,0:T(1,128)} %get-tuple-element.9.l_in, f32[8,128,512]{2,1,0:T(8,128)} %get-tuple-element.10.acc_in, ...), custom_call_target="tpu_custom_call" | custom-call | flops 2147483648 | bytes 8421376 | tf_op jit(solution)/shard_map/pallas_call | solution.py:190
  177.8 35.9 %all_to_all.70 = bf16[32,128,128]{2,1,0:T(8,128)(2,1)S(1)} all-to-all(bf16[32,128,128]{2,1,0:T(8,128)(2,1)} %bitcast.44), channel_id=1, replica_groups=mesh['blk'=16,'head'=32] {'head'}, dimensions={0} | all-to-all | bytes 2097152 | tf_op jit(solution)/shard_map/all_to_all | solution.py:233
  213.7 1.1 copy_bitcast_fusion
  (27 shorter events, 4.4 us)
Async XLA Ops:
  0.0 51.0 %copy-start = (bf16[128,4096]{1,0:T(8,128)(2,1)S(1)}, bf16[128,4096]{1,0:T(8,128)(2,1)}, u32[]{:S(2)}) copy-start(bf16[128,4096]{1,0:T(8,128)(2,1)} %param.5) | copy-start | bytes 3145732
  0.0 1.7 copy-start.5
  5.1 41.1 %all-to-all-start.1 = ((bf16[64,32,256]{2,0,1:T(8,128)(2,1)}), bf16[64,32,256]{2,0,1:T(8,128)(2,1)}, u32[]{:S(2)}, u32[]{:S(2)}) async-start(bf16[64,32,256]{2,0,1:T(8,128)(2,1)} %all_to_all.56), calls=%async_computation.1 | async-start | bytes 2097152 | tf_op jit(solution)/shard_map/all_to_all | solution.py:203
  46.2 33.0 %all-to-all-start.2 = ((bf16[64,32,256]{2,0,1:T(8,128)(2,1)}), bf16[64,32,256]{2,0,1:T(8,128)(2,1)S(1)}, u32[]{:S(2)}, u32[]{:S(2)}) async-start(bf16[64,32,256]{2,0,1:T(8,128)(2,1)} %all_to_all.59), calls=%async_computation.2 | async-start | bytes 2097152 | tf_op jit(solution)/shard_map/all_to_all | solution.py:203
  52.3 85.6 %copy-start.6 = (s32[128,6]{0,1:T(8,128)S(1)}, s32[128,6]{0,1:T(8,128)}, u32[]{:S(2)}) copy-start(s32[128,6]{0,1:T(8,128)} %param.8) | copy-start | bytes 9220
  52.3 86.3 %copy-start.7 = (s32[128]{0:T(128)S(1)}, s32[128]{0:T(128)}, u32[]{:S(2)}) copy-start(s32[128]{0:T(128)} %param.9) | copy-start | bytes 1540
  79.2 60.1 %all-to-all-start = ((bf16[128,32,128]{2,0,1:T(8,128)(2,1)}), bf16[128,32,128]{2,0,1:T(8,128)(2,1)S(1)}, u32[]{:S(2)}, u32[]{:S(2)}) async-start(bf16[128,32,128]{2,0,1:T(8,128)(2,1)} %copy_bitcast_fusion.1), calls=%async_computation | async-start | bytes 2097152 | tf_op jit(solution)/shard_map/all_to_all | solution.py:203
  84.2 39.4 %collective-permute-start = (bf16[2048,256]{1,0:T(8,128)(2,1)}, bf16[2048,256]{1,0:T(8,128)(2,1)S(1)}, u32[]{:S(2)}, u32[]{:S(2)}) collective-permute-start(bf16[2048,256]{1,0:T(8,128)(2,1)} %bitcast.5), channel_id=1, source_target_pairs={{0,32},{32,64},{64,96},{96,128},{128,160},{160,192},{192,224},{224... | collective-permute-start | bytes 3145736 | tf_op jit(solution)/shard_map/ppermute | solution.py:18
  87.4 37.7 %collective-permute-start.1 = (bf16[2048,256]{1,0:T(8,128)(2,1)}, bf16[2048,256]{1,0:T(8,128)(2,1)S(1)}, u32[]{:S(2)}, u32[]{:S(2)}) collective-permute-start(bf16[2048,256]{1,0:T(8,128)(2,1)} %bitcast.5), channel_id=1, source_target_pairs={{0,480},{32,0},{64,32},{96,64},{128,96},{160,128},{192,160},{224,1... | collective-permute-start | bytes 3145736 | tf_op jit(solution)/shard_map/ppermute | solution.py:18
  123.6 1.0 copy-start.2
  125.2 1.0 copy-start.3
  129.0 33.5 %collective-permute-start.2 = (bf16[2048,256]{1,0:T(8,128)(2,1)}, bf16[2048,256]{1,0:T(8,128)(2,1)S(1)}, u32[]{:S(2)}, u32[]{:S(2)}) collective-permute-start(bf16[2048,256]{1,0:T(8,128)(2,1)} %bitcast.11), channel_id=1, source_target_pairs={{0,32},{32,64},{64,96},{96,128},{128,160},{160,192},{192,224},{224... | collective-permute-start | bytes 3145736 | tf_op jit(solution)/shard_map/ppermute | solution.py:18
  130.9 31.6 %collective-permute-start.3 = (bf16[2048,256]{1,0:T(8,128)(2,1)}, bf16[2048,256]{1,0:T(8,128)(2,1)}, u32[]{:S(2)}, u32[]{:S(2)}) collective-permute-start(bf16[2048,256]{1,0:T(8,128)(2,1)} %bitcast.11), channel_id=1, source_target_pairs={{0,480},{32,0},{64,32},{96,64},{128,96},{160,128},{192,160},{224,1... | collective-permute-start | bytes 3145736 | tf_op jit(solution)/shard_map/ppermute | solution.py:18
  139.3 1.0 copy-start.1
  162.5 1.0 copy-start.4

commit v9 on v7

--- a/solution.py
+++ b/solution.py
@@ -117,16 +117,20 @@
         [keys.reshape(rows, heads, HD), values.reshape(rows, heads, HD)], axis=2
     ).reshape(rows, 2 * model)
     half = rows // 2
+    query_pairs = queries.reshape(half, 2, heads, HD).transpose(0, 2, 1, 3)
+    with_queries = jnp.concatenate(
+        [paired[half:].reshape(half, heads, 2 * HD), query_pairs.reshape(half, heads, 2 * HD)], axis=2
+    ).reshape(half, 4 * model)
     kv_parts = []
     tie = None
-    for piece in (paired[:half], paired[half:]):
+    for piece in (paired[:half], with_queries):
         kv_rows = to_heads(piece)
         if tie is not None:
-            kv_rows = kv_rows + tie
+            query_rows = kv_rows[:, 2 * HD:].reshape(2 * kv_rows.shape[0], HD)
+            kv_rows = kv_rows[:, :2 * HD] + tie
         earlier, later = from_behind(kv_rows, "blk", 1), from_behind(kv_rows, "blk", -1)
         tie = ((earlier[0, 0] + later[0, 0]) * 0).astype(kv_rows.dtype)
         kv_parts.append((kv_rows, earlier, later))
-    query_rows = to_heads(queries)
     slab_shape = (lax.axis_size("head") * half // (BLOCK // 2), BLOCK // 2, 2 * HD)
     kv_parts = [kv_parts[h][p].reshape(slab_shape) for p in range(3) for h in range(2)]
     blocks_here = query_rows.shape[0] // BLOCK

time: 200 us -> 225 us (1.12)
  local copies, waits for them, and re-layouts: 13.2 us -> 22.2 us
  other arithmetic: 0.16 us -> 9.08 us
  waiting for transfers between devices: 78 us -> 86.9 us
    ppermute x4, waiting for transfers between devices: 24.4 us -> 64.2 us  [from_behind(): return lax.ppermute(value, axis, pairs)]
    all_to_all x3 -> x2, waiting for transfers between devices: 53.6 us -> 22.7 us  [to_heads(): return lax.all_to_all(x, 'head', split_axis=1, concat_axis=0, tiled=True)]
    another operation x1 -> x2, local copies, waits for them, and re-layouts: 0.14 us -> 8.82 us  [local(): jnp.stack([keys.reshape(rows, heads, HD), values.reshape(rows, heads, HD)...]
    another operation x0 -> x1, other arithmetic: none -> 7.71 us  [local(): jnp.stack([keys.reshape(rows, heads, HD), values.reshape(rows, heads, HD)...]
    all_to_all x3 -> x2, starting transfers between devices: 23.7 us -> 17.8 us  [to_heads(): return lax.all_to_all(x, 'head', split_axis=1, concat_axis=0, tiled=True)]
    ppermute x4, starting transfers between devices: 14.5 us -> 18.4 us  [from_behind(): return lax.ppermute(value, axis, pairs)]
    reshape x0 -> x4, local copies, waits for them, and re-layouts: none -> 3.65 us  [the longest x1 1.16 us: local(): query_rows = kv_rows[:, 2 * HD:].reshape(2 * kv_rows.shape[0], HD)]
    slice x3 -> x0, local copies, waits for them, and re-layouts: 2.56 us -> none  [the longest x2 1.48 us: local(): paired[half:]]
  transfers between devices with their start and end apart: 7 -> 6, of which waited for: 7 -> 5; matrix products, arithmetic and copies ran while one was open for 3% -> 4% of each run, Pallas kernels for 0% -> 0%
where the time goes in v9:
time: 225 us; the launch traced here: 224 us
  waiting for transfers between devices  86.9 us (39%)
  blocking collectives  37.2 us (17%)
  starting transfers between devices  36.2 us (16%)
  Pallas kernels  31 us (14%)
  local copies, waits for them, and re-layouts  22.2 us (10%)
  other arithmetic  9.08 us (4%)
    ppermute x4, waiting for transfers between devices, from_behind(): return lax.ppermute(value, axis, pairs)  64.2 us
    all_to_all x1, blocking collectives, local(): lax.all_to_all(attended_rows, 'head', split_axis=0, concat_axis=1, tiled=...  37.2 us
    pallas_call x1, Pallas kernels, attend(): pl.pallas_call(attention_kernel, out_shape=jax.ShapeDtypeStruct((rows, wi...  31 us
    all_to_all x2, waiting for transfers between devices, to_heads(): return lax.all_to_all(x, 'head', split_axis=1, concat_axis=0, tiled=True)  22.7 us
    ppermute x4, starting transfers between devices, from_behind(): return lax.ppermute(value, axis, pairs)  18.4 us
    all_to_all x2, starting transfers between devices, to_heads(): return lax.all_to_all(x, 'head', split_axis=1, concat_axis=0, tiled=True)  17.8 us
    another operation x2, local copies, waits for them, and re-layouts, local(): jnp.stack([keys.reshape(rows, heads, HD), values.reshape(rows, heads, HD)...  8.82 us
    another operation x1, other arithmetic, local(): jnp.stack([keys.reshape(rows, heads, HD), values.reshape(rows, heads, HD)...  7.71 us
  transfers between devices with their start and end apart: 6, of which 5 were waited for; matrix products, arithmetic and copies ran while one was open for 4% of the time, Pallas kernels for 0%

profile of v9, /device:TPU:1, one launch (start us, length us, event | category | flops | bytes accessed | tf_op | source)
XLA Modules:
  0.0 224.0 jit_solution(5642725622714473875)
XLA Ops:
  0.0 4.9 %stack_reshape.8 = bf16[128,32,1,128]{3,2,1,0:T(2,128)(2,1)S(1)} reshape(bf16[128,4096]{1,0:T(8,128)(2,1)} %param.6) | data formatting | bytes 2097152 | tf_op jit(solution)/shard_map/stack;reshape | solution.py:116
  4.9 4.0 %stack_reshape.9 = bf16[128,32,1,128]{3,2,1,0:T(2,128)(2,1)} reshape(bf16[128,4096]{1,0:T(8,128)(2,1)S(1)} %copy-done) | data formatting | bytes 2097152 | tf_op jit(solution)/shard_map/stack;reshape | solution.py:116
  8.8 7.7 %pad_maximum_fusion.1 = (bf16[64,32,2,128]{3,2,1,0:T(2,128)(2,1)}, bf16[64,32,2,128]{3,2,1,0:T(2,128)(2,1)S(1)}) fusion(bf16[128,32,1,128]{3,2,1,0:T(2,128)(2,1)} %stack_reshape.9, bf16[128,32,1,128]{3,2,1,0:T(2,128)(2,1)S(1)} %stack_reshape.8), kind=kLoop, calls=%fused_computation.6 | loop fusion | flops 4194304 | bytes 4194304 | tf_op jit(solution)/shard_map/stack | solution.py:116
  16.5 1.7 all_to_all.43
  18.3 1.6 copy.27
  19.9 13.0 %all-to-all-start.1 = ((bf16[64,32,256]{2,0,1:T(8,128)(2,1)}), bf16[64,32,256]{2,0,1:T(8,128)(2,1)}, u32[]{:S(2)}, u32[]{:S(2)}) async-start(bf16[64,32,256]{2,0,1:T(8,128)(2,1)} %copy.27), calls=%async_computation.1 | async-start | bytes 2097152 | tf_op jit(solution)/shard_map/all_to_all | solution.py:112
  33.1 1.1 copy.33
  34.9 0.7 reshape.54
  35.8 2.5 %copy.26 = bf16[64,32,512]{2,0,1:T(8,128)(2,1)} copy(bf16[64,32,512]{2,1,0:T(8,128)(2,1)S(1)} %pad_maximum_fusion) | data formatting | bytes 4194304 | tf_op jit(solution)/shard_map/concatenate | solution.py:121
  38.3 22.7 %all-to-all-done.1 = bf16[64,32,256]{2,0,1:T(8,128)(2,1)} async-done(((bf16[64,32,256]{2,0,1:T(8,128)(2,1)}), bf16[64,32,256]{2,0,1:T(8,128)(2,1)}, u32[]{:S(2)}, u32[]{:S(2)}) %all-to-all-start.1) | async-done | bytes 1048608 | tf_op jit(solution)/shard_map/all_to_all | solution.py:112
  61.0 4.9 %all-to-all-start = ((bf16[64,32,512]{2,0,1:T(8,128)(2,1)}), bf16[64,32,512]{2,0,1:T(8,128)(2,1)S(1)}, u32[]{:S(2)}, u32[]{:S(2)}) async-start(bf16[64,32,512]{2,0,1:T(8,128)(2,1)} %copy.26), calls=%async_computation | async-start | bytes 4194304 | tf_op jit(solution)/shard_map/all_to_all | solution.py:112
  65.9 7.3 %collective-permute-start.1 = (bf16[2048,256]{1,0:T(8,128)(2,1)}, bf16[2048,256]{1,0:T(8,128)(2,1)S(1)}, u32[]{:S(2)}, u32[]{:S(2)}) collective-permute-start(bf16[2048,256]{1,0:T(8,128)(2,1)} %bitcast.6), channel_id=1, source_target_pairs={{0,480},{32,0},{64,32},{96,64},{128,96},{160,128},{192,160},{224,1... | collective-permute-start | bytes 3145736 | tf_op jit(solution)/shard_map/ppermute | solution.py:18
  73.2 1.9 collective-permute-start
  75.1 34.8 %collective-permute-done.1 = bf16[2048,256]{1,0:T(8,128)(2,1)S(1)} collective-permute-done((bf16[2048,256]{1,0:T(8,128)(2,1)}, bf16[2048,256]{1,0:T(8,128)(2,1)S(1)}, u32[]{:S(2)}, u32[]{:S(2)}) %collective-permute-start.1) | collective-permute-done | bytes 1048608 | tf_op jit(solution)/shard_map/ppermute | solution.py:18
  110.5 5.2 %collective-permute-done = bf16[2048,256]{1,0:T(8,128)(2,1)S(1)} collective-permute-done((bf16[2048,256]{1,0:T(8,128)(2,1)}, bf16[2048,256]{1,0:T(8,128)(2,1)S(1)}, u32[]{:S(2)}, u32[]{:S(2)}) %collective-permute-start) | collective-permute-done | bytes 1048608 | tf_op jit(solution)/shard_map/ppermute | solution.py:18
  117.7 1.1 slice_add_fusion
  118.8 7.1 %collective-permute-start.3 = (bf16[2048,256]{1,0:T(8,128)(2,1)}, bf16[2048,256]{1,0:T(8,128)(2,1)S(1)}, u32[]{:S(2)}, u32[]{:S(2)}) collective-permute-start(bf16[2048,256]{1,0:T(8,128)(2,1)} %get-tuple-element.7), channel_id=1, source_target_pairs={{0,480},{32,0},{64,32},{96,64},{128,96},{160,128},{192,160},{224,1... | collective-permute-start | bytes 3145736 | tf_op jit(solution)/shard_map/ppermute | solution.py:18
  125.9 2.1 collective-permute-start.2
  129.5 1.2 reshape.57.q_ref
  130.6 16.7 %collective-permute-done.3 = bf16[2048,256]{1,0:T(8,128)(2,1)S(1)} collective-permute-done((bf16[2048,256]{1,0:T(8,128)(2,1)}, bf16[2048,256]{1,0:T(8,128)(2,1)S(1)}, u32[]{:S(2)}, u32[]{:S(2)}) %collective-permute-start.3) | collective-permute-done | bytes 1048608 | tf_op jit(solution)/shard_map/ppermute | solution.py:18
  147.3 7.4 %collective-permute-done.2 = bf16[2048,256]{1,0:T(8,128)(2,1)} collective-permute-done((bf16[2048,256]{1,0:T(8,128)(2,1)}, bf16[2048,256]{1,0:T(8,128)(2,1)}, u32[]{:S(2)}, u32[]{:S(2)}) %collective-permute-start.2) | collective-permute-done | bytes 1048608 | tf_op jit(solution)/shard_map/ppermute | solution.py:18
  154.8 31.0 %shard_map.55 = bf16[4096,128]{1,0:T(8,128)(2,1)} custom-call(s32[48]{0:T(128)} %reshape.53.idx_ref, s32[8]{0:T(128)} %dynamic_slice.7.cnt_ref, bf16[4096,128]{1,0:T(8,128)(2,1)} %reshape.57.q_ref, bf16[8,256,256]{2,1,0:T(8,128)(2,1)} %bitcast.4.refs_0_, bf16[8,256,256]{2,1,0:T(8,128)(2,1)} %bitcast.9.refs_1_, bf16[8,256,256]{2,1,0:T(8,128)(2,1)} %bitcast.33, ...), custom_call_target="tpu_custom_call" | custom-call | flops 6442450944 | bytes 8388608 | tf_op jit(solution)/shard_map/pallas_call | solution.py:99
  185.7 37.2 %all_to_all.54 = bf16[32,128,128]{2,1,0:T(8,128)(2,1)S(1)} all-to-all(bf16[32,128,128]{2,1,0:T(8,128)(2,1)} %bitcast.31), channel_id=1, replica_groups=mesh['blk'=16,'head'=32] {'head'}, dimensions={0} | all-to-all | bytes 2097152 | tf_op jit(solution)/shard_map/all_to_all | solution.py:144
  222.9 1.1 copy_bitcast_fusion
  (24 shorter events, 3.8 us)
Async XLA Ops:
  0.0 4.9 %copy-start = (bf16[128,4096]{1,0:T(8,128)(2,1)S(1)}, bf16[128,4096]{1,0:T(8,128)(2,1)}, u32[]{:S(2)}) copy-start(bf16[128,4096]{1,0:T(8,128)(2,1)} %param.7) | copy-start | bytes 3145732
  18.3 14.5 %copy-start.1 = (bf16[128,4096]{1,0:T(8,128)(2,1)S(1)}, bf16[128,4096]{1,0:T(8,128)(2,1)}, u32[]{:S(2)}) copy-start(bf16[128,4096]{1,0:T(8,128)(2,1)} %param.5) | copy-start | bytes 3145732
  19.9 41.1 %all-to-all-start.1 = ((bf16[64,32,256]{2,0,1:T(8,128)(2,1)}), bf16[64,32,256]{2,0,1:T(8,128)(2,1)}, u32[]{:S(2)}, u32[]{:S(2)}) async-start(bf16[64,32,256]{2,0,1:T(8,128)(2,1)} %copy.27), calls=%async_computation.1 | async-start | bytes 2097152 | tf_op jit(solution)/shard_map/all_to_all | solution.py:112
  61.0 56.7 %all-to-all-start = ((bf16[64,32,512]{2,0,1:T(8,128)(2,1)}), bf16[64,32,512]{2,0,1:T(8,128)(2,1)S(1)}, u32[]{:S(2)}, u32[]{:S(2)}) async-start(bf16[64,32,512]{2,0,1:T(8,128)(2,1)} %copy.26), calls=%async_computation | async-start | bytes 4194304 | tf_op jit(solution)/shard_map/all_to_all | solution.py:112
  65.9 44.0 %collective-permute-start.1 = (bf16[2048,256]{1,0:T(8,128)(2,1)}, bf16[2048,256]{1,0:T(8,128)(2,1)S(1)}, u32[]{:S(2)}, u32[]{:S(2)}) collective-permute-start(bf16[2048,256]{1,0:T(8,128)(2,1)} %bitcast.6), channel_id=1, source_target_pairs={{0,480},{32,0},{64,32},{96,64},{128,96},{160,128},{192,160},{224,1... | collective-permute-start | bytes 3145736 | tf_op jit(solution)/shard_map/ppermute | solution.py:18
  73.2 42.6 %collective-permute-start = (bf16[2048,256]{1,0:T(8,128)(2,1)}, bf16[2048,256]{1,0:T(8,128)(2,1)S(1)}, u32[]{:S(2)}, u32[]{:S(2)}) collective-permute-start(bf16[2048,256]{1,0:T(8,128)(2,1)} %bitcast.6), channel_id=1, source_target_pairs={{0,32},{32,64},{64,96},{96,128},{128,160},{160,192},{192,224},{224... | collective-permute-start | bytes 3145736 | tf_op jit(solution)/shard_map/ppermute | solution.py:18
  109.9 7.7 %copy-start.3 = (bf16[2048,256]{1,0:T(8,128)(2,1)}, bf16[2048,256]{1,0:T(8,128)(2,1)S(1)}, u32[]{:S(2)}) copy-start(bf16[2048,256]{1,0:T(8,128)(2,1)S(1)} %collective-permute-done.1) | copy-start | bytes 3145732
  115.8 1.9 copy-start.4
  117.7 10.3 %copy-start.6 = (s32[128]{0:T(128)S(1)}, s32[128]{0:T(128)}, u32[]{:S(2)}) copy-start(s32[128]{0:T(128)} %param.9) | copy-start | bytes 1540
  117.7 11.0 %copy-start.2 = (s32[128,6]{0,1:T(8,128)S(1)}, s32[128,6]{0,1:T(8,128)}, u32[]{:S(2)}) copy-start(s32[128,6]{0,1:T(8,128)} %param.8) | copy-start | bytes 9220
  118.8 28.5 %collective-permute-start.3 = (bf16[2048,256]{1,0:T(8,128)(2,1)}, bf16[2048,256]{1,0:T(8,128)(2,1)S(1)}, u32[]{:S(2)}, u32[]{:S(2)}) collective-permute-start(bf16[2048,256]{1,0:T(8,128)(2,1)} %get-tuple-element.7), channel_id=1, source_target_pairs={{0,480},{32,0},{64,32},{96,64},{128,96},{160,128},{192,160},{224,1... | collective-permute-start | bytes 3145736 | tf_op jit(solution)/shard_map/ppermute | solution.py:18
  125.9 28.8 %collective-permute-start.2 = (bf16[2048,256]{1,0:T(8,128)(2,1)}, bf16[2048,256]{1,0:T(8,128)(2,1)}, u32[]{:S(2)}, u32[]{:S(2)}) collective-permute-start(bf16[2048,256]{1,0:T(8,128)(2,1)} %get-tuple-element.7), channel_id=1, source_target_pairs={{0,32},{32,64},{64,96},{96,128},{128,160},{160,192},{192,224},{224... | collective-permute-start | bytes 3145736 | tf_op jit(solution)/shard_map/ppermute | solution.py:18
  147.3 7.5 %copy-start.5 = (bf16[2048,256]{1,0:T(8,128)(2,1)}, bf16[2048,256]{1,0:T(8,128)(2,1)S(1)}, u32[]{:S(2)}) copy-start(bf16[2048,256]{1,0:T(8,128)(2,1)S(1)} %collective-permute-done.3) | copy-start | bytes 3145732

commit v10 on v7

--- a/solution.py
+++ b/solution.py
@@ -29,11 +29,11 @@
         copies = []
         for i, slab in enumerate(slabs):
             part, half = (1, 0, 2)[i // 2], i % 2
-            for column, dst in ((0, k_scr), (width, v_scr)):
+            for kind, dst in ((0, k_scr), (1, v_scr)):
                 copy = pltpu.make_async_copy(
-                    slab.at[:, :, pl.ds(column, width)],
+                    slab.at[:, :, kind],
                     dst.at[pl.ds(part * blocks, blocks), half],
-                    sem.at[2 * i + column // width],
+                    sem.at[2 * i + kind],
                 )
                 copy.start()
                 copies.append(copy)
@@ -73,6 +73,7 @@
 def attend(query_rows, kv_parts, local_index, count_rows):
     rows, width = query_rows.shape
     blocks_here = rows // BLOCK
+    _, devs, _, part_rows, _ = kv_parts[0].shape
     shard_rows = rows
     flops = blocks_here * MAXB * BLOCK * BLOCK * width * 4
     cost = pl.CostEstimate(
@@ -87,8 +88,8 @@
         in_specs=[pl.BlockSpec((BLOCK, width), lambda b, idx, cnt: (b, 0))] + [any_spec] * 6,
         out_specs=pl.BlockSpec((BLOCK, width), lambda b, idx, cnt: (b, 0)),
         scratch_shapes=[
-            pltpu.VMEM((3 * blocks_here, 2, BLOCK // 2, width), jnp.bfloat16),
-            pltpu.VMEM((3 * blocks_here, 2, BLOCK // 2, width), jnp.bfloat16),
+            pltpu.VMEM((3 * blocks_here, 2, devs, part_rows, width), jnp.bfloat16),
+            pltpu.VMEM((3 * blocks_here, 2, devs, part_rows, width), jnp.bfloat16),
             pltpu.VMEM((MAXB, BLOCK, BLOCK), jnp.float32),
             pltpu.VMEM((1, BLOCK), jnp.float32),
             pltpu.VMEM((1, BLOCK), jnp.float32),
@@ -111,23 +112,20 @@
     def to_heads(x):
         return lax.all_to_all(x, "head", split_axis=1, concat_axis=0, tiled=True)
 
-    rows, model = keys.shape
-    heads = model // HD
-    paired = jnp.stack(
-        [keys.reshape(rows, heads, HD), values.reshape(rows, heads, HD)], axis=2
-    ).reshape(rows, 2 * model)
+    rows = keys.shape[0]
     half = rows // 2
     kv_parts = []
     tie = None
-    for piece in (paired[:half], paired[half:]):
-        kv_rows = to_heads(piece)
+    for start in (0, half):
+        kv_rows = to_heads(jnp.concatenate([keys[start:start + half], values[start:start + half]], axis=0))
         if tie is not None:
             kv_rows = kv_rows + tie
         earlier, later = from_behind(kv_rows, "blk", 1), from_behind(kv_rows, "blk", -1)
         tie = ((earlier[0, 0] + later[0, 0]) * 0).astype(kv_rows.dtype)
         kv_parts.append((kv_rows, earlier, later))
     query_rows = to_heads(queries)
-    slab_shape = (lax.axis_size("head") * half // (BLOCK // 2), BLOCK // 2, 2 * HD)
+    devs = BLOCK // rows
+    slab_shape = (lax.axis_size("head") // devs, devs, 2, half, HD)
     kv_parts = [kv_parts[h][p].reshape(slab_shape) for p in range(3) for h in range(2)]
     blocks_here = query_rows.shape[0] // BLOCK
     total_blocks = blocks_here * cycle_size

time: 200 us -> 197 us (0.985)
  local copies, waits for them, and re-layouts: 13.2 us -> 8 us
  other arithmetic: 0.16 us -> 2.71 us
    all_to_all x3 -> x1, local copies, waits for them, and re-layouts: 4.26 us -> 1.26 us  [to_heads(): return lax.all_to_all(x, 'head', split_axis=1, concat_axis=0, tiled=True)]
    all_to_all x0 -> x2, other arithmetic: none -> 2.56 us  [to_heads(): return lax.all_to_all(x, 'head', split_axis=1, concat_axis=0, tiled=True)]
where the time goes in v10:
time: 197 us; the launch traced here: 196 us
  waiting for transfers between devices  78.6 us (40%)
  starting transfers between devices  38.3 us (19%)
  blocking collectives  37.2 us (19%)
  Pallas kernels  29.7 us (15%)
  local copies, waits for them, and re-layouts  8 us (4%)
  other arithmetic  2.71 us (1%)
    all_to_all x3, waiting for transfers between devices, to_heads(): return lax.all_to_all(x, 'head', split_axis=1, concat_axis=0, tiled=True)  55 us
    all_to_all x1, blocking collectives, local(): lax.all_to_all(attended_rows, 'head', split_axis=0, concat_axis=1, tiled=...  37.2 us
    pallas_call x1, Pallas kernels, attend(): pl.pallas_call(attention_kernel, out_shape=jax.ShapeDtypeStruct((rows, wi...  29.7 us
    all_to_all x3, starting transfers between devices, to_heads(): return lax.all_to_all(x, 'head', split_axis=1, concat_axis=0, tiled=True)  23.7 us
    ppermute x4, waiting for transfers between devices, from_behind(): return lax.ppermute(value, axis, pairs)  23.6 us
    ppermute x4, starting transfers between devices, from_behind(): return lax.ppermute(value, axis, pairs)  14.6 us
  transfers between devices with their start and end apart: 7, of which 7 were waited for; matrix products, arithmetic and copies ran while one was open for 3% of the time, Pallas kernels for 0%

profile of v10, /device:TPU:1, one launch (start us, length us, event | category | flops | bytes accessed | tf_op | source)
XLA Modules:
  0.0 196.0 jit_solution(11249415987461060778)
XLA Ops:
  0.0 1.7 fusion.2
  1.8 1.3 copy_bitcast_fusion.2
  3.0 12.9 %all-to-all-start.1 = ((bf16[128,32,128]{2,0,1:T(8,128)(2,1)}), bf16[128,32,128]{2,0,1:T(8,128)(2,1)S(1)}, u32[]{:S(2)}, u32[]{:S(2)}) async-start(bf16[128,32,128]{2,0,1:T(8,128)(2,1)} %copy_bitcast_fusion.2), calls=%async_computation.1 | async-start | bytes 2097152 | tf_op jit(solution)/shard_map/all_to_all | solution.py:113
  15.9 1.3 copy_bitcast_fusion.1
  17.2 26.8 %all-to-all-done.1 = bf16[128,32,128]{2,0,1:T(8,128)(2,1)S(1)} async-done(((bf16[128,32,128]{2,0,1:T(8,128)(2,1)}), bf16[128,32,128]{2,0,1:T(8,128)(2,1)S(1)}, u32[]{:S(2)}, u32[]{:S(2)}) %all-to-all-start.1) | async-done | bytes 1048608 | tf_op jit(solution)/shard_map/all_to_all | solution.py:113
  44.1 4.8 %all-to-all-start.2 = ((bf16[128,32,128]{2,0,1:T(8,128)(2,1)}), bf16[128,32,128]{2,0,1:T(8,128)(2,1)S(1)}, u32[]{:S(2)}, u32[]{:S(2)}) async-start(bf16[128,32,128]{2,0,1:T(8,128)(2,1)} %copy_bitcast_fusion.1), calls=%async_computation.2 | async-start | bytes 2097152 | tf_op jit(solution)/shard_map/all_to_all | solution.py:113
  48.9 7.3 %collective-permute-start.1 = (bf16[4096,128]{1,0:T(8,128)(2,1)S(1)}, bf16[4096,128]{1,0:T(8,128)(2,1)}, u32[]{:S(2)}, u32[]{:S(2)}) collective-permute-start(bf16[4096,128]{1,0:T(8,128)(2,1)S(1)} %bitcast.43), channel_id=1, source_target_pairs={{0,480},{32,0},{64,32},{96,64},{128,96},{160,128},{192,160},{224,1... | collective-permute-start | bytes 3145736 | tf_op jit(solution)/shard_map/ppermute | solution.py:18
  56.2 1.9 collective-permute-start
  58.1 1.3 copy_bitcast_fusion.3
  59.4 17.8 %all-to-all-done.2 = bf16[128,32,128]{2,0,1:T(8,128)(2,1)S(1)} async-done(((bf16[128,32,128]{2,0,1:T(8,128)(2,1)}), bf16[128,32,128]{2,0,1:T(8,128)(2,1)S(1)}, u32[]{:S(2)}, u32[]{:S(2)}) %all-to-all-start.2) | async-done | bytes 1048608 | tf_op jit(solution)/shard_map/all_to_all | solution.py:113
  77.2 6.0 %all-to-all-start = ((bf16[128,32,128]{2,0,1:T(8,128)(2,1)}), bf16[128,32,128]{2,0,1:T(8,128)(2,1)}, u32[]{:S(2)}, u32[]{:S(2)}) async-start(bf16[128,32,128]{2,0,1:T(8,128)(2,1)} %copy_bitcast_fusion.3), calls=%async_computation | async-start | bytes 2097152 | tf_op jit(solution)/shard_map/all_to_all | solution.py:113
  83.2 2.7 %collective-permute-done.1 = bf16[4096,128]{1,0:T(8,128)(2,1)} collective-permute-done((bf16[4096,128]{1,0:T(8,128)(2,1)S(1)}, bf16[4096,128]{1,0:T(8,128)(2,1)}, u32[]{:S(2)}, u32[]{:S(2)}) %collective-permute-start.1) | collective-permute-done | bytes 1048608 | tf_op jit(solution)/shard_map/ppermute | solution.py:18
  85.9 1.3 slice.25
  87.1 4.3 %collective-permute-done = bf16[4096,128]{1,0:T(8,128)(2,1)} collective-permute-done((bf16[4096,128]{1,0:T(8,128)(2,1)S(1)}, bf16[4096,128]{1,0:T(8,128)(2,1)}, u32[]{:S(2)}, u32[]{:S(2)}) %collective-permute-start) | collective-permute-done | bytes 1048608 | tf_op jit(solution)/shard_map/ppermute | solution.py:18
  91.5 1.2 slice.24
  94.0 3.5 %collective-permute-start.3 = (bf16[4096,128]{1,0:T(8,128)(2,1)S(1)}, bf16[4096,128]{1,0:T(8,128)(2,1)}, u32[]{:S(2)}, u32[]{:S(2)}) collective-permute-start(bf16[4096,128]{1,0:T(8,128)(2,1)S(1)} %bitcast.40), channel_id=1, source_target_pairs={{0,480},{32,0},{64,32},{96,64},{128,96},{160,128},{192,160},{224,1... | collective-permute-start | bytes 3145736 | tf_op jit(solution)/shard_map/ppermute | solution.py:18
  97.6 1.9 collective-permute-start.2
  100.3 0.7 reshape.40.idx_ref
  101.0 10.4 %all-to-all-done = bf16[128,32,128]{2,0,1:T(8,128)(2,1)} async-done(((bf16[128,32,128]{2,0,1:T(8,128)(2,1)}), bf16[128,32,128]{2,0,1:T(8,128)(2,1)}, u32[]{:S(2)}, u32[]{:S(2)}) %all-to-all-start) | async-done | bytes 1048608 | tf_op jit(solution)/shard_map/all_to_all | solution.py:113
  111.4 11.3 %collective-permute-done.3 = bf16[4096,128]{1,0:T(8,128)(2,1)} collective-permute-done((bf16[4096,128]{1,0:T(8,128)(2,1)S(1)}, bf16[4096,128]{1,0:T(8,128)(2,1)}, u32[]{:S(2)}, u32[]{:S(2)}) %collective-permute-start.3) | collective-permute-done | bytes 1048608 | tf_op jit(solution)/shard_map/ppermute | solution.py:18
  122.7 5.2 %collective-permute-done.2 = bf16[4096,128]{1,0:T(8,128)(2,1)} collective-permute-done((bf16[4096,128]{1,0:T(8,128)(2,1)S(1)}, bf16[4096,128]{1,0:T(8,128)(2,1)}, u32[]{:S(2)}, u32[]{:S(2)}) %collective-permute-start.2) | collective-permute-done | bytes 1048608 | tf_op jit(solution)/shard_map/ppermute | solution.py:18
  127.9 29.7 %shard_map.55 = bf16[4096,128]{1,0:T(8,128)(2,1)} custom-call(s32[48]{0:T(128)} %reshape.40.idx_ref, s32[8]{0:T(128)} %dynamic_slice.7.cnt_ref, bf16[4096,128]{1,0:T(8,128)(2,1)} %bitcast.1.q_ref, bf16[8,4,2,64,128]{4,3,2,1,0:T(8,128)(2,1)} %bitcast.45, bf16[8,4,2,64,128]{4,3,2,1,0:T(8,128)(2,1)} %bitcast.42, bf16[8,4,2,64,128]{4,3,2,1,0:T(8,128)(2,1)} %bitcast.9.refs_2_, ...), custom_call_target="tpu_custom_call" | custom-call | flops 6442450944 | bytes 8388608 | tf_op jit(solution)/shard_map/pallas_call | solution.py:100
  157.7 37.2 %all_to_all.70 = bf16[32,128,128]{2,1,0:T(8,128)(2,1)S(1)} all-to-all(bf16[32,128,128]{2,1,0:T(8,128)(2,1)} %bitcast.46), channel_id=1, replica_groups=mesh['blk'=16,'head'=32] {'head'}, dimensions={0} | all-to-all | bytes 2097152 | tf_op jit(solution)/shard_map/all_to_all | solution.py:138
  194.9 1.1 copy_bitcast_fusion
  (14 shorter events, 0.9 us)
Async XLA Ops:
  0.0 58.1 %copy-start = (bf16[128,4096]{1,0:T(8,128)(2,1)S(1)}, bf16[128,4096]{1,0:T(8,128)(2,1)}, u32[]{:S(2)}) copy-start(bf16[128,4096]{1,0:T(8,128)(2,1)} %param.5) | copy-start | bytes 3145732
  3.0 41.1 %all-to-all-start.1 = ((bf16[128,32,128]{2,0,1:T(8,128)(2,1)}), bf16[128,32,128]{2,0,1:T(8,128)(2,1)S(1)}, u32[]{:S(2)}, u32[]{:S(2)}) async-start(bf16[128,32,128]{2,0,1:T(8,128)(2,1)} %copy_bitcast_fusion.2), calls=%async_computation.1 | async-start | bytes 2097152 | tf_op jit(solution)/shard_map/all_to_all | solution.py:113
  44.1 12.1 %copy-start.2 = (bf16[128,32,128]{2,0,1:T(8,128)(2,1)}, bf16[128,32,128]{2,0,1:T(8,128)(2,1)S(1)}, u32[]{:S(2)}) copy-start(bf16[128,32,128]{2,0,1:T(8,128)(2,1)S(1)} %all-to-all-done.1) | copy-start | bytes 3145732
  44.1 33.1 %all-to-all-start.2 = ((bf16[128,32,128]{2,0,1:T(8,128)(2,1)}), bf16[128,32,128]{2,0,1:T(8,128)(2,1)S(1)}, u32[]{:S(2)}, u32[]{:S(2)}) async-start(bf16[128,32,128]{2,0,1:T(8,128)(2,1)} %copy_bitcast_fusion.1), calls=%async_computation.2 | async-start | bytes 2097152 | tf_op jit(solution)/shard_map/all_to_all | solution.py:113
  48.9 37.0 %collective-permute-start.1 = (bf16[4096,128]{1,0:T(8,128)(2,1)S(1)}, bf16[4096,128]{1,0:T(8,128)(2,1)}, u32[]{:S(2)}, u32[]{:S(2)}) collective-permute-start(bf16[4096,128]{1,0:T(8,128)(2,1)S(1)} %bitcast.43), channel_id=1, source_target_pairs={{0,480},{32,0},{64,32},{96,64},{128,96},{160,128},{192,160},{224,1... | collective-permute-start | bytes 3145736 | tf_op jit(solution)/shard_map/ppermute | solution.py:18
  56.2 35.3 %collective-permute-start = (bf16[4096,128]{1,0:T(8,128)(2,1)S(1)}, bf16[4096,128]{1,0:T(8,128)(2,1)}, u32[]{:S(2)}, u32[]{:S(2)}) collective-permute-start(bf16[4096,128]{1,0:T(8,128)(2,1)S(1)} %bitcast.44), channel_id=1, source_target_pairs={{0,32},{32,64},{64,96},{96,128},{128,160},{160,192},{192,224},{224... | collective-permute-start | bytes 3145736 | tf_op jit(solution)/shard_map/ppermute | solution.py:18
  77.2 34.2 %all-to-all-start = ((bf16[128,32,128]{2,0,1:T(8,128)(2,1)}), bf16[128,32,128]{2,0,1:T(8,128)(2,1)}, u32[]{:S(2)}, u32[]{:S(2)}) async-start(bf16[128,32,128]{2,0,1:T(8,128)(2,1)} %copy_bitcast_fusion.3), calls=%async_computation | async-start | bytes 2097152 | tf_op jit(solution)/shard_map/all_to_all | solution.py:113
  93.9 5.6 %copy-start.4 = (s32[128]{0:T(128)S(1)}, s32[128]{0:T(128)}, u32[]{:S(2)}) copy-start(s32[128]{0:T(128)} %param.9) | copy-start | bytes 1540
  93.9 6.2 %copy-start.3 = (s32[128,6]{0,1:T(8,128)S(1)}, s32[128,6]{0,1:T(8,128)}, u32[]{:S(2)}) copy-start(s32[128,6]{0,1:T(8,128)} %param.8) | copy-start | bytes 9220
  94.0 33.9 %copy-start.1 = (bf16[128,32,128]{2,0,1:T(8,128)(2,1)}, bf16[128,32,128]{2,0,1:T(8,128)(2,1)S(1)}, u32[]{:S(2)}) copy-start(bf16[128,32,128]{2,0,1:T(8,128)(2,1)S(1)} %broadcast_add_fusion) | copy-start | bytes 3145732
  94.0 28.6 %collective-permute-start.3 = (bf16[4096,128]{1,0:T(8,128)(2,1)S(1)}, bf16[4096,128]{1,0:T(8,128)(2,1)}, u32[]{:S(2)}, u32[]{:S(2)}) collective-permute-start(bf16[4096,128]{1,0:T(8,128)(2,1)S(1)} %bitcast.40), channel_id=1, source_target_pairs={{0,480},{32,0},{64,32},{96,64},{128,96},{160,128},{192,160},{224,1... | collective-permute-start | bytes 3145736 | tf_op jit(solution)/shard_map/ppermute | solution.py:18
  97.6 30.4 %collective-permute-start.2 = (bf16[4096,128]{1,0:T(8,128)(2,1)S(1)}, bf16[4096,128]{1,0:T(8,128)(2,1)}, u32[]{:S(2)}, u32[]{:S(2)}) collective-permute-start(bf16[4096,128]{1,0:T(8,128)(2,1)S(1)} %bitcast.41), channel_id=1, source_target_pairs={{0,32},{32,64},{64,96},{96,128},{128,160},{160,192},{192,224},{224... | collective-permute-start | bytes 3145736 | tf_op jit(solution)/shard_map/ppermute | solution.py:18

commit v11 on v10

--- a/solution.py
+++ b/solution.py
@@ -115,13 +115,13 @@
     rows = keys.shape[0]
     half = rows // 2
     kv_parts = []
-    tie = None
     for start in (0, half):
         kv_rows = to_heads(jnp.concatenate([keys[start:start + half], values[start:start + half]], axis=0))
-        if tie is not None:
-            kv_rows = kv_rows + tie
+        if kv_parts:
+            own, earlier, later = kv_parts[0]
+            kv_rows, earlier, later = lax.optimization_barrier((kv_rows, earlier, later))
+            kv_parts[0] = (own, earlier, later)
         earlier, later = from_behind(kv_rows, "blk", 1), from_behind(kv_rows, "blk", -1)
-        tie = ((earlier[0, 0] + later[0, 0]) * 0).astype(kv_rows.dtype)
         kv_parts.append((kv_rows, earlier, later))
     query_rows = to_heads(queries)
     devs = BLOCK // rows

time: 197 us -> 199 us (1.010)
  local copies, waits for them, and re-layouts: 8 us -> 10.6 us
  waiting for transfers between devices: 78.6 us -> 76.3 us
  Pallas kernels: 29.7 us -> 31.7 us
    slice x2 -> x0, local copies, waits for them, and re-layouts: 2.46 us -> none  [local(): tie = ((earlier[0, 0] + later[0, 0]) * 0).astype(kv_rows.dtype)]
    all_to_all x1 -> x2, local copies, waits for them, and re-layouts: 1.26 us -> 3.52 us  [to_heads(): return lax.all_to_all(x, 'head', split_axis=1, concat_axis=0, tiled=True)]
    all_to_all x3, waiting for transfers between devices: 55 us -> 53 us  [to_heads(): return lax.all_to_all(x, 'head', split_axis=1, concat_axis=0, tiled=True)]
    unnamed x10 -> x12, local copies, waits for them, and re-layouts: 0.02 us -> 2.02 us
  transfers between devices with their start and end apart: 7 -> 7, of which waited for: 7 -> 7; matrix products, arithmetic and copies ran while one was open for 3% -> 4% of each run, Pallas kernels for 0% -> 0%
where the time goes in v11:
time: 199 us; the launch traced here: 198 us
  waiting for transfers between devices  76.3 us (38%)
  blocking collectives  38.5 us (19%)
  starting transfers between devices  38.1 us (19%)
  Pallas kernels  31.7 us (16%)
  local copies, waits for them, and re-layouts  10.6 us (5%)
  other arithmetic  2.92 us (1%)
    all_to_all x3, waiting for transfers between devices, to_heads(): return lax.all_to_all(x, 'head', split_axis=1, concat_axis=0, tiled=True)  53 us
    all_to_all x1, blocking collectives, local(): lax.all_to_all(attended_rows, 'head', split_axis=0, concat_axis=1, tiled=...  38.5 us
    pallas_call x1, Pallas kernels, attend(): pl.pallas_call(attention_kernel, out_shape=jax.ShapeDtypeStruct((rows, wi...  31.7 us
    all_to_all x3, starting transfers between devices, to_heads(): return lax.all_to_all(x, 'head', split_axis=1, concat_axis=0, tiled=True)  23.7 us
    ppermute x4, waiting for transfers between devices, from_behind(): return lax.ppermute(value, axis, pairs)  23.3 us
    ppermute x4, starting transfers between devices, from_behind(): return lax.ppermute(value, axis, pairs)  14.5 us
  transfers between devices with their start and end apart: 7, of which 7 were waited for; matrix products, arithmetic and copies ran while one was open for 4% of the time, Pallas kernels for 0%

profile of v11, /device:TPU:1, one launch (start us, length us, event | category | flops | bytes accessed | tf_op | source)
XLA Modules:
  0.0 198.3 jit_solution(7925076304505152345)
XLA Ops:
  0.0 2.6 %fusion.2 = (bf16[64,4096]{1,0:T(8,128)(2,1)S(1)}, bf16[64,4096]{1,0:T(8,128)(2,1)S(1)}, bf16[64,4096]{1,0:T(8,128)(2,1)S(1)}, bf16[64,4096]{1,0:T(8,128)(2,1)}) fusion(bf16[128,4096]{1,0:T(8,128)(2,1)} %param.6, bf16[128,4096]{1,0:T(8,128)(2,1)} %param.7), kind=kLoop, calls=%fused_computation.10 | loop fusion | bytes 4194304 | tf_op jit(solution)/shard_map/slice | solution.py:119
  2.6 1.3 copy_bitcast_fusion.1
  3.9 13.0 %all-to-all-start.1 = ((bf16[128,32,128]{2,0,1:T(8,128)(2,1)}), bf16[128,32,128]{2,0,1:T(8,128)(2,1)}, u32[]{:S(2)}, u32[]{:S(2)}) async-start(bf16[128,32,128]{2,0,1:T(8,128)(2,1)} %copy_bitcast_fusion.1), calls=%async_computation.1 | async-start | bytes 2097152 | tf_op jit(solution)/shard_map/all_to_all | solution.py:113
  17.3 1.5 copy.23
  18.8 1.6 pad_maximum_fusion
  20.4 2.3 %copy.20 = bf16[128,32,128]{2,0,1:T(8,128)(2,1)} copy(bf16[128,32,128]{0,2,1:T(8,128)(2,1)} %bitcast.34) | data formatting | bytes 2097152 | tf_op jit(solution)/shard_map/all_to_all | solution.py:113
  22.7 22.3 %all-to-all-done.1 = bf16[128,32,128]{2,0,1:T(8,128)(2,1)} async-done(((bf16[128,32,128]{2,0,1:T(8,128)(2,1)}), bf16[128,32,128]{2,0,1:T(8,128)(2,1)}, u32[]{:S(2)}, u32[]{:S(2)}) %all-to-all-start.1) | async-done | bytes 1048608 | tf_op jit(solution)/shard_map/all_to_all | solution.py:113
  45.0 4.8 %all-to-all-start.2 = ((bf16[128,32,128]{2,0,1:T(8,128)(2,1)}), bf16[128,32,128]{2,0,1:T(8,128)(2,1)S(1)}, u32[]{:S(2)}, u32[]{:S(2)}) async-start(bf16[128,32,128]{2,0,1:T(8,128)(2,1)} %copy.20), calls=%async_computation.2 | async-start | bytes 2097152 | tf_op jit(solution)/shard_map/all_to_all | solution.py:113
  49.8 7.3 %collective-permute-start.1 = (bf16[4096,128]{1,0:T(8,128)(2,1)}, bf16[4096,128]{1,0:T(8,128)(2,1)}, u32[]{:S(2)}, u32[]{:S(2)}) collective-permute-start(bf16[4096,128]{1,0:T(8,128)(2,1)} %bitcast.7), channel_id=1, source_target_pairs={{0,480},{32,0},{64,32},{96,64},{128,96},{160,128},{192,160},{224,1... | collective-permute-start | bytes 3145736 | tf_op jit(solution)/shard_map/ppermute | solution.py:18
  57.1 1.9 collective-permute-start
  59.0 1.3 copy_bitcast_fusion.2
  60.3 17.8 %all-to-all-done.2 = bf16[128,32,128]{2,0,1:T(8,128)(2,1)S(1)} async-done(((bf16[128,32,128]{2,0,1:T(8,128)(2,1)}), bf16[128,32,128]{2,0,1:T(8,128)(2,1)S(1)}, u32[]{:S(2)}, u32[]{:S(2)}) %all-to-all-start.2) | async-done | bytes 1048608 | tf_op jit(solution)/shard_map/all_to_all | solution.py:113
  78.1 5.9 %all-to-all-start = ((bf16[128,32,128]{2,0,1:T(8,128)(2,1)}), bf16[128,32,128]{2,0,1:T(8,128)(2,1)S(1)}, u32[]{:S(2)}, u32[]{:S(2)}) async-start(bf16[128,32,128]{2,0,1:T(8,128)(2,1)} %copy_bitcast_fusion.2), calls=%async_computation | async-start | bytes 2097152 | tf_op jit(solution)/shard_map/all_to_all | solution.py:113
  84.0 2.9 %collective-permute-done.1 = bf16[4096,128]{1,0:T(8,128)(2,1)} collective-permute-done((bf16[4096,128]{1,0:T(8,128)(2,1)}, bf16[4096,128]{1,0:T(8,128)(2,1)}, u32[]{:S(2)}, u32[]{:S(2)}) %collective-permute-start.1) | collective-permute-done | bytes 1048608 | tf_op jit(solution)/shard_map/ppermute | solution.py:18
  87.0 5.7 %collective-permute-done = bf16[4096,128]{1,0:T(8,128)(2,1)} collective-permute-done((bf16[4096,128]{1,0:T(8,128)(2,1)}, bf16[4096,128]{1,0:T(8,128)(2,1)}, u32[]{:S(2)}, u32[]{:S(2)}) %collective-permute-start) | collective-permute-done | bytes 1048608 | tf_op jit(solution)/shard_map/ppermute | solution.py:18
  92.7 2.1 %collective-permute-start.3 = (bf16[4096,128]{1,0:T(8,128)(2,1)S(1)}, bf16[4096,128]{1,0:T(8,128)(2,1)}, u32[]{:S(2)}, u32[]{:S(2)}) collective-permute-start(bf16[4096,128]{1,0:T(8,128)(2,1)S(1)} %bitcast.35), channel_id=1, source_target_pairs={{0,480},{32,0},{64,32},{96,64},{128,96},{160,128},{192,160},{224,1... | collective-permute-start | bytes 3145736 | tf_op jit(solution)/shard_map/ppermute | solution.py:18
  94.8 3.2 %collective-permute-start.2 = (bf16[4096,128]{1,0:T(8,128)(2,1)S(1)}, bf16[4096,128]{1,0:T(8,128)(2,1)}, u32[]{:S(2)}, u32[]{:S(2)}) collective-permute-start(bf16[4096,128]{1,0:T(8,128)(2,1)S(1)} %bitcast.36), channel_id=1, source_target_pairs={{0,32},{32,64},{64,96},{96,128},{128,160},{160,192},{192,224},{224... | collective-permute-start | bytes 3145736 | tf_op jit(solution)/shard_map/ppermute | solution.py:18
  98.8 0.7 reshape.34.idx_ref
  99.5 12.8 %all-to-all-done = bf16[128,32,128]{2,0,1:T(8,128)(2,1)S(1)} async-done(((bf16[128,32,128]{2,0,1:T(8,128)(2,1)}), bf16[128,32,128]{2,0,1:T(8,128)(2,1)S(1)}, u32[]{:S(2)}, u32[]{:S(2)}) %all-to-all-start) | async-done | bytes 1048608 | tf_op jit(solution)/shard_map/all_to_all | solution.py:113
  112.3 8.3 %collective-permute-done.3 = bf16[4096,128]{1,0:T(8,128)(2,1)} collective-permute-done((bf16[4096,128]{1,0:T(8,128)(2,1)S(1)}, bf16[4096,128]{1,0:T(8,128)(2,1)}, u32[]{:S(2)}, u32[]{:S(2)}) %collective-permute-start.3) | collective-permute-done | bytes 1048608 | tf_op jit(solution)/shard_map/ppermute | solution.py:18
  120.6 6.3 %collective-permute-done.2 = bf16[4096,128]{1,0:T(8,128)(2,1)} collective-permute-done((bf16[4096,128]{1,0:T(8,128)(2,1)S(1)}, bf16[4096,128]{1,0:T(8,128)(2,1)}, u32[]{:S(2)}, u32[]{:S(2)}) %collective-permute-start.2) | collective-permute-done | bytes 1048608 | tf_op jit(solution)/shard_map/ppermute | solution.py:18
  127.0 31.7 %shard_map.55 = bf16[4096,128]{1,0:T(8,128)(2,1)} custom-call(s32[48]{0:T(128)} %reshape.34.idx_ref, s32[8]{0:T(128)} %dynamic_slice.7.cnt_ref, bf16[4096,128]{1,0:T(8,128)(2,1)} %bitcast.38, bf16[8,4,2,64,128]{4,3,2,1,0:T(8,128)(2,1)} %bitcast.3.refs_0_, bf16[8,4,2,64,128]{4,3,2,1,0:T(8,128)(2,1)} %bitcast.37, bf16[8,4,2,64,128]{4,3,2,1,0:T(8,128)(2,1)} %bitcast.10.refs_2_, ...), custom_call_target="tpu_custom_call" | custom-call | flops 6442450944 | bytes 8388608 | tf_op jit(solution)/shard_map/pallas_call | solution.py:100
  158.6 38.5 %all_to_all.76 = bf16[32,128,128]{2,1,0:T(8,128)(2,1)S(1)} all-to-all(bf16[32,128,128]{2,1,0:T(8,128)(2,1)} %bitcast.39), channel_id=1, replica_groups=mesh['blk'=16,'head'=32] {'head'}, dimensions={0} | all-to-all | bytes 2097152 | tf_op jit(solution)/shard_map/all_to_all | solution.py:138
  197.2 1.1 copy_bitcast_fusion
  (14 shorter events, 1.3 us)
Async XLA Ops:
  0.0 59.0 %copy-start = (bf16[128,4096]{1,0:T(8,128)(2,1)S(1)}, bf16[128,4096]{1,0:T(8,128)(2,1)}, u32[]{:S(2)}) copy-start(bf16[128,4096]{1,0:T(8,128)(2,1)} %param.5) | copy-start | bytes 3145732
  3.9 41.1 %all-to-all-start.1 = ((bf16[128,32,128]{2,0,1:T(8,128)(2,1)}), bf16[128,32,128]{2,0,1:T(8,128)(2,1)}, u32[]{:S(2)}, u32[]{:S(2)}) async-start(bf16[128,32,128]{2,0,1:T(8,128)(2,1)} %copy_bitcast_fusion.1), calls=%async_computation.1 | async-start | bytes 2097152 | tf_op jit(solution)/shard_map/all_to_all | solution.py:113
  45.0 33.1 %all-to-all-start.2 = ((bf16[128,32,128]{2,0,1:T(8,128)(2,1)}), bf16[128,32,128]{2,0,1:T(8,128)(2,1)S(1)}, u32[]{:S(2)}, u32[]{:S(2)}) async-start(bf16[128,32,128]{2,0,1:T(8,128)(2,1)} %copy.20), calls=%async_computation.2 | async-start | bytes 2097152 | tf_op jit(solution)/shard_map/all_to_all | solution.py:113
  49.8 37.2 %collective-permute-start.1 = (bf16[4096,128]{1,0:T(8,128)(2,1)}, bf16[4096,128]{1,0:T(8,128)(2,1)}, u32[]{:S(2)}, u32[]{:S(2)}) collective-permute-start(bf16[4096,128]{1,0:T(8,128)(2,1)} %bitcast.7), channel_id=1, source_target_pairs={{0,480},{32,0},{64,32},{96,64},{128,96},{160,128},{192,160},{224,1... | collective-permute-start | bytes 3145736 | tf_op jit(solution)/shard_map/ppermute | solution.py:18
  57.1 35.6 %collective-permute-start = (bf16[4096,128]{1,0:T(8,128)(2,1)}, bf16[4096,128]{1,0:T(8,128)(2,1)}, u32[]{:S(2)}, u32[]{:S(2)}) collective-permute-start(bf16[4096,128]{1,0:T(8,128)(2,1)} %bitcast.7), channel_id=1, source_target_pairs={{0,32},{32,64},{64,96},{96,128},{128,160},{160,192},{192,224},{224... | collective-permute-start | bytes 3145736 | tf_op jit(solution)/shard_map/ppermute | solution.py:18
  60.3 37.7 %copy-start.4 = (s32[128]{0:T(128)S(1)}, s32[128]{0:T(128)}, u32[]{:S(2)}) copy-start(s32[128]{0:T(128)} %param.9) | copy-start | bytes 1540
  60.3 38.3 %copy-start.3 = (s32[128,6]{0,1:T(8,128)S(1)}, s32[128,6]{0,1:T(8,128)}, u32[]{:S(2)}) copy-start(s32[128,6]{0,1:T(8,128)} %param.8) | copy-start | bytes 9220
  78.1 16.7 %copy-start.1 = (bf16[128,32,128]{2,0,1:T(8,128)(2,1)}, bf16[128,32,128]{2,0,1:T(8,128)(2,1)S(1)}, u32[]{:S(2)}) copy-start(bf16[128,32,128]{2,0,1:T(8,128)(2,1)S(1)} %all-to-all-done.2) | copy-start | bytes 3145732
  78.1 34.2 %all-to-all-start = ((bf16[128,32,128]{2,0,1:T(8,128)(2,1)}), bf16[128,32,128]{2,0,1:T(8,128)(2,1)S(1)}, u32[]{:S(2)}, u32[]{:S(2)}) async-start(bf16[128,32,128]{2,0,1:T(8,128)(2,1)} %copy_bitcast_fusion.2), calls=%async_computation | async-start | bytes 2097152 | tf_op jit(solution)/shard_map/all_to_all | solution.py:113
  92.7 28.0 %collective-permute-start.3 = (bf16[4096,128]{1,0:T(8,128)(2,1)S(1)}, bf16[4096,128]{1,0:T(8,128)(2,1)}, u32[]{:S(2)}, u32[]{:S(2)}) collective-permute-start(bf16[4096,128]{1,0:T(8,128)(2,1)S(1)} %bitcast.35), channel_id=1, source_target_pairs={{0,480},{32,0},{64,32},{96,64},{128,96},{160,128},{192,160},{224,1... | collective-permute-start | bytes 3145736 | tf_op jit(solution)/shard_map/ppermute | solution.py:18
  94.8 32.2 %collective-permute-start.2 = (bf16[4096,128]{1,0:T(8,128)(2,1)S(1)}, bf16[4096,128]{1,0:T(8,128)(2,1)}, u32[]{:S(2)}, u32[]{:S(2)}) collective-permute-start(bf16[4096,128]{1,0:T(8,128)(2,1)S(1)} %bitcast.36), channel_id=1, source_target_pairs={{0,32},{32,64},{64,96},{96,128},{128,160},{160,192},{192,224},{224... | collective-permute-start | bytes 3145736 | tf_op jit(solution)/shard_map/ppermute | solution.py:18
  112.3 14.7 %copy-start.2 = (bf16[128,32,128]{2,0,1:T(8,128)(2,1)}, bf16[128,32,128]{2,0,1:T(8,128)(2,1)S(1)}, u32[]{:S(2)}) copy-start(bf16[128,32,128]{2,0,1:T(8,128)(2,1)S(1)} %all-to-all-done) | copy-start | bytes 3145732

commit v12 on v10

--- a/solution.py
+++ b/solution.py
@@ -10,6 +10,7 @@
 HD = 128
 BLOCK = 512
 MAXB = 6
+MINB = 3
 
 
 def from_behind(value, axis, steps):
@@ -44,7 +45,7 @@
     amount = cnt_ref[b]
     m_scr[...] = jnp.full(m_scr.shape, -jnp.inf, jnp.float32)
     for j in range(MAXB):
-        @pl.when(j < amount)
+        @pl.when(True if j < MINB else j < amount)
         def _scores():
             key_block = k_scr[idx_ref[b * MAXB + j]].reshape(BLOCK, HD)
             scores = lax.dot_general(
@@ -57,7 +58,7 @@
     l_scr[...] = jnp.zeros(l_scr.shape, jnp.float32)
     acc_scr[...] = jnp.zeros(acc_scr.shape, jnp.float32)
     for j in range(MAXB):
-        @pl.when(j < amount)
+        @pl.when(True if j < MINB else j < amount)
         def _mix():
             value_block = v_scr[idx_ref[b * MAXB + j]].reshape(BLOCK, HD)
             expo = jnp.exp(s_scr[j] - m_scr[...])

time: 197 us -> 193 us (0.980)
  Pallas kernels: 29.7 us -> 25.6 us
    pallas_call x1, Pallas kernels: 29.7 us -> 25.6 us  [attend(): pl.pallas_call(attention_kernel, out_shape=jax.ShapeDtypeStruct((rows, wi...]
where the time goes in v12:
time: 193 us; the launch traced here: 192 us
  waiting for transfers between devices  78.6 us (41%)
  starting transfers between devices  38.3 us (20%)
  blocking collectives  37.2 us (19%)
  Pallas kernels  25.6 us (13%)
  local copies, waits for them, and re-layouts  8 us (4%)
  other arithmetic  2.71 us (1%)
    all_to_all x3, waiting for transfers between devices, to_heads(): return lax.all_to_all(x, 'head', split_axis=1, concat_axis=0, tiled=True)  55 us
    all_to_all x1, blocking collectives, local(): lax.all_to_all(attended_rows, 'head', split_axis=0, concat_axis=1, tiled=...  37.2 us
    pallas_call x1, Pallas kernels, attend(): pl.pallas_call(attention_kernel, out_shape=jax.ShapeDtypeStruct((rows, wi...  25.6 us
    all_to_all x3, starting transfers between devices, to_heads(): return lax.all_to_all(x, 'head', split_axis=1, concat_axis=0, tiled=True)  23.7 us
    ppermute x4, waiting for transfers between devices, from_behind(): return lax.ppermute(value, axis, pairs)  23.6 us
    ppermute x4, starting transfers between devices, from_behind(): return lax.ppermute(value, axis, pairs)  14.6 us
  transfers between devices with their start and end apart: 7, of which 7 were waited for; matrix products, arithmetic and copies ran while one was open for 3% of the time, Pallas kernels for 0%

profile of v12, /device:TPU:1, one launch (start us, length us, event | category | flops | bytes accessed | tf_op | source)
XLA Modules:
  0.0 191.9 jit_solution(6876200079506954989)
XLA Ops:
  0.0 1.7 fusion.2
  1.8 1.3 copy_bitcast_fusion.2
  3.0 12.9 %all-to-all-start.1 = ((bf16[128,32,128]{2,0,1:T(8,128)(2,1)}), bf16[128,32,128]{2,0,1:T(8,128)(2,1)S(1)}, u32[]{:S(2)}, u32[]{:S(2)}) async-start(bf16[128,32,128]{2,0,1:T(8,128)(2,1)} %copy_bitcast_fusion.2), calls=%async_computation.1 | async-start | bytes 2097152 | tf_op jit(solution)/shard_map/all_to_all | solution.py:114
  15.9 1.3 copy_bitcast_fusion.1
  17.2 26.8 %all-to-all-done.1 = bf16[128,32,128]{2,0,1:T(8,128)(2,1)S(1)} async-done(((bf16[128,32,128]{2,0,1:T(8,128)(2,1)}), bf16[128,32,128]{2,0,1:T(8,128)(2,1)S(1)}, u32[]{:S(2)}, u32[]{:S(2)}) %all-to-all-start.1) | async-done | bytes 1048608 | tf_op jit(solution)/shard_map/all_to_all | solution.py:114
  44.1 4.8 %all-to-all-start.2 = ((bf16[128,32,128]{2,0,1:T(8,128)(2,1)}), bf16[128,32,128]{2,0,1:T(8,128)(2,1)S(1)}, u32[]{:S(2)}, u32[]{:S(2)}) async-start(bf16[128,32,128]{2,0,1:T(8,128)(2,1)} %copy_bitcast_fusion.1), calls=%async_computation.2 | async-start | bytes 2097152 | tf_op jit(solution)/shard_map/all_to_all | solution.py:114
  48.9 7.3 %collective-permute-start.1 = (bf16[4096,128]{1,0:T(8,128)(2,1)S(1)}, bf16[4096,128]{1,0:T(8,128)(2,1)}, u32[]{:S(2)}, u32[]{:S(2)}) collective-permute-start(bf16[4096,128]{1,0:T(8,128)(2,1)S(1)} %bitcast.43), channel_id=1, source_target_pairs={{0,480},{32,0},{64,32},{96,64},{128,96},{160,128},{192,160},{224,1... | collective-permute-start | bytes 3145736 | tf_op jit(solution)/shard_map/ppermute | solution.py:19
  56.2 1.9 %collective-permute-start = (bf16[4096,128]{1,0:T(8,128)(2,1)S(1)}, bf16[4096,128]{1,0:T(8,128)(2,1)}, u32[]{:S(2)}, u32[]{:S(2)}) collective-permute-start(bf16[4096,128]{1,0:T(8,128)(2,1)S(1)} %bitcast.44), channel_id=1, source_target_pairs={{0,32},{32,64},{64,96},{96,128},{128,160},{160,192},{192,224},{224... | collective-permute-start | bytes 3145736 | tf_op jit(solution)/shard_map/ppermute | solution.py:19
  58.1 1.3 copy_bitcast_fusion.3
  59.4 17.8 %all-to-all-done.2 = bf16[128,32,128]{2,0,1:T(8,128)(2,1)S(1)} async-done(((bf16[128,32,128]{2,0,1:T(8,128)(2,1)}), bf16[128,32,128]{2,0,1:T(8,128)(2,1)S(1)}, u32[]{:S(2)}, u32[]{:S(2)}) %all-to-all-start.2) | async-done | bytes 1048608 | tf_op jit(solution)/shard_map/all_to_all | solution.py:114
  77.2 6.0 %all-to-all-start = ((bf16[128,32,128]{2,0,1:T(8,128)(2,1)}), bf16[128,32,128]{2,0,1:T(8,128)(2,1)}, u32[]{:S(2)}, u32[]{:S(2)}) async-start(bf16[128,32,128]{2,0,1:T(8,128)(2,1)} %copy_bitcast_fusion.3), calls=%async_computation | async-start | bytes 2097152 | tf_op jit(solution)/shard_map/all_to_all | solution.py:114
  83.2 2.7 %collective-permute-done.1 = bf16[4096,128]{1,0:T(8,128)(2,1)} collective-permute-done((bf16[4096,128]{1,0:T(8,128)(2,1)S(1)}, bf16[4096,128]{1,0:T(8,128)(2,1)}, u32[]{:S(2)}, u32[]{:S(2)}) %collective-permute-start.1) | collective-permute-done | bytes 1048608 | tf_op jit(solution)/shard_map/ppermute | solution.py:19
  85.9 1.3 slice.25
  87.1 4.3 %collective-permute-done = bf16[4096,128]{1,0:T(8,128)(2,1)} collective-permute-done((bf16[4096,128]{1,0:T(8,128)(2,1)S(1)}, bf16[4096,128]{1,0:T(8,128)(2,1)}, u32[]{:S(2)}, u32[]{:S(2)}) %collective-permute-start) | collective-permute-done | bytes 1048608 | tf_op jit(solution)/shard_map/ppermute | solution.py:19
  91.5 1.2 slice.24
  94.0 3.5 %collective-permute-start.3 = (bf16[4096,128]{1,0:T(8,128)(2,1)S(1)}, bf16[4096,128]{1,0:T(8,128)(2,1)}, u32[]{:S(2)}, u32[]{:S(2)}) collective-permute-start(bf16[4096,128]{1,0:T(8,128)(2,1)S(1)} %bitcast.40), channel_id=1, source_target_pairs={{0,480},{32,0},{64,32},{96,64},{128,96},{160,128},{192,160},{224,1... | collective-permute-start | bytes 3145736 | tf_op jit(solution)/shard_map/ppermute | solution.py:19
  97.6 1.9 %collective-permute-start.2 = (bf16[4096,128]{1,0:T(8,128)(2,1)S(1)}, bf16[4096,128]{1,0:T(8,128)(2,1)}, u32[]{:S(2)}, u32[]{:S(2)}) collective-permute-start(bf16[4096,128]{1,0:T(8,128)(2,1)S(1)} %bitcast.41), channel_id=1, source_target_pairs={{0,32},{32,64},{64,96},{96,128},{128,160},{160,192},{192,224},{224... | collective-permute-start | bytes 3145736 | tf_op jit(solution)/shard_map/ppermute | solution.py:19
  100.3 0.7 reshape.40.idx_ref
  101.0 10.4 %all-to-all-done = bf16[128,32,128]{2,0,1:T(8,128)(2,1)} async-done(((bf16[128,32,128]{2,0,1:T(8,128)(2,1)}), bf16[128,32,128]{2,0,1:T(8,128)(2,1)}, u32[]{:S(2)}, u32[]{:S(2)}) %all-to-all-start) | async-done | bytes 1048608 | tf_op jit(solution)/shard_map/all_to_all | solution.py:114
  111.4 11.3 %collective-permute-done.3 = bf16[4096,128]{1,0:T(8,128)(2,1)} collective-permute-done((bf16[4096,128]{1,0:T(8,128)(2,1)S(1)}, bf16[4096,128]{1,0:T(8,128)(2,1)}, u32[]{:S(2)}, u32[]{:S(2)}) %collective-permute-start.3) | collective-permute-done | bytes 1048608 | tf_op jit(solution)/shard_map/ppermute | solution.py:19
  122.7 5.2 %collective-permute-done.2 = bf16[4096,128]{1,0:T(8,128)(2,1)} collective-permute-done((bf16[4096,128]{1,0:T(8,128)(2,1)S(1)}, bf16[4096,128]{1,0:T(8,128)(2,1)}, u32[]{:S(2)}, u32[]{:S(2)}) %collective-permute-start.2) | collective-permute-done | bytes 1048608 | tf_op jit(solution)/shard_map/ppermute | solution.py:19
  127.9 25.6 %shard_map.55 = bf16[4096,128]{1,0:T(8,128)(2,1)} custom-call(s32[48]{0:T(128)} %reshape.40.idx_ref, s32[8]{0:T(128)} %dynamic_slice.7.cnt_ref, bf16[4096,128]{1,0:T(8,128)(2,1)} %bitcast.1.q_ref, bf16[8,4,2,64,128]{4,3,2,1,0:T(8,128)(2,1)} %bitcast.45, bf16[8,4,2,64,128]{4,3,2,1,0:T(8,128)(2,1)} %bitcast.42, bf16[8,4,2,64,128]{4,3,2,1,0:T(8,128)(2,1)} %bitcast.9.refs_2_, ...), custom_call_target="tpu_custom_call" | custom-call | flops 6442450944 | bytes 8388608 | tf_op jit(solution)/shard_map/pallas_call | solution.py:101
  153.6 37.2 %all_to_all.70 = bf16[32,128,128]{2,1,0:T(8,128)(2,1)S(1)} all-to-all(bf16[32,128,128]{2,1,0:T(8,128)(2,1)} %bitcast.46), channel_id=1, replica_groups=mesh['blk'=16,'head'=32] {'head'}, dimensions={0} | all-to-all | bytes 2097152 | tf_op jit(solution)/shard_map/all_to_all | solution.py:139
  190.8 1.1 copy_bitcast_fusion
  (14 shorter events, 0.9 us)
Async XLA Ops:
  0.0 58.1 %copy-start = (bf16[128,4096]{1,0:T(8,128)(2,1)S(1)}, bf16[128,4096]{1,0:T(8,128)(2,1)}, u32[]{:S(2)}) copy-start(bf16[128,4096]{1,0:T(8,128)(2,1)} %param.5) | copy-start | bytes 3145732
  3.0 41.1 %all-to-all-start.1 = ((bf16[128,32,128]{2,0,1:T(8,128)(2,1)}), bf16[128,32,128]{2,0,1:T(8,128)(2,1)S(1)}, u32[]{:S(2)}, u32[]{:S(2)}) async-start(bf16[128,32,128]{2,0,1:T(8,128)(2,1)} %copy_bitcast_fusion.2), calls=%async_computation.1 | async-start | bytes 2097152 | tf_op jit(solution)/shard_map/all_to_all | solution.py:114
  44.1 12.1 %copy-start.2 = (bf16[128,32,128]{2,0,1:T(8,128)(2,1)}, bf16[128,32,128]{2,0,1:T(8,128)(2,1)S(1)}, u32[]{:S(2)}) copy-start(bf16[128,32,128]{2,0,1:T(8,128)(2,1)S(1)} %all-to-all-done.1) | copy-start | bytes 3145732
  44.1 33.1 %all-to-all-start.2 = ((bf16[128,32,128]{2,0,1:T(8,128)(2,1)}), bf16[128,32,128]{2,0,1:T(8,128)(2,1)S(1)}, u32[]{:S(2)}, u32[]{:S(2)}) async-start(bf16[128,32,128]{2,0,1:T(8,128)(2,1)} %copy_bitcast_fusion.1), calls=%async_computation.2 | async-start | bytes 2097152 | tf_op jit(solution)/shard_map/all_to_all | solution.py:114
  48.9 37.0 %collective-permute-start.1 = (bf16[4096,128]{1,0:T(8,128)(2,1)S(1)}, bf16[4096,128]{1,0:T(8,128)(2,1)}, u32[]{:S(2)}, u32[]{:S(2)}) collective-permute-start(bf16[4096,128]{1,0:T(8,128)(2,1)S(1)} %bitcast.43), channel_id=1, source_target_pairs={{0,480},{32,0},{64,32},{96,64},{128,96},{160,128},{192,160},{224,1... | collective-permute-start | bytes 3145736 | tf_op jit(solution)/shard_map/ppermute | solution.py:19
  56.2 35.3 %collective-permute-start = (bf16[4096,128]{1,0:T(8,128)(2,1)S(1)}, bf16[4096,128]{1,0:T(8,128)(2,1)}, u32[]{:S(2)}, u32[]{:S(2)}) collective-permute-start(bf16[4096,128]{1,0:T(8,128)(2,1)S(1)} %bitcast.44), channel_id=1, source_target_pairs={{0,32},{32,64},{64,96},{96,128},{128,160},{160,192},{192,224},{224... | collective-permute-start | bytes 3145736 | tf_op jit(solution)/shard_map/ppermute | solution.py:19
  77.2 34.2 %all-to-all-start = ((bf16[128,32,128]{2,0,1:T(8,128)(2,1)}), bf16[128,32,128]{2,0,1:T(8,128)(2,1)}, u32[]{:S(2)}, u32[]{:S(2)}) async-start(bf16[128,32,128]{2,0,1:T(8,128)(2,1)} %copy_bitcast_fusion.3), calls=%async_computation | async-start | bytes 2097152 | tf_op jit(solution)/shard_map/all_to_all | solution.py:114
  93.9 5.6 %copy-start.4 = (s32[128]{0:T(128)S(1)}, s32[128]{0:T(128)}, u32[]{:S(2)}) copy-start(s32[128]{0:T(128)} %param.9) | copy-start | bytes 1540
  93.9 6.2 %copy-start.3 = (s32[128,6]{0,1:T(8,128)S(1)}, s32[128,6]{0,1:T(8,128)}, u32[]{:S(2)}) copy-start(s32[128,6]{0,1:T(8,128)} %param.8) | copy-start | bytes 9220
  94.0 33.9 %copy-start.1 = (bf16[128,32,128]{2,0,1:T(8,128)(2,1)}, bf16[128,32,128]{2,0,1:T(8,128)(2,1)S(1)}, u32[]{:S(2)}) copy-start(bf16[128,32,128]{2,0,1:T(8,128)(2,1)S(1)} %broadcast_add_fusion) | copy-start | bytes 3145732
  94.0 28.6 %collective-permute-start.3 = (bf16[4096,128]{1,0:T(8,128)(2,1)S(1)}, bf16[4096,128]{1,0:T(8,128)(2,1)}, u32[]{:S(2)}, u32[]{:S(2)}) collective-permute-start(bf16[4096,128]{1,0:T(8,128)(2,1)S(1)} %bitcast.40), channel_id=1, source_target_pairs={{0,480},{32,0},{64,32},{96,64},{128,96},{160,128},{192,160},{224,1... | collective-permute-start | bytes 3145736 | tf_op jit(solution)/shard_map/ppermute | solution.py:19
  97.6 30.4 %collective-permute-start.2 = (bf16[4096,128]{1,0:T(8,128)(2,1)S(1)}, bf16[4096,128]{1,0:T(8,128)(2,1)}, u32[]{:S(2)}, u32[]{:S(2)}) collective-permute-start(bf16[4096,128]{1,0:T(8,128)(2,1)S(1)} %bitcast.41), channel_id=1, source_target_pairs={{0,32},{32,64},{64,96},{96,128},{128,160},{160,192},{192,224},{224... | collective-permute-start | bytes 3145736 | tf_op jit(solution)/shard_map/ppermute | solution.py:19

commit v13 on v12

--- a/solution.py
+++ b/solution.py
@@ -43,30 +43,35 @@
 
     scale = HD ** (-0.5)
     amount = cnt_ref[b]
-    m_scr[...] = jnp.full(m_scr.shape, -jnp.inf, jnp.float32)
-    for j in range(MAXB):
-        @pl.when(True if j < MINB else j < amount)
-        def _scores():
-            key_block = k_scr[idx_ref[b * MAXB + j]].reshape(BLOCK, HD)
-            scores = lax.dot_general(
-                key_block, q_ref[...], (((1,), (1,)), ((), ())),
-                preferred_element_type=jnp.float32,
-            ) * scale
-            s_scr[j] = scores
-            m_scr[...] = jnp.maximum(m_scr[...], jnp.max(scores, axis=0, keepdims=True))
+    amount = jnp.clip(amount, MINB, MAXB)
+    for used in range(MINB, MAXB + 1):
+        @pl.when(amount == used)
+        def _attend():
+            m_scr[...] = jnp.full(m_scr.shape, -jnp.inf, jnp.float32)
+            for j in range(used):
+                @pl.when(True)
+                def _scores():
+                    key_block = k_scr[idx_ref[b * MAXB + j]].reshape(BLOCK, HD)
+                    scores = lax.dot_general(
+                        key_block, q_ref[...], (((1,), (1,)), ((), ())),
+                        preferred_element_type=jnp.float32,
+                    ) * scale
+                    s_scr[j] = scores
+                    m_scr[...] = jnp.maximum(m_scr[...], jnp.max(scores, axis=0, keepdims=True))
 
-    l_scr[...] = jnp.zeros(l_scr.shape, jnp.float32)
-    acc_scr[...] = jnp.zeros(acc_scr.shape, jnp.float32)
-    for j in range(MAXB):
-        @pl.when(True if j < MINB else j < amount)
-        def _mix():
-            value_block = v_scr[idx_ref[b * MAXB + j]].reshape(BLOCK, HD)
-            expo = jnp.exp(s_scr[j] - m_scr[...])
-            l_scr[...] += jnp.sum(expo, axis=0, keepdims=True)
-            acc_scr[...] += lax.dot_general(
-                value_block, expo.astype(jnp.bfloat16), (((0,), (0,)), ((), ())),
-                preferred_element_type=jnp.float32,
-            )
+            l_scr[...] = jnp.zeros(l_scr.shape, jnp.float32)
+            acc_scr[...] = jnp.zeros(acc_scr.shape, jnp.float32)
+            for j in range(used):
+                @pl.when(True)
+                def _mix():
+                    value_block = v_scr[idx_ref[b * MAXB + j]].reshape(BLOCK, HD)
+                    expo = jnp.exp(s_scr[j] - m_scr[...])
+                    l_scr[...] += jnp.sum(expo, axis=0, keepdims=True)
+                    acc_scr[...] += lax.dot_general(
+                        value_block, expo.astype(jnp.bfloat16), (((0,), (0,)), ((), ())),
+                        preferred_element_type=jnp.float32,
+                    )
+
 
     o_ref[...] = jnp.transpose(acc_scr[...] / l_scr[...]).astype(o_ref.dtype)
 

time: 193 us -> 187 us (0.969)
  Pallas kernels: 25.6 us -> 20.5 us
    pallas_call x1, Pallas kernels: 25.6 us -> 20.5 us  [attend(): pl.pallas_call(attention_kernel, out_shape=jax.ShapeDtypeStruct((rows, wi...]
  transfers between devices with their start and end apart: 7 -> 7, of which waited for: 7 -> 7; matrix products, arithmetic and copies ran while one was open for 3% -> 4% of each run, Pallas kernels for 0% -> 0%
where the time goes in v13:
time: 187 us
  waiting for transfers between devices  78.6 us (42%)
  starting transfers between devices  38.3 us (20%)
  blocking collectives  37.2 us (20%)
  Pallas kernels  20.5 us (11%)
  local copies, waits for them, and re-layouts  8 us (4%)
  other arithmetic  2.71 us (1%)
    all_to_all x3, waiting for transfers between devices, to_heads(): return lax.all_to_all(x, 'head', split_axis=1, concat_axis=0, tiled=True)  55 us
    all_to_all x1, blocking collectives, local(): lax.all_to_all(attended_rows, 'head', split_axis=0, concat_axis=1, tiled=...  37.2 us
    all_to_all x3, starting transfers between devices, to_heads(): return lax.all_to_all(x, 'head', split_axis=1, concat_axis=0, tiled=True)  23.7 us
    ppermute x4, waiting for transfers between devices, from_behind(): return lax.ppermute(value, axis, pairs)  23.6 us
    pallas_call x1, Pallas kernels, attend(): pl.pallas_call(attention_kernel, out_shape=jax.ShapeDtypeStruct((rows, wi...  20.5 us
    ppermute x4, starting transfers between devices, from_behind(): return lax.ppermute(value, axis, pairs)  14.6 us
  transfers between devices with their start and end apart: 7, of which 7 were waited for; matrix products, arithmetic and copies ran while one was open for 4% of the time, Pallas kernels for 0%

profile of v13, /device:TPU:1, one launch (start us, length us, event | category | flops | bytes accessed | tf_op | source)
XLA Modules:
  0.0 186.7 jit_solution(6726168905865004449)
XLA Ops:
  0.0 1.7 fusion.2
  1.8 1.3 copy_bitcast_fusion.2
  3.0 12.9 %all-to-all-start.1 = ((bf16[128,32,128]{2,0,1:T(8,128)(2,1)}), bf16[128,32,128]{2,0,1:T(8,128)(2,1)S(1)}, u32[]{:S(2)}, u32[]{:S(2)}) async-start(bf16[128,32,128]{2,0,1:T(8,128)(2,1)} %copy_bitcast_fusion.2), calls=%async_computation.1 | async-start | bytes 2097152 | tf_op jit(solution)/shard_map/all_to_all | solution.py:119
  15.9 1.3 copy_bitcast_fusion.1
  17.2 26.8 %all-to-all-done.1 = bf16[128,32,128]{2,0,1:T(8,128)(2,1)S(1)} async-done(((bf16[128,32,128]{2,0,1:T(8,128)(2,1)}), bf16[128,32,128]{2,0,1:T(8,128)(2,1)S(1)}, u32[]{:S(2)}, u32[]{:S(2)}) %all-to-all-start.1) | async-done | bytes 1048608 | tf_op jit(solution)/shard_map/all_to_all | solution.py:119
  44.1 4.8 %all-to-all-start.2 = ((bf16[128,32,128]{2,0,1:T(8,128)(2,1)}), bf16[128,32,128]{2,0,1:T(8,128)(2,1)S(1)}, u32[]{:S(2)}, u32[]{:S(2)}) async-start(bf16[128,32,128]{2,0,1:T(8,128)(2,1)} %copy_bitcast_fusion.1), calls=%async_computation.2 | async-start | bytes 2097152 | tf_op jit(solution)/shard_map/all_to_all | solution.py:119
  48.9 7.3 %collective-permute-start.1 = (bf16[4096,128]{1,0:T(8,128)(2,1)S(1)}, bf16[4096,128]{1,0:T(8,128)(2,1)}, u32[]{:S(2)}, u32[]{:S(2)}) collective-permute-start(bf16[4096,128]{1,0:T(8,128)(2,1)S(1)} %bitcast.43), channel_id=1, source_target_pairs={{0,480},{32,0},{64,32},{96,64},{128,96},{160,128},{192,160},{224,1... | collective-permute-start | bytes 3145736 | tf_op jit(solution)/shard_map/ppermute | solution.py:19
  56.2 1.9 %collective-permute-start = (bf16[4096,128]{1,0:T(8,128)(2,1)S(1)}, bf16[4096,128]{1,0:T(8,128)(2,1)}, u32[]{:S(2)}, u32[]{:S(2)}) collective-permute-start(bf16[4096,128]{1,0:T(8,128)(2,1)S(1)} %bitcast.44), channel_id=1, source_target_pairs={{0,32},{32,64},{64,96},{96,128},{128,160},{160,192},{192,224},{224... | collective-permute-start | bytes 3145736 | tf_op jit(solution)/shard_map/ppermute | solution.py:19
  58.1 1.3 copy_bitcast_fusion.3
  59.4 17.8 %all-to-all-done.2 = bf16[128,32,128]{2,0,1:T(8,128)(2,1)S(1)} async-done(((bf16[128,32,128]{2,0,1:T(8,128)(2,1)}), bf16[128,32,128]{2,0,1:T(8,128)(2,1)S(1)}, u32[]{:S(2)}, u32[]{:S(2)}) %all-to-all-start.2) | async-done | bytes 1048608 | tf_op jit(solution)/shard_map/all_to_all | solution.py:119
  77.2 6.0 %all-to-all-start = ((bf16[128,32,128]{2,0,1:T(8,128)(2,1)}), bf16[128,32,128]{2,0,1:T(8,128)(2,1)}, u32[]{:S(2)}, u32[]{:S(2)}) async-start(bf16[128,32,128]{2,0,1:T(8,128)(2,1)} %copy_bitcast_fusion.3), calls=%async_computation | async-start | bytes 2097152 | tf_op jit(solution)/shard_map/all_to_all | solution.py:119
  83.2 2.7 %collective-permute-done.1 = bf16[4096,128]{1,0:T(8,128)(2,1)} collective-permute-done((bf16[4096,128]{1,0:T(8,128)(2,1)S(1)}, bf16[4096,128]{1,0:T(8,128)(2,1)}, u32[]{:S(2)}, u32[]{:S(2)}) %collective-permute-start.1) | collective-permute-done | bytes 1048608 | tf_op jit(solution)/shard_map/ppermute | solution.py:19
  85.9 1.3 slice.25
  87.1 4.3 %collective-permute-done = bf16[4096,128]{1,0:T(8,128)(2,1)} collective-permute-done((bf16[4096,128]{1,0:T(8,128)(2,1)S(1)}, bf16[4096,128]{1,0:T(8,128)(2,1)}, u32[]{:S(2)}, u32[]{:S(2)}) %collective-permute-start) | collective-permute-done | bytes 1048608 | tf_op jit(solution)/shard_map/ppermute | solution.py:19
  91.5 1.2 slice.24
  94.0 3.5 %collective-permute-start.3 = (bf16[4096,128]{1,0:T(8,128)(2,1)S(1)}, bf16[4096,128]{1,0:T(8,128)(2,1)}, u32[]{:S(2)}, u32[]{:S(2)}) collective-permute-start(bf16[4096,128]{1,0:T(8,128)(2,1)S(1)} %bitcast.40), channel_id=1, source_target_pairs={{0,480},{32,0},{64,32},{96,64},{128,96},{160,128},{192,160},{224,1... | collective-permute-start | bytes 3145736 | tf_op jit(solution)/shard_map/ppermute | solution.py:19
  97.6 1.9 %collective-permute-start.2 = (bf16[4096,128]{1,0:T(8,128)(2,1)S(1)}, bf16[4096,128]{1,0:T(8,128)(2,1)}, u32[]{:S(2)}, u32[]{:S(2)}) collective-permute-start(bf16[4096,128]{1,0:T(8,128)(2,1)S(1)} %bitcast.41), channel_id=1, source_target_pairs={{0,32},{32,64},{64,96},{96,128},{128,160},{160,192},{192,224},{224... | collective-permute-start | bytes 3145736 | tf_op jit(solution)/shard_map/ppermute | solution.py:19
  100.3 0.7 reshape.40.idx_ref
  101.0 10.4 %all-to-all-done = bf16[128,32,128]{2,0,1:T(8,128)(2,1)} async-done(((bf16[128,32,128]{2,0,1:T(8,128)(2,1)}), bf16[128,32,128]{2,0,1:T(8,128)(2,1)}, u32[]{:S(2)}, u32[]{:S(2)}) %all-to-all-start) | async-done | bytes 1048608 | tf_op jit(solution)/shard_map/all_to_all | solution.py:119
  111.4 11.3 %collective-permute-done.3 = bf16[4096,128]{1,0:T(8,128)(2,1)} collective-permute-done((bf16[4096,128]{1,0:T(8,128)(2,1)S(1)}, bf16[4096,128]{1,0:T(8,128)(2,1)}, u32[]{:S(2)}, u32[]{:S(2)}) %collective-permute-start.3) | collective-permute-done | bytes 1048608 | tf_op jit(solution)/shard_map/ppermute | solution.py:19
  122.7 5.2 %collective-permute-done.2 = bf16[4096,128]{1,0:T(8,128)(2,1)} collective-permute-done((bf16[4096,128]{1,0:T(8,128)(2,1)S(1)}, bf16[4096,128]{1,0:T(8,128)(2,1)}, u32[]{:S(2)}, u32[]{:S(2)}) %collective-permute-start.2) | collective-permute-done | bytes 1048608 | tf_op jit(solution)/shard_map/ppermute | solution.py:19
  127.9 20.5 %shard_map.55 = bf16[4096,128]{1,0:T(8,128)(2,1)} custom-call(s32[48]{0:T(128)} %reshape.40.idx_ref, s32[8]{0:T(128)} %dynamic_slice.7.cnt_ref, bf16[4096,128]{1,0:T(8,128)(2,1)} %bitcast.1.q_ref, bf16[8,4,2,64,128]{4,3,2,1,0:T(8,128)(2,1)} %bitcast.45, bf16[8,4,2,64,128]{4,3,2,1,0:T(8,128)(2,1)} %bitcast.42, bf16[8,4,2,64,128]{4,3,2,1,0:T(8,128)(2,1)} %bitcast.9.refs_2_, ...), custom_call_target="tpu_custom_call" | custom-call | flops 6442450944 | bytes 8388608 | tf_op jit(solution)/shard_map/pallas_call | solution.py:106
  148.4 37.2 %all_to_all.70 = bf16[32,128,128]{2,1,0:T(8,128)(2,1)S(1)} all-to-all(bf16[32,128,128]{2,1,0:T(8,128)(2,1)} %bitcast.46), channel_id=1, replica_groups=mesh['blk'=16,'head'=32] {'head'}, dimensions={0} | all-to-all | bytes 2097152 | tf_op jit(solution)/shard_map/all_to_all | solution.py:144
  185.6 1.1 copy_bitcast_fusion
  (14 shorter events, 0.9 us)
Async XLA Ops:
  0.0 58.1 %copy-start = (bf16[128,4096]{1,0:T(8,128)(2,1)S(1)}, bf16[128,4096]{1,0:T(8,128)(2,1)}, u32[]{:S(2)}) copy-start(bf16[128,4096]{1,0:T(8,128)(2,1)} %param.5) | copy-start | bytes 3145732
  3.0 41.1 %all-to-all-start.1 = ((bf16[128,32,128]{2,0,1:T(8,128)(2,1)}), bf16[128,32,128]{2,0,1:T(8,128)(2,1)S(1)}, u32[]{:S(2)}, u32[]{:S(2)}) async-start(bf16[128,32,128]{2,0,1:T(8,128)(2,1)} %copy_bitcast_fusion.2), calls=%async_computation.1 | async-start | bytes 2097152 | tf_op jit(solution)/shard_map/all_to_all | solution.py:119
  44.1 12.1 %copy-start.2 = (bf16[128,32,128]{2,0,1:T(8,128)(2,1)}, bf16[128,32,128]{2,0,1:T(8,128)(2,1)S(1)}, u32[]{:S(2)}) copy-start(bf16[128,32,128]{2,0,1:T(8,128)(2,1)S(1)} %all-to-all-done.1) | copy-start | bytes 3145732
  44.1 33.1 %all-to-all-start.2 = ((bf16[128,32,128]{2,0,1:T(8,128)(2,1)}), bf16[128,32,128]{2,0,1:T(8,128)(2,1)S(1)}, u32[]{:S(2)}, u32[]{:S(2)}) async-start(bf16[128,32,128]{2,0,1:T(8,128)(2,1)} %copy_bitcast_fusion.1), calls=%async_computation.2 | async-start | bytes 2097152 | tf_op jit(solution)/shard_map/all_to_all | solution.py:119
  48.9 37.0 %collective-permute-start.1 = (bf16[4096,128]{1,0:T(8,128)(2,1)S(1)}, bf16[4096,128]{1,0:T(8,128)(2,1)}, u32[]{:S(2)}, u32[]{:S(2)}) collective-permute-start(bf16[4096,128]{1,0:T(8,128)(2,1)S(1)} %bitcast.43), channel_id=1, source_target_pairs={{0,480},{32,0},{64,32},{96,64},{128,96},{160,128},{192,160},{224,1... | collective-permute-start | bytes 3145736 | tf_op jit(solution)/shard_map/ppermute | solution.py:19
  56.2 35.3 %collective-permute-start = (bf16[4096,128]{1,0:T(8,128)(2,1)S(1)}, bf16[4096,128]{1,0:T(8,128)(2,1)}, u32[]{:S(2)}, u32[]{:S(2)}) collective-permute-start(bf16[4096,128]{1,0:T(8,128)(2,1)S(1)} %bitcast.44), channel_id=1, source_target_pairs={{0,32},{32,64},{64,96},{96,128},{128,160},{160,192},{192,224},{224... | collective-permute-start | bytes 3145736 | tf_op jit(solution)/shard_map/ppermute | solution.py:19
  77.2 34.2 %all-to-all-start = ((bf16[128,32,128]{2,0,1:T(8,128)(2,1)}), bf16[128,32,128]{2,0,1:T(8,128)(2,1)}, u32[]{:S(2)}, u32[]{:S(2)}) async-start(bf16[128,32,128]{2,0,1:T(8,128)(2,1)} %copy_bitcast_fusion.3), calls=%async_computation | async-start | bytes 2097152 | tf_op jit(solution)/shard_map/all_to_all | solution.py:119
  93.9 5.6 %copy-start.4 = (s32[128]{0:T(128)S(1)}, s32[128]{0:T(128)}, u32[]{:S(2)}) copy-start(s32[128]{0:T(128)} %param.9) | copy-start | bytes 1540
  93.9 6.2 %copy-start.3 = (s32[128,6]{0,1:T(8,128)S(1)}, s32[128,6]{0,1:T(8,128)}, u32[]{:S(2)}) copy-start(s32[128,6]{0,1:T(8,128)} %param.8) | copy-start | bytes 9220
  94.0 33.9 %copy-start.1 = (bf16[128,32,128]{2,0,1:T(8,128)(2,1)}, bf16[128,32,128]{2,0,1:T(8,128)(2,1)S(1)}, u32[]{:S(2)}) copy-start(bf16[128,32,128]{2,0,1:T(8,128)(2,1)S(1)} %broadcast_add_fusion) | copy-start | bytes 3145732
  94.0 28.6 %collective-permute-start.3 = (bf16[4096,128]{1,0:T(8,128)(2,1)S(1)}, bf16[4096,128]{1,0:T(8,128)(2,1)}, u32[]{:S(2)}, u32[]{:S(2)}) collective-permute-start(bf16[4096,128]{1,0:T(8,128)(2,1)S(1)} %bitcast.40), channel_id=1, source_target_pairs={{0,480},{32,0},{64,32},{96,64},{128,96},{160,128},{192,160},{224,1... | collective-permute-start | bytes 3145736 | tf_op jit(solution)/shard_map/ppermute | solution.py:19
  97.6 30.4 %collective-permute-start.2 = (bf16[4096,128]{1,0:T(8,128)(2,1)S(1)}, bf16[4096,128]{1,0:T(8,128)(2,1)}, u32[]{:S(2)}, u32[]{:S(2)}) collective-permute-start(bf16[4096,128]{1,0:T(8,128)(2,1)S(1)} %bitcast.41), channel_id=1, source_target_pairs={{0,32},{32,64},{64,96},{96,128},{128,160},{160,192},{192,224},{224... | collective-permute-start | bytes 3145736 | tf_op jit(solution)/shard_map/ppermute | solution.py:19

commit v14 on v13

--- a/solution.py
+++ b/solution.py
@@ -47,33 +47,26 @@
     for used in range(MINB, MAXB + 1):
         @pl.when(amount == used)
         def _attend():
-            m_scr[...] = jnp.full(m_scr.shape, -jnp.inf, jnp.float32)
+            top = jnp.full(m_scr.shape, -jnp.inf, jnp.float32)
             for j in range(used):
-                @pl.when(True)
-                def _scores():
-                    key_block = k_scr[idx_ref[b * MAXB + j]].reshape(BLOCK, HD)
-                    scores = lax.dot_general(
-                        key_block, q_ref[...], (((1,), (1,)), ((), ())),
-                        preferred_element_type=jnp.float32,
-                    ) * scale
-                    s_scr[j] = scores
-                    m_scr[...] = jnp.maximum(m_scr[...], jnp.max(scores, axis=0, keepdims=True))
-
-            l_scr[...] = jnp.zeros(l_scr.shape, jnp.float32)
-            acc_scr[...] = jnp.zeros(acc_scr.shape, jnp.float32)
+                key_block = k_scr[idx_ref[b * MAXB + j]].reshape(BLOCK, HD)
+                scores = lax.dot_general(
+                    key_block, q_ref[...], (((1,), (1,)), ((), ())),
+                    preferred_element_type=jnp.float32,
+                ) * scale
+                s_scr[j] = scores
+                top = jnp.maximum(top, jnp.max(scores, axis=0, keepdims=True))
+            total = jnp.zeros(l_scr.shape, jnp.float32)
+            mixed = jnp.zeros(acc_scr.shape, jnp.float32)
             for j in range(used):
-                @pl.when(True)
-                def _mix():
-                    value_block = v_scr[idx_ref[b * MAXB + j]].reshape(BLOCK, HD)
-                    expo = jnp.exp(s_scr[j] - m_scr[...])
-                    l_scr[...] += jnp.sum(expo, axis=0, keepdims=True)
-                    acc_scr[...] += lax.dot_general(
-                        value_block, expo.astype(jnp.bfloat16), (((0,), (0,)), ((), ())),
-                        preferred_element_type=jnp.float32,
-                    )
-
-
-    o_ref[...] = jnp.transpose(acc_scr[...] / l_scr[...]).astype(o_ref.dtype)
+                value_block = v_scr[idx_ref[b * MAXB + j]].reshape(BLOCK, HD)
+                expo = jnp.exp(s_scr[j] - top)
+                total = total + jnp.sum(expo, axis=0, keepdims=True)
+                mixed = mixed + lax.dot_general(
+                    value_block, expo.astype(jnp.bfloat16), (((0,), (0,)), ((), ())),
+                    preferred_element_type=jnp.float32,
+                )
+            o_ref[...] = jnp.transpose(mixed / total).astype(o_ref.dtype)
 
 
 def attend(query_rows, kv_parts, local_index, count_rows):

time: 187 us -> 187 us (level)
  no operation moved by 1% of the time
where the time goes in v14:
time: 187 us; the launch traced here: 186 us
  waiting for transfers between devices  78.6 us (42%)
  starting transfers between devices  38.3 us (20%)
  blocking collectives  37.2 us (20%)
  Pallas kernels  19.5 us (10%)
  local copies, waits for them, and re-layouts  8 us (4%)
  other arithmetic  2.71 us (1%)
    all_to_all x3, waiting for transfers between devices, to_heads(): return lax.all_to_all(x, 'head', split_axis=1, concat_axis=0, tiled=True)  55 us
    all_to_all x1, blocking collectives, local(): lax.all_to_all(attended_rows, 'head', split_axis=0, concat_axis=1, tiled=...  37.2 us
    all_to_all x3, starting transfers between devices, to_heads(): return lax.all_to_all(x, 'head', split_axis=1, concat_axis=0, tiled=True)  23.7 us
    ppermute x4, waiting for transfers between devices, from_behind(): return lax.ppermute(value, axis, pairs)  23.6 us
    pallas_call x1, Pallas kernels, attend(): pl.pallas_call(attention_kernel, out_shape=jax.ShapeDtypeStruct((rows, wi...  19.5 us
    ppermute x4, starting transfers between devices, from_behind(): return lax.ppermute(value, axis, pairs)  14.6 us
  transfers between devices with their start and end apart: 7, of which 7 were waited for; matrix products, arithmetic and copies ran while one was open for 4% of the time, Pallas kernels for 0%

profile of v14, /device:TPU:1, one launch (start us, length us, event | category | flops | bytes accessed | tf_op | source)
XLA Modules:
  0.0 185.7 jit_solution(16657641871224781793)
XLA Ops:
  0.0 1.7 fusion.2
  1.8 1.3 copy_bitcast_fusion.2
  3.0 12.9 %all-to-all-start.1 = ((bf16[128,32,128]{2,0,1:T(8,128)(2,1)}), bf16[128,32,128]{2,0,1:T(8,128)(2,1)S(1)}, u32[]{:S(2)}, u32[]{:S(2)}) async-start(bf16[128,32,128]{2,0,1:T(8,128)(2,1)} %copy_bitcast_fusion.2), calls=%async_computation.1 | async-start | bytes 2097152 | tf_op jit(solution)/shard_map/all_to_all | solution.py:112
  15.9 1.3 copy_bitcast_fusion.1
  17.2 26.8 %all-to-all-done.1 = bf16[128,32,128]{2,0,1:T(8,128)(2,1)S(1)} async-done(((bf16[128,32,128]{2,0,1:T(8,128)(2,1)}), bf16[128,32,128]{2,0,1:T(8,128)(2,1)S(1)}, u32[]{:S(2)}, u32[]{:S(2)}) %all-to-all-start.1) | async-done | bytes 1048608 | tf_op jit(solution)/shard_map/all_to_all | solution.py:112
  44.1 4.8 %all-to-all-start.2 = ((bf16[128,32,128]{2,0,1:T(8,128)(2,1)}), bf16[128,32,128]{2,0,1:T(8,128)(2,1)S(1)}, u32[]{:S(2)}, u32[]{:S(2)}) async-start(bf16[128,32,128]{2,0,1:T(8,128)(2,1)} %copy_bitcast_fusion.1), calls=%async_computation.2 | async-start | bytes 2097152 | tf_op jit(solution)/shard_map/all_to_all | solution.py:112
  48.9 7.3 %collective-permute-start.1 = (bf16[4096,128]{1,0:T(8,128)(2,1)S(1)}, bf16[4096,128]{1,0:T(8,128)(2,1)}, u32[]{:S(2)}, u32[]{:S(2)}) collective-permute-start(bf16[4096,128]{1,0:T(8,128)(2,1)S(1)} %bitcast.43), channel_id=1, source_target_pairs={{0,480},{32,0},{64,32},{96,64},{128,96},{160,128},{192,160},{224,1... | collective-permute-start | bytes 3145736 | tf_op jit(solution)/shard_map/ppermute | solution.py:19
  56.2 1.9 %collective-permute-start = (bf16[4096,128]{1,0:T(8,128)(2,1)S(1)}, bf16[4096,128]{1,0:T(8,128)(2,1)}, u32[]{:S(2)}, u32[]{:S(2)}) collective-permute-start(bf16[4096,128]{1,0:T(8,128)(2,1)S(1)} %bitcast.44), channel_id=1, source_target_pairs={{0,32},{32,64},{64,96},{96,128},{128,160},{160,192},{192,224},{224... | collective-permute-start | bytes 3145736 | tf_op jit(solution)/shard_map/ppermute | solution.py:19
  58.1 1.3 copy_bitcast_fusion.3
  59.4 17.8 %all-to-all-done.2 = bf16[128,32,128]{2,0,1:T(8,128)(2,1)S(1)} async-done(((bf16[128,32,128]{2,0,1:T(8,128)(2,1)}), bf16[128,32,128]{2,0,1:T(8,128)(2,1)S(1)}, u32[]{:S(2)}, u32[]{:S(2)}) %all-to-all-start.2) | async-done | bytes 1048608 | tf_op jit(solution)/shard_map/all_to_all | solution.py:112
  77.2 6.0 %all-to-all-start = ((bf16[128,32,128]{2,0,1:T(8,128)(2,1)}), bf16[128,32,128]{2,0,1:T(8,128)(2,1)}, u32[]{:S(2)}, u32[]{:S(2)}) async-start(bf16[128,32,128]{2,0,1:T(8,128)(2,1)} %copy_bitcast_fusion.3), calls=%async_computation | async-start | bytes 2097152 | tf_op jit(solution)/shard_map/all_to_all | solution.py:112
  83.2 2.7 %collective-permute-done.1 = bf16[4096,128]{1,0:T(8,128)(2,1)} collective-permute-done((bf16[4096,128]{1,0:T(8,128)(2,1)S(1)}, bf16[4096,128]{1,0:T(8,128)(2,1)}, u32[]{:S(2)}, u32[]{:S(2)}) %collective-permute-start.1) | collective-permute-done | bytes 1048608 | tf_op jit(solution)/shard_map/ppermute | solution.py:19
  85.9 1.3 slice.25
  87.1 4.3 %collective-permute-done = bf16[4096,128]{1,0:T(8,128)(2,1)} collective-permute-done((bf16[4096,128]{1,0:T(8,128)(2,1)S(1)}, bf16[4096,128]{1,0:T(8,128)(2,1)}, u32[]{:S(2)}, u32[]{:S(2)}) %collective-permute-start) | collective-permute-done | bytes 1048608 | tf_op jit(solution)/shard_map/ppermute | solution.py:19
  91.5 1.2 slice.24
  94.0 3.5 %collective-permute-start.3 = (bf16[4096,128]{1,0:T(8,128)(2,1)S(1)}, bf16[4096,128]{1,0:T(8,128)(2,1)}, u32[]{:S(2)}, u32[]{:S(2)}) collective-permute-start(bf16[4096,128]{1,0:T(8,128)(2,1)S(1)} %bitcast.40), channel_id=1, source_target_pairs={{0,480},{32,0},{64,32},{96,64},{128,96},{160,128},{192,160},{224,1... | collective-permute-start | bytes 3145736 | tf_op jit(solution)/shard_map/ppermute | solution.py:19
  97.6 1.9 %collective-permute-start.2 = (bf16[4096,128]{1,0:T(8,128)(2,1)S(1)}, bf16[4096,128]{1,0:T(8,128)(2,1)}, u32[]{:S(2)}, u32[]{:S(2)}) collective-permute-start(bf16[4096,128]{1,0:T(8,128)(2,1)S(1)} %bitcast.41), channel_id=1, source_target_pairs={{0,32},{32,64},{64,96},{96,128},{128,160},{160,192},{192,224},{224... | collective-permute-start | bytes 3145736 | tf_op jit(solution)/shard_map/ppermute | solution.py:19
  100.3 0.7 reshape.40.idx_ref
  101.0 10.4 %all-to-all-done = bf16[128,32,128]{2,0,1:T(8,128)(2,1)} async-done(((bf16[128,32,128]{2,0,1:T(8,128)(2,1)}), bf16[128,32,128]{2,0,1:T(8,128)(2,1)}, u32[]{:S(2)}, u32[]{:S(2)}) %all-to-all-start) | async-done | bytes 1048608 | tf_op jit(solution)/shard_map/all_to_all | solution.py:112
  111.4 11.3 %collective-permute-done.3 = bf16[4096,128]{1,0:T(8,128)(2,1)} collective-permute-done((bf16[4096,128]{1,0:T(8,128)(2,1)S(1)}, bf16[4096,128]{1,0:T(8,128)(2,1)}, u32[]{:S(2)}, u32[]{:S(2)}) %collective-permute-start.3) | collective-permute-done | bytes 1048608 | tf_op jit(solution)/shard_map/ppermute | solution.py:19
  122.7 5.2 %collective-permute-done.2 = bf16[4096,128]{1,0:T(8,128)(2,1)} collective-permute-done((bf16[4096,128]{1,0:T(8,128)(2,1)S(1)}, bf16[4096,128]{1,0:T(8,128)(2,1)}, u32[]{:S(2)}, u32[]{:S(2)}) %collective-permute-start.2) | collective-permute-done | bytes 1048608 | tf_op jit(solution)/shard_map/ppermute | solution.py:19
  127.9 19.5 %shard_map.55 = bf16[4096,128]{1,0:T(8,128)(2,1)} custom-call(s32[48]{0:T(128)} %reshape.40.idx_ref, s32[8]{0:T(128)} %dynamic_slice.7.cnt_ref, bf16[4096,128]{1,0:T(8,128)(2,1)} %bitcast.1.q_ref, bf16[8,4,2,64,128]{4,3,2,1,0:T(8,128)(2,1)} %bitcast.45, bf16[8,4,2,64,128]{4,3,2,1,0:T(8,128)(2,1)} %bitcast.42, bf16[8,4,2,64,128]{4,3,2,1,0:T(8,128)(2,1)} %bitcast.9.refs_2_, ...), custom_call_target="tpu_custom_call" | custom-call | flops 6442450944 | bytes 8388608 | tf_op jit(solution)/shard_map/pallas_call | solution.py:99
  147.4 37.2 %all_to_all.70 = bf16[32,128,128]{2,1,0:T(8,128)(2,1)S(1)} all-to-all(bf16[32,128,128]{2,1,0:T(8,128)(2,1)} %bitcast.46), channel_id=1, replica_groups=mesh['blk'=16,'head'=32] {'head'}, dimensions={0} | all-to-all | bytes 2097152 | tf_op jit(solution)/shard_map/all_to_all | solution.py:137
  184.6 1.1 copy_bitcast_fusion
  (14 shorter events, 0.9 us)
Async XLA Ops:
  0.0 58.1 %copy-start = (bf16[128,4096]{1,0:T(8,128)(2,1)S(1)}, bf16[128,4096]{1,0:T(8,128)(2,1)}, u32[]{:S(2)}) copy-start(bf16[128,4096]{1,0:T(8,128)(2,1)} %param.5) | copy-start | bytes 3145732
  3.0 41.1 %all-to-all-start.1 = ((bf16[128,32,128]{2,0,1:T(8,128)(2,1)}), bf16[128,32,128]{2,0,1:T(8,128)(2,1)S(1)}, u32[]{:S(2)}, u32[]{:S(2)}) async-start(bf16[128,32,128]{2,0,1:T(8,128)(2,1)} %copy_bitcast_fusion.2), calls=%async_computation.1 | async-start | bytes 2097152 | tf_op jit(solution)/shard_map/all_to_all | solution.py:112
  44.1 12.1 %copy-start.2 = (bf16[128,32,128]{2,0,1:T(8,128)(2,1)}, bf16[128,32,128]{2,0,1:T(8,128)(2,1)S(1)}, u32[]{:S(2)}) copy-start(bf16[128,32,128]{2,0,1:T(8,128)(2,1)S(1)} %all-to-all-done.1) | copy-start | bytes 3145732
  44.1 33.1 %all-to-all-start.2 = ((bf16[128,32,128]{2,0,1:T(8,128)(2,1)}), bf16[128,32,128]{2,0,1:T(8,128)(2,1)S(1)}, u32[]{:S(2)}, u32[]{:S(2)}) async-start(bf16[128,32,128]{2,0,1:T(8,128)(2,1)} %copy_bitcast_fusion.1), calls=%async_computation.2 | async-start | bytes 2097152 | tf_op jit(solution)/shard_map/all_to_all | solution.py:112
  48.9 37.0 %collective-permute-start.1 = (bf16[4096,128]{1,0:T(8,128)(2,1)S(1)}, bf16[4096,128]{1,0:T(8,128)(2,1)}, u32[]{:S(2)}, u32[]{:S(2)}) collective-permute-start(bf16[4096,128]{1,0:T(8,128)(2,1)S(1)} %bitcast.43), channel_id=1, source_target_pairs={{0,480},{32,0},{64,32},{96,64},{128,96},{160,128},{192,160},{224,1... | collective-permute-start | bytes 3145736 | tf_op jit(solution)/shard_map/ppermute | solution.py:19
  56.2 35.3 %collective-permute-start = (bf16[4096,128]{1,0:T(8,128)(2,1)S(1)}, bf16[4096,128]{1,0:T(8,128)(2,1)}, u32[]{:S(2)}, u32[]{:S(2)}) collective-permute-start(bf16[4096,128]{1,0:T(8,128)(2,1)S(1)} %bitcast.44), channel_id=1, source_target_pairs={{0,32},{32,64},{64,96},{96,128},{128,160},{160,192},{192,224},{224... | collective-permute-start | bytes 3145736 | tf_op jit(solution)/shard_map/ppermute | solution.py:19
  77.2 34.2 %all-to-all-start = ((bf16[128,32,128]{2,0,1:T(8,128)(2,1)}), bf16[128,32,128]{2,0,1:T(8,128)(2,1)}, u32[]{:S(2)}, u32[]{:S(2)}) async-start(bf16[128,32,128]{2,0,1:T(8,128)(2,1)} %copy_bitcast_fusion.3), calls=%async_computation | async-start | bytes 2097152 | tf_op jit(solution)/shard_map/all_to_all | solution.py:112
  93.9 5.6 %copy-start.4 = (s32[128]{0:T(128)S(1)}, s32[128]{0:T(128)}, u32[]{:S(2)}) copy-start(s32[128]{0:T(128)} %param.9) | copy-start | bytes 1540
  93.9 6.2 %copy-start.3 = (s32[128,6]{0,1:T(8,128)S(1)}, s32[128,6]{0,1:T(8,128)}, u32[]{:S(2)}) copy-start(s32[128,6]{0,1:T(8,128)} %param.8) | copy-start | bytes 9220
  94.0 33.9 %copy-start.1 = (bf16[128,32,128]{2,0,1:T(8,128)(2,1)}, bf16[128,32,128]{2,0,1:T(8,128)(2,1)S(1)}, u32[]{:S(2)}) copy-start(bf16[128,32,128]{2,0,1:T(8,128)(2,1)S(1)} %broadcast_add_fusion) | copy-start | bytes 3145732
  94.0 28.6 %collective-permute-start.3 = (bf16[4096,128]{1,0:T(8,128)(2,1)S(1)}, bf16[4096,128]{1,0:T(8,128)(2,1)}, u32[]{:S(2)}, u32[]{:S(2)}) collective-permute-start(bf16[4096,128]{1,0:T(8,128)(2,1)S(1)} %bitcast.40), channel_id=1, source_target_pairs={{0,480},{32,0},{64,32},{96,64},{128,96},{160,128},{192,160},{224,1... | collective-permute-start | bytes 3145736 | tf_op jit(solution)/shard_map/ppermute | solution.py:19
  97.6 30.4 %collective-permute-start.2 = (bf16[4096,128]{1,0:T(8,128)(2,1)S(1)}, bf16[4096,128]{1,0:T(8,128)(2,1)}, u32[]{:S(2)}, u32[]{:S(2)}) collective-permute-start(bf16[4096,128]{1,0:T(8,128)(2,1)S(1)} %bitcast.41), channel_id=1, source_target_pairs={{0,32},{32,64},{64,96},{96,128},{128,160},{160,192},{192,224},{224... | collective-permute-start | bytes 3145736 | tf_op jit(solution)/shard_map/ppermute | solution.py:19
